TPU v7x, 128 devices: a whole 4x4x4 slice. The times are simulated.
128 devices in a mesh: seq: 4 (over z), exp: 32 (over y, x, core).
Axes of the slice: x: 4, y: 4, z: 4, core: 2. Of those that a mesh axis runs over, the one named last changes fastest.
Arguments:
- streams: bfloat16 [8192, 4, 3584], P(('seq', 'exp')), may hold values from -6 to 6
- phi_matrix: bfloat16 [24, 14336], replicated, may hold values from -0.046875 to 0.046875
- mix_scale: float32 [3], replicated, may hold values from 0.5 to 2
- mix_bias: float32 [24], replicated, may hold values from -1 to 1
- router: bfloat16 [32, 3584], replicated, may hold values from -0.09375 to 0.09375
- expert_index_table: int32 [8192, 8], P(('seq', 'exp')), may hold values from 0 to 31, all different within a row; in each aligned block of 64 rows (0 to 63, 64 to 127, ...) at most 20 rows name the same one
- w_gate: bfloat16 [32, 3584, 2048], P('exp', None, 'seq'), may hold values from -0.09375 to 0.09375
- w_up: bfloat16 [32, 3584, 2048], P('exp', None, 'seq'), may hold values from -0.09375 to 0.09375
- down_weight: bfloat16 [32, 2048, 3584], P('exp', 'seq'), may hold values from -0.125 to 0.125
Outputs:
- new_streams: bfloat16 [8192, 4, 3584], P(('seq', 'exp'))
Inputs may be any that keep to these rules, and one draw needn't show every extreme that they name: `expert_index_table`: each row names 8 different experts; among the 64 rows of one device (aligned blocks of 64 rows) no expert is named by more than 20 rows, a bound that some block reaches; every expert is named somewhere.
All inputs are finite; a program needn't handle non-finite values.
Results may differ from a plain program's by a relative error of at most 0.012.
Values may be sent and summed in bfloat16 or wider, within the bound.
No kernel may reach another device: no remote copies, remote signals or barrier semaphores. Data moves between devices by JAX's collectives and lax.ppermute only.
A program may use at most 192 MiB of HBM per device.

v0:
```python
import jax
import jax.numpy as jnp
from jax import lax
from jax.sharding import PartitionSpec as P

BALANCE_SWEEPS = 20
EXPERTS = 32
CAP = 20


def mix_coefficients(streams, phi_matrix, mix_scale, mix_bias):
    count = streams.shape[1]
    flat = streams.astype(jnp.float32).reshape(streams.shape[0], -1)
    normed = flat * lax.rsqrt(jnp.mean(flat * flat, axis=1, keepdims=True) + 1e-06)
    normed = normed.astype(jnp.bfloat16)
    coeffs = lax.dot_general(
        normed, phi_matrix, (((1,), (1,)), ((), ())), preferred_element_type=jnp.float32
    )
    pre = jax.nn.sigmoid(mix_scale[0] * coeffs[:, :count] + mix_bias[:count])
    post = 2.0 * jax.nn.sigmoid(
        mix_scale[1] * coeffs[:, count : 2 * count] + mix_bias[count : 2 * count]
    )
    logits = mix_scale[2] * coeffs[:, 2 * count :] + mix_bias[2 * count :]
    mixing = jnp.exp(logits).reshape(-1, count, count)
    for sweep_step in range(BALANCE_SWEEPS):
        mixing = mixing / jnp.sum(mixing, axis=2, keepdims=True)
        mixing = mixing / jnp.sum(mixing, axis=1, keepdims=True)
    return (pre, post, mixing)


def mix_input(streams, pre):
    total = pre[:, 0, None] * streams[:, 0, :].astype(jnp.float32)
    for stream in range(1, streams.shape[1]):
        total = total + pre[:, stream, None] * streams[:, stream, :].astype(jnp.float32)
    return total.astype(jnp.bfloat16)


def mix_output(streams, mixing, post, moe_out):
    rows = []
    for target in range(streams.shape[1]):
        total = mixing[:, target, 0, None] * streams[:, 0, :].astype(jnp.float32)
        for source in range(1, streams.shape[1]):
            total = total + mixing[:, target, source, None] * streams[:, source, :].astype(
                jnp.float32
            )
        rows.append(total + post[:, target, None] * moe_out)
    return jnp.stack(rows, axis=1).astype(jnp.bfloat16)


def route_gates(layer_in, router, expert_index_table):
    logits = lax.dot_general(
        layer_in, router, (((1,), (1,)), ((), ())), preferred_element_type=jnp.float32
    )
    affinity = jax.nn.sigmoid(logits)
    chosen = jnp.take_along_axis(affinity, expert_index_table, axis=1)
    return 2.5 * chosen / jnp.sum(chosen, axis=1, keepdims=True)


def slot_ranks(expert_index_table):
    flat = expert_index_table.reshape(-1)
    onehot = (flat[:, None] == lax.iota(jnp.int32, EXPERTS)[None, :]).astype(jnp.int32)
    prior_value = jnp.cumsum(onehot, axis=0) - onehot
    return jnp.sum(prior_value * onehot, axis=1).reshape(expert_index_table.shape)


def expert_block(blocks, w_gate, w_up, down_weight):
    count, local, slots, width = blocks.shape
    rows = blocks.transpose(1, 0, 2, 3).reshape(local, count * slots, width)
    gate_part = jnp.einsum("erd,edf->erf", rows, w_gate, preferred_element_type=jnp.float32)
    up_part = jnp.einsum("erd,edf->erf", rows, w_up, preferred_element_type=jnp.float32)
    hidden = (jax.nn.silu(gate_part) * up_part).astype(jnp.bfloat16)
    part = jnp.einsum(
        "erf,efd->erd", hidden, down_weight, preferred_element_type=jnp.float32
    ).astype(jnp.bfloat16)
    return part.reshape(local, count, slots, width).transpose(1, 0, 2, 3)


def weigh_slots(returned_rows, targets, gates):
    selected_slot = jnp.take(returned_rows, targets.reshape(-1), axis=0)
    selected_slot = selected_slot.reshape(
        targets.shape[0], targets.shape[1], returned_rows.shape[1]
    )
    return jnp.sum(gates[:, :, None] * selected_slot, axis=1)


def body(
    streams, phi_matrix, mix_scale, mix_bias, router, expert_index_table, w_gate, w_up, down_weight
):
    pre, post, mixing = mix_coefficients(streams, phi_matrix, mix_scale, mix_bias)
    layer_in = mix_input(streams, pre)
    width = layer_in.shape[1]
    owners = lax.axis_size("exp")
    local = w_gate.shape[0]
    gates = route_gates(layer_in, router, expert_index_table)
    targets = expert_index_table * CAP + slot_ranks(expert_index_table)
    places = lax.iota(jnp.int32, EXPERTS * CAP)
    dispatch = jnp.any(places[:, None, None] == targets[None, :, :], axis=2).astype(jnp.bfloat16)
    send = jnp.dot(dispatch, layer_in, preferred_element_type=jnp.float32).astype(jnp.bfloat16)
    send = send.reshape(owners, local, CAP, width)
    gathered = lax.all_gather(
        lax.all_to_all(send, "exp", split_axis=0, concat_axis=0, tiled=True),
        "seq",
        axis=0,
        tiled=True,
    )
    part = expert_block(gathered, w_gate, w_up, down_weight)
    summed = lax.psum_scatter(part, "seq", scatter_dimension=0, tiled=True).astype(jnp.float32)
    returned = lax.all_to_all(
        summed.astype(jnp.bfloat16), "exp", split_axis=0, concat_axis=0, tiled=True
    ).astype(summed.dtype)
    moe_out = weigh_slots(returned.reshape(-1, width), targets, gates)
    return mix_output(streams, mixing, post, moe_out)


def solution(mesh):
    in_specs = (
        P(("seq", "exp"), None, None),
        P(),
        P(),
        P(),
        P(),
        P(("seq", "exp"), None),
        P("exp", None, "seq"),
        P("exp", None, "seq"),
        P("exp", "seq", None),
    )
    out_specs = P(("seq", "exp"), None, None)
    return jax.shard_map(body, mesh=mesh, in_specs=in_specs, out_specs=out_specs, check_vma=False)
```

profile of v0, /device:TPU:44, one launch (start us, length us, event | category | flops | bytes accessed | tf_op | source)
XLA Modules:
  0.0 694.8 jit_solution(11217916974579340434)
XLA Ops:
  6.5 0.0 copy-start
  6.5 0.0 all-gather.2.cloned.1.call-start
  6.6 0.9 copy.85
  7.5 0.1 eq.42
  7.6 0.1 eq.38
  7.7 3.0 multiply_reduce_fusion
  10.7 7.8 %fusion.120 = (bf16[64,1,3584]{2,1,0:T(2,128)(2,1)S(1)}, bf16[64,1,3584]{2,1,0:T(2,128)(2,1)}, bf16[64,1,3584]{2,1,0:T(2,128)(2,1)}, bf16[64,1,3584]{2,1,0:T(2,128)(2,1)}) fusion(bf16[64,4,3584]{2,1,0:T(4,128)(2,1)} %param.9), kind=kLoop, calls=%fused_computation.235 | loop fusion | bytes 3670016 | tf_op jit(solution)/shard_map/slice | solution.py:41
  18.5 0.0 copy-done.9
  18.5 0.1 fusion.122
  18.6 0.0 copy-done.8
  18.6 0.7 fusion.121
  19.2 0.6 fusion.85
  19.9 2.3 reduce-window.6
  22.2 0.2 slice_reduce_fusion
  22.4 0.1 fusion.84
  22.5 0.1 reshape.444
  22.6 0.1 copy.88
  22.7 0.1 copy.90
  22.8 0.0 copy-start.5
  22.8 0.5 fusion.31
  23.3 0.5 copy.102
  23.8 0.7 fusion.29
  24.4 1.5 fusion.98
  25.9 0.0 copy-done.3
  25.9 0.0 copy-done.4
  25.9 0.0 copy-done.5
  26.0 0.6 fusion.78
  26.6 3.5 convolution_convert_fusion.1
  30.1 7.2 %reshape.445 = bf16[32,1,20,3584]{3,2,0,1:T(8,128)(2,1)} reshape(bf16[640,3584]{1,0:T(8,128)(2,1)} %convolution_convert_fusion.1) | data formatting | bytes 9175040 | tf_op jit(solution)/shard_map/reshape | solution.py:99
  37.4 69.4 %all_to_all.10 = bf16[32,1,20,3584]{3,2,1,0:T(8,128)(2,1)S(1)} all-to-all(bf16[32,1,20,3584]{3,2,1,0:T(8,128)(2,1)} %bitcast.155), channel_id=1, replica_groups=mesh['seq'=4,'exp'=32] {'exp'}, dimensions={0} | all-to-all | bytes 9175040 | tf_op jit(solution)/shard_map/all_to_all | solution.py:101
  106.7 3.5 copy.92
  110.2 0.0 all-gather.2.cloned.1.call-update
  110.2 0.2 reduce-scatter.2.cloned.1.call-start
  110.5 168.3 %all-gather.2.cloned.1.call-done = bf16[128,1,20,3584]{3,0,2,1:T(8,128)(2,1)} async-done(((bf16[32,1,20,3584]{3,0,2,1:T(8,128)(2,1)}), bf16[128,1,20,3584]{3,0,2,1:T(8,128)(2,1)}) %all-gather.2.cloned.1.call-update) | async-done | bytes 18350096 | tf_op jit(solution)/shard_map/all_gather | solution.py:100
  278.8 23.4 %copy.93 = bf16[128,1,20,3584]{3,2,0,1:T(8,128)(2,1)} copy(bf16[128,1,20,3584]{3,0,2,1:T(8,128)(2,1)} %all-gather.2.cloned.1.call-done) | data formatting | bytes 36700160 | tf_op jit(solution)/shard_map/all_gather | solution.py:100
  302.2 25.1 %reshape.446 = bf16[2560,3584]{1,0:T(8,128)(2,1)} reshape(bf16[128,1,20,3584]{3,2,0,1:T(8,128)(2,1)} %copy.93) | data formatting | bytes 36700160 | tf_op jit(solution)/shard_map/reshape.7
  327.3 15.9 %fusion.26 = f32[2560,512]{1,0:T(8,128)} fusion(bf16[2560,3584]{1,0:T(8,128)(2,1)} %reshape.446, bf16[1,3584,512]{2,1,0:T(8,128)(2,1)} %param.15), kind=kOutput, calls=%fused_computation.30 | convolution fusion | flops 9395240960 | bytes 27262976 | tf_op jit(solution)/shard_map/erd,edf->erf/dot_general | solution.py:69
  343.2 27.8 %convolution_convert_fusion = bf16[2560,3584]{1,0:T(8,128)(2,1)} fusion(bf16[1,512,3584]{2,1,0:T(8,128)(2,1)} %param.17, bf16[2560,3584]{1,0:T(8,128)(2,1)} %reshape.446, f32[2560,512]{1,0:T(8,128)} %fusion.26, bf16[1,3584,512]{2,1,0:T(8,128)(2,1)} %param.16), kind=kOutput, calls=%fused_computation.21 | convolution fusion | flops 18807521280 | bytes 49283072 | tf_op jit(solution)/shard_map/erf,efd->erd/dot_general | solution.py:72
  371.0 25.0 %transpose_reshape.3 = bf16[128,1,20,3584]{3,2,0,1:T(8,128)(2,1)} reshape(bf16[2560,3584]{1,0:T(8,128)(2,1)} %convolution_convert_fusion) | data formatting | bytes 36700160 | tf_op jit(solution)/shard_map/transpose;reshape | solution.py:75
  396.0 0.0 reduce-scatter.2.cloned.1.call-update
  396.0 0.1 slice.143
  396.1 0.1 reshape.452
  396.2 0.1 copy.82
  396.3 0.1 reshape.467
  396.4 0.1 copy.89
  396.5 0.5 copy-done.6
  396.9 0.3 fusion.34
  397.2 3.9 gather_fusion.1
  401.1 0.1 reshape.470
  401.2 0.1 copy.83
  401.3 0.1 copy.84
  401.4 0.8 fusion.87
  402.3 183.9 %reduce-scatter.2.cloned.1.call-done = bf16[32,1,20,3584]{3,2,0,1:T(8,128)(2,1)} async-done(((bf16[128,1,20,3584]{3,2,0,1:T(8,128)(2,1)}), bf16[32,1,20,3584]{3,2,0,1:T(8,128)(2,1)}) %reduce-scatter.2.cloned.1.call-update) | async-done | bytes 4587536 | tf_op jit(solution)/shard_map/reduce_scatter | solution.py:107
  586.2 7.5 %all-to-all-start.1 = ((bf16[32,1,20,3584]{3,2,1,0:T(8,128)(2,1)}), bf16[32,1,20,3584]{3,2,1,0:T(8,128)(2,1)}, u32[]{:S(2)}, u32[]{:S(2)}) async-start(bf16[32,1,20,3584]{3,2,1,0:T(8,128)(2,1)} %bitcast.157), calls=%async_computation.2 | async-start | bytes 11010048 | tf_op jit(solution)/shard_map/all_to_all | solution.py:108
  594.4 62.9 %all-to-all-done.1 = bf16[32,1,20,3584]{3,2,1,0:T(8,128)(2,1)} async-done(((bf16[32,1,20,3584]{3,2,1,0:T(8,128)(2,1)}), bf16[32,1,20,3584]{3,2,1,0:T(8,128)(2,1)}, u32[]{:S(2)}, u32[]{:S(2)}) %all-to-all-start.1) | async-done | bytes 4587552 | tf_op jit(solution)/shard_map/all_to_all | solution.py:108
  657.3 8.1 %reshape.458 = f32[640,3584]{1,0:T(8,128)} reshape(bf16[32,1,20,3584]{3,2,1,0:T(8,128)(2,1)} %all-to-all-done.1) | data formatting | bytes 13762560 | tf_op jit(solution)/shard_map/reshape | solution.py:111
  665.4 11.7 %gather_fusion = f32[512,3584]{1,0:T(8,128)} fusion(f32[640,3584]{1,0:T(8,128)} %reshape.458, s32[1024]{0:T(1024)S(1)} %pad_clamp_fusion), kind=kCustom, calls=%fused_computation | custom fusion | bytes 14682112 | tf_op jit(solution)/shard_map/jit(_take)/gather | solution.py:79
  677.1 6.1 fusion.20
  683.3 0.9 fusion.63
  684.1 0.0 copy-start.1
  684.2 0.9 fusion.58
  685.0 0.2 pad_maximum_fusion
  685.3 2.6 copy.96
  687.9 0.0 copy-done.1
  (45 shorter events, 0.9 us)
Async XLA Ops:
  6.5 17.2 %copy-start = (bf16[24,14336]{1,0:T(8,128)(2,1)S(1)}, bf16[24,14336]{1,0:T(8,128)(2,1)}, u32[]{:S(2)}) copy-start(bf16[24,14336]{1,0:T(8,128)(2,1)} %param.10) | copy-start | bytes 2064388
  6.5 16.1 %copy-start.7 = (s32[64,8]{0,1:T(8,128)S(1)}, s32[64,8]{0,1:T(8,128)}, u32[]{:S(2)}) copy-start(s32[64,8]{0,1:T(8,128)} %param.14) | copy-start | bytes 6148
  6.5 16.7 %copy-start.2 = (bf16[64,4,3584]{2,1,0:T(4,128)(2,1)S(1)}, bf16[64,4,3584]{2,1,0:T(4,128)(2,1)}, u32[]{:S(2)}) copy-start(bf16[64,4,3584]{2,1,0:T(4,128)(2,1)} %param.9) | copy-start | bytes 5505028
  6.5 11.9 %copy-start.9 = (f32[24]{0:T(128)S(1)}, f32[24]{0:T(128)}, u32[]{:S(2)}) copy-start(f32[24]{0:T(128)} %param.12) | copy-start | bytes 292
  6.5 12.0 %copy-start.8 = (f32[3]{0:T(128)S(1)}, f32[3]{0:T(128)}, u32[]{:S(2)}) copy-start(f32[3]{0:T(128)} %param.11) | copy-start | bytes 40
  6.5 272.3 %all-gather.2.cloned.1.call-start = ((), (), s32[]{:S(2)}) async-start(), calls=%async_computation.3 | async-start | bytes 22937600 | tf_op jit(solution)/shard_map/all_gather | solution.py:100
  22.8 3.1 copy-start.3
  22.8 3.1 copy-start.4
  22.8 3.2 copy-start.5
  110.2 476.0 %reduce-scatter.2.cloned.1.call-start = ((), (), s32[]{:S(2)}) async-start(), calls=%async_computation.4 | async-start | bytes 27525120 | tf_op jit(solution)/shard_map/reduce_scatter | solution.py:107
  396.0 0.9 copy-start.6
  586.2 71.1 %all-to-all-start.1 = ((bf16[32,1,20,3584]{3,2,1,0:T(8,128)(2,1)}), bf16[32,1,20,3584]{3,2,1,0:T(8,128)(2,1)}, u32[]{:S(2)}, u32[]{:S(2)}) async-start(bf16[32,1,20,3584]{3,2,1,0:T(8,128)(2,1)} %bitcast.157), calls=%async_computation.2 | async-start | bytes 11010048 | tf_op jit(solution)/shard_map/all_to_all | solution.py:108
  684.1 3.8 copy-start.1
Sparse Core Ops, SparseCore 0:
  110.4 168.4 all-gather.1
  396.1 190.0 reduce-scatter.1
where the time goes:
time: 704 us; the launch traced here: 695 us
  waiting for transfers between devices  415 us (59%)
  local copies, waits for them, and re-layouts  122 us (17%)
  blocking collectives  69.4 us (10%)
  matrix products  48.2 us (7%)
  other arithmetic  18.3 us (3%)
  between operations  13.7 us (2%)
  starting transfers between devices  7.71 us (1%)
    reduce_scatter x1, waiting for transfers between devices, body(): lax.psum_scatter(part, 'seq', scatter_dimension=0, tiled=True)  184 us
    all_gather x1, waiting for transfers between devices, body(): lax.all_gather(lax.all_to_all(send, 'exp', split_axis=0, concat_axis=0, t...  168 us
    all_to_all x1, blocking collectives, body(): lax.all_to_all(send, 'exp', split_axis=0, concat_axis=0, tiled=True)  69.4 us
    all_to_all x1, waiting for transfers between devices, body(): lax.all_to_all(summed.astype(jnp.bfloat16), 'exp', split_axis=0, concat_a...  62.9 us
    dot_general x1, matrix products, expert_block(): jnp.einsum('erf,efd->erd', hidden, down_weight, preferred_element_type=jn...  27.8 us
    another operation x2, local copies, waits for them, and re-layouts  25.1 us
    another operation x1, local copies, waits for them, and re-layouts, expert_block(): return part.reshape(local, count, slots, width).transpose(1, 0, 2, 3)  25 us
    all_gather x1, local copies, waits for them, and re-layouts, body(): lax.all_gather(lax.all_to_all(send, 'exp', split_axis=0, concat_axis=0, t...  23.4 us
  transfers between devices with their start and end apart: 3, of which 3 were waited for; matrix products, arithmetic and copies ran while one was open for 1% of the time, Pallas kernels for 0%

commit v1 on v0

v1 whole, which is shorter than its diff:
```python
import functools

import jax
import jax.numpy as jnp
from jax import lax
from jax.experimental import pallas as pl
from jax.experimental.pallas import tpu as pltpu
from jax.sharding import Mesh, PartitionSpec as P

BALANCE_SWEEPS = 20
EXPERTS = 32
CAP = 20
TOK = 64
GROUP = 256
SLOTS = GROUP // TOK * CAP
PER_STEP = 2
GATE_LANES = 128
RING = 4


def mix_coefficients(streams, phi_matrix, mix_scale, mix_bias):
    count = streams.shape[1]
    flat = streams.astype(jnp.float32).reshape(streams.shape[0], -1)
    normed = flat * lax.rsqrt(jnp.mean(flat * flat, axis=1, keepdims=True) + 1e-06)
    normed = normed.astype(jnp.bfloat16)
    coeffs = lax.dot_general(
        normed, phi_matrix, (((1,), (1,)), ((), ())), preferred_element_type=jnp.float32
    )
    pre = jax.nn.sigmoid(mix_scale[0] * coeffs[:, :count] + mix_bias[:count])
    post = 2.0 * jax.nn.sigmoid(
        mix_scale[1] * coeffs[:, count : 2 * count] + mix_bias[count : 2 * count]
    )
    logits = mix_scale[2] * coeffs[:, 2 * count :] + mix_bias[2 * count :]
    mixing = jnp.exp(logits).reshape(-1, count, count)
    for sweep_step in range(BALANCE_SWEEPS):
        mixing = mixing / jnp.sum(mixing, axis=2, keepdims=True)
        mixing = mixing / jnp.sum(mixing, axis=1, keepdims=True)
    return (pre, post, mixing)


def mix_input(streams, pre):
    total = pre[:, 0, None] * streams[:, 0, :].astype(jnp.float32)
    for stream in range(1, streams.shape[1]):
        total = total + pre[:, stream, None] * streams[:, stream, :].astype(jnp.float32)
    return total.astype(jnp.bfloat16)


def mix_output(streams, mixing, post, moe_out):
    rows = []
    for target in range(streams.shape[1]):
        total = mixing[:, target, 0, None] * streams[:, 0, :].astype(jnp.float32)
        for source in range(1, streams.shape[1]):
            total = total + mixing[:, target, source, None] * streams[:, source, :].astype(
                jnp.float32
            )
        rows.append(total + post[:, target, None] * moe_out)
    return jnp.stack(rows, axis=1).astype(jnp.bfloat16)


def dense_gates(layer_in, router, expert_index_table):
    logits = lax.dot_general(
        layer_in, router, (((1,), (1,)), ((), ())), preferred_element_type=jnp.float32
    )
    affinity = jax.nn.sigmoid(logits)
    experts = lax.iota(jnp.int32, EXPERTS)
    named = jnp.any(expert_index_table[:, :, None] == experts[None, None, :], axis=1)
    chosen = jnp.where(named, affinity, 0.0)
    gates = 2.5 * chosen / jnp.sum(chosen, axis=1, keepdims=True)
    high = lax.reduce_precision(gates, 8, 7)
    low = gates - high
    pad = jnp.zeros((gates.shape[0], GATE_LANES - 2 * EXPERTS), jnp.float32)
    return jnp.concatenate([high, low, pad], axis=1).astype(jnp.bfloat16)


def expert_kernel(
    ids, x_ref, wg0, wu0, wd0, wg1, wu1, wd1, o_ref, st_ref, gate_ref, rows_ref, y_ref
):
    width = o_ref.shape[-1]
    tile = min(512, width)
    lane = lax.broadcasted_iota(jnp.int32, (GROUP, GATE_LANES), 1)
    row = lax.broadcasted_iota(jnp.int32, (GROUP, GROUP), 0)
    col = lax.broadcasted_iota(jnp.int32, (GROUP, GROUP), 1)
    before = ((col < row) & (col // TOK == row // TOK)).astype(jnp.float32).astype(jnp.bfloat16)
    block = lax.broadcasted_iota(jnp.int32, (GROUP, 1), 0) // TOK
    slot_of = lax.broadcasted_iota(jnp.int32, (GROUP, 2 * SLOTS), 1)
    slot_lane = lax.broadcasted_iota(jnp.int32, (SLOTS, GATE_LANES), 1)
    for g in range(PER_STEP):
        rows = pl.ds(g * GROUP, GROUP)
        gates = x_ref[rows, width : width + GATE_LANES]
        hit = (gates.astype(jnp.float32) != 0.0).astype(jnp.float32)
        rank = jnp.dot(before, hit.astype(jnp.bfloat16), preferred_element_type=jnp.float32)
        slots = []
        for e in range(2):
            mine = lane == ids[e]
            rank_e = jnp.sum(jnp.where(mine, rank, 0.0), axis=1, keepdims=True)
            hit_e = jnp.sum(jnp.where(mine, hit, 0.0), axis=1, keepdims=True)
            place = rank_e.astype(jnp.int32) + block * CAP + e * SLOTS
            slots.append(jnp.where(hit_e > 0.0, place, -1))
        st = (slot_of == slots[0]) | (slot_of == slots[1])
        st_ref[g] = st.astype(jnp.float32).astype(jnp.bfloat16)
        picked = lax.dot_general(
            st_ref[g], gates, (((0,), (0,)), ((), ())), preferred_element_type=jnp.float32
        )
        for e in range(2):
            own = picked[e * SLOTS : (e + 1) * SLOTS]
            wanted = (slot_lane == ids[e]) | (slot_lane == ids[e] + EXPERTS)
            gate_ref[e, pl.ds(g * SLOTS, SLOTS), :] = jnp.broadcast_to(
                jnp.sum(jnp.where(wanted, own, 0.0), axis=1, keepdims=True), (SLOTS, GATE_LANES)
            )

        @pl.loop(0, width // tile)
        def _(n):
            cols = pl.ds(pl.multiple_of(n * tile, tile), tile)
            rows_ref[g, :, cols] = lax.dot_general(
                st_ref[g],
                x_ref[rows, cols],
                (((0,), (0,)), ((), ())),
                preferred_element_type=jnp.float32,
            ).astype(jnp.bfloat16)

    for e, (wg, wu, wd) in enumerate(((wg0, wu0, wd0), (wg1, wu1, wd1))):
        mine = slice(e * SLOTS, (e + 1) * SLOTS)
        xs = jnp.concatenate([rows_ref[g, mine, :] for g in range(PER_STEP)], axis=0)
        gate_part = jnp.dot(xs, wg[...], preferred_element_type=jnp.float32)
        up_part = jnp.dot(xs, wu[...], preferred_element_type=jnp.float32)
        hidden = gate_part / (1.0 + jnp.exp(-gate_part)) * up_part
        hidden = (hidden * gate_ref[e, :, 0:1]).astype(jnp.bfloat16)

        @pl.loop(0, width // tile)
        def _(n):
            cols = pl.ds(pl.multiple_of(n * tile, tile), tile)
            part = jnp.dot(hidden, wd[:, cols], preferred_element_type=jnp.float32)
            part = part.astype(jnp.bfloat16)
            for g in range(PER_STEP):
                y_ref[g, mine, cols] = part[g * SLOTS : (g + 1) * SLOTS]

    for g in range(PER_STEP):

        @pl.loop(0, width // tile)
        def _(n):
            cols = pl.ds(pl.multiple_of(n * tile, tile), tile)
            out = jnp.dot(st_ref[g], y_ref[g, :, cols], preferred_element_type=jnp.float32)
            out = out.astype(jnp.bfloat16)
            for b in range(GROUP // TOK):
                o_ref[g * (GROUP // TOK) + b, 0, :, cols] = out[b * TOK : (b + 1) * TOK]


def expert_call(ids, gathered, weights, width, ff):
    tokens = gathered.shape[0]
    step = PER_STEP * GROUP
    steps = tokens // step
    planes = RING
    per_plane = steps // planes
    chips = tokens // TOK // planes
    rows = PER_STEP * SLOTS
    whole = lambda shape: pl.BlockSpec(
        shape, lambda i, ids: (0, 0), pipeline_mode=pl.Buffered(1)
    )
    up, down = whole((width, ff)), whole((ff, width))
    return pl.pallas_call(
        expert_kernel,
        out_shape=jax.ShapeDtypeStruct((chips, planes, TOK, width), jnp.bfloat16),
        grid_spec=pltpu.PrefetchScalarGridSpec(
            num_scalar_prefetch=1,
            grid=(steps,),
            in_specs=[
                pl.BlockSpec((step, width + GATE_LANES), lambda i, ids: (i, 0)),
                up, up, down, up, up, down,
            ],
            out_specs=pl.BlockSpec(
                (step // TOK, 1, TOK, width),
                lambda i, ids: (i % per_plane, i // per_plane, 0, 0),
            ),
            scratch_shapes=[
                pltpu.VMEM((PER_STEP, GROUP, 2 * SLOTS), jnp.bfloat16),
                pltpu.VMEM((2, rows, GATE_LANES), jnp.float32),
                pltpu.VMEM((PER_STEP, 2 * SLOTS, width), jnp.bfloat16),
                pltpu.VMEM((PER_STEP, 2 * SLOTS, width), jnp.bfloat16),
            ],
        ),
        compiler_params=pltpu.CompilerParams(
            dimension_semantics=("arbitrary",), vmem_limit_bytes=58 << 20
        ),
        cost_estimate=pl.CostEstimate(
            flops=12 * steps * rows * width * ff,
            bytes_accessed=4 * tokens * width,
            transcendentals=0,
        ),
        name="experts",
    )(ids, gathered, *weights)


def body(
    streams, phi_matrix, mix_scale, mix_bias, router, expert_index_table, w_gate, w_up, down_weight
):
    width, ff = w_gate.shape[1], w_gate.shape[2]
    swap = [(0, 1), (1, 0)]
    own = (w_gate[0], w_up[0], down_weight[0])
    other = tuple(lax.ppermute(w, "c", swap) for w in own)
    pre, post, mixing = mix_coefficients(streams, phi_matrix, mix_scale, mix_bias)
    layer_in = mix_input(streams, pre)
    gates = dense_gates(layer_in, router, expert_index_table)
    packed = jnp.concatenate([layer_in, gates], axis=1)
    gathered = lax.all_gather(packed, ("z", "y", "x"), axis=0, tiled=True)
    core = lax.axis_index("c")
    pair = 2 * (lax.axis_index("y") * RING + lax.axis_index("x"))
    ids = jnp.stack([pair + core, pair + 1 - core]).astype(jnp.int32)
    dense = expert_call(ids, gathered, own + other, width, ff)
    summed = lax.psum_scatter(
        dense.reshape(-1, width), ("y", "x"), scatter_dimension=0, tiled=True
    ).reshape(RING, TOK, width)
    plane = lax.axis_index("z")
    moe_out = lax.dynamic_index_in_dim(summed, plane, 0, keepdims=False).astype(jnp.float32)
    for shift in range(1, RING):
        away = lax.dynamic_index_in_dim(summed, (plane + shift) % RING, 0, keepdims=False)
        ring = [(i, (i + shift) % RING) for i in range(RING)]
        moe_out = moe_out + lax.ppermute(away, "z", ring).astype(jnp.float32)
    return mix_output(streams, mixing, post, moe_out)


def solution(mesh):
    torus = Mesh(mesh.devices.reshape(RING, RING, RING, 2), ("z", "y", "x", "c"))
    tokens, experts = ("z", "y", "x", "c"), ("y", "x", "c")
    in_specs = (
        P(tokens, None, None),
        P(),
        P(),
        P(),
        P(),
        P(tokens, None),
        P(experts, None, "z"),
        P(experts, None, "z"),
        P(experts, "z", None),
    )
    out_specs = P(tokens, None, None)
    return jax.shard_map(
        body, mesh=torus, in_specs=in_specs, out_specs=out_specs, check_vma=False
    )
```

time: 704 us -> 508 us (0.72)
  Pallas kernels: 0 us -> 120 us
  local copies, waits for them, and re-layouts: 122 us -> 10.4 us
  waiting for transfers between devices: 415 us -> 341 us
  blocking collectives: 69.4 us -> 0 us
  matrix products: 48.2 us -> 1.03 us
  other arithmetic: 18.3 us -> 10.8 us
    pallas_call x0 -> x1, Pallas kernels: none -> 120 us  [expert_call(): pl.pallas_call(expert_kernel, out_shape=jax.ShapeDtypeStruct((chips, plan...]
    all_to_all x1 -> x0, blocking collectives: 69.4 us -> none  [body(): lax.all_to_all(send, 'exp', split_axis=0, concat_axis=0, tiled=True)]
    all_to_all x1 -> x0, waiting for transfers between devices: 62.9 us -> none  [body(): lax.all_to_all(summed.astype(jnp.bfloat16), 'exp', split_axis=0, concat_a...]
    another operation x3 -> x0, local copies, waits for them, and re-layouts: 50.1 us -> none
    dot_general x4 -> x1, matrix products: 47.5 us -> 0.36 us  [dense_gates(): lax.dot_general(layer_in, router, (((1,), (1,)), ((), ())), preferred_ele...]
    all_gather x1, waiting for transfers between devices: 168 us -> 133 us  [body(): gathered = lax.all_gather(packed, ('z', 'y', 'x'), axis=0, tiled=True)]
    ppermute x0 -> x6, waiting for transfers between devices: none -> 35.2 us  [the longest x3 19.2 us: body(): moe_out = moe_out + lax.ppermute(away, 'z', ring).astype(jnp.float32)]
    all_gather x1 -> x0, local copies, waits for them, and re-layouts: 23.4 us -> none  [body(): lax.all_gather(lax.all_to_all(send, 'exp', split_axis=0, concat_axis=0, t...]
  transfers between devices with their start and end apart: 3 -> 8, of which waited for: 3 -> 8; matrix products, arithmetic and copies ran while one was open for 1% -> 0% of each run, Pallas kernels for 0% -> 0%
where the time goes in v1:
time: 508 us; the launch traced here: 503 us
  waiting for transfers between devices  341 us (67%)
  Pallas kernels  120 us (24%)
  between operations  13.6 us (3%)
  other arithmetic  10.8 us (2%)
  local copies, waits for them, and re-layouts  10.4 us (2%)
  starting transfers between devices  5.58 us (1%)
    reduce_scatter x1, waiting for transfers between devices, body(): lax.psum_scatter(dense.reshape(-1, width), ('y', 'x'), scatter_dimension=...  173 us
    all_gather x1, waiting for transfers between devices, body(): gathered = lax.all_gather(packed, ('z', 'y', 'x'), axis=0, tiled=True)  133 us
    pallas_call x1, Pallas kernels, expert_call(): pl.pallas_call(expert_kernel, out_shape=jax.ShapeDtypeStruct((chips, plan...  120 us
    ppermute x3, waiting for transfers between devices, body(): moe_out = moe_out + lax.ppermute(away, 'z', ring).astype(jnp.float32)  19.2 us
    ppermute x3, waiting for transfers between devices, body(): other = tuple((lax.ppermute(w, 'c', swap) for w in own))  16 us
  transfers between devices with their start and end apart: 8, of which 8 were waited for; matrix products, arithmetic and copies ran while one was open for 0% of the time, Pallas kernels for 0%

profile of v1, /device:TPU:44, one launch (start us, length us, event | category | flops | bytes accessed | tf_op | source)
XLA Modules:
  0.0 502.6 jit_solution(4156618354814438543)
XLA Ops:
  6.5 0.0 copy-start
  6.5 0.0 copy-start.2
  6.5 0.0 all-gather.2.cloned.1.call-start
  6.5 3.1 multiply_reduce_fusion
  9.6 0.0 copy-done.2
  9.6 2.7 fusion.109
  12.3 0.0 copy-start.5
  12.3 0.0 copy-start.3
  12.3 0.5 copy.29
  12.8 0.1 copy-done.5
  13.0 0.1 fusion.111
  13.1 0.0 copy-done.3
  13.1 0.7 fusion.110
  13.7 0.0 copy-done
  13.7 0.0 copy-start.4
  13.7 0.7 fusion.19
  14.4 1.4 fusion.82
  15.8 0.0 copy-done.4
  15.9 0.1 copy.22
  16.0 0.0 copy-start.6
  16.0 0.6 fusion.52
  16.6 0.3 copy-done.6
  16.9 0.4 fusion.112
  17.3 0.1 fusion.75
  17.4 0.9 concatenate.6
  18.3 0.0 all-gather.2.cloned.1.call-update
  18.3 0.0 reduce-scatter.2.cloned.1.call-start
  18.3 0.1 collective-permute-start
  18.4 0.5 collective-permute-start.1
  18.9 0.1 collective-permute-start.2
  19.0 0.6 pad_add_fusion.ids
  19.6 5.6 %collective-permute-done.wg1 = bf16[3584,512]{1,0:T(8,128)(2,1)} collective-permute-done((bf16[3584,512]{1,0:T(8,128)(2,1)}, bf16[3584,512]{1,0:T(8,128)(2,1)}, u32[]{:S(2)}, u32[]{:S(2)}) %collective-permute-start) | collective-permute-done | bytes 3670048 | tf_op jit(solution)/shard_map/ppermute | solution.py:199
  25.2 5.2 %collective-permute-done.1.wu1 = bf16[3584,512]{1,0:T(8,128)(2,1)} collective-permute-done((bf16[3584,512]{1,0:T(8,128)(2,1)}, bf16[3584,512]{1,0:T(8,128)(2,1)}, u32[]{:S(2)}, u32[]{:S(2)}) %collective-permute-start.1) | collective-permute-done | bytes 3670048 | tf_op jit(solution)/shard_map/ppermute | solution.py:199
  30.4 5.2 %collective-permute-done.2.wd1 = bf16[512,3584]{1,0:T(8,128)(2,1)} collective-permute-done((bf16[512,3584]{1,0:T(8,128)(2,1)}, bf16[512,3584]{1,0:T(8,128)(2,1)}, u32[]{:S(2)}, u32[]{:S(2)}) %collective-permute-start.2) | collective-permute-done | bytes 3670048 | tf_op jit(solution)/shard_map/ppermute | solution.py:199
  35.7 132.9 %all-gather.2.cloned.1.call-done.x_ref = bf16[4096,3712]{1,0:T(8,128)(2,1)} async-done(((bf16[64,3712]{1,0:T(8,128)(2,1)}), bf16[4096,3712]{1,0:T(8,128)(2,1)}) %all-gather.2.cloned.1.call-update) | async-done | bytes 30408720 | tf_op jit(solution)/shard_map/all_gather | solution.py:204
  168.6 120.5 %experts.1 = bf16[16,4,64,3584]{3,2,1,0:T(8,128)(2,1)} custom-call(s32[2]{0:T(128)} %pad_add_fusion.ids, bf16[4096,3712]{1,0:T(8,128)(2,1)} %all-gather.2.cloned.1.call-done.x_ref, bf16[3584,512]{1,0:T(8,128)(2,1)} %bitcast.134, bf16[3584,512]{1,0:T(8,128)(2,1)} %bitcast.136, bf16[512,3584]{1,0:T(8,128)(2,1)} %bitcast.138, ...), custom_call_target="tpu_custom_call" | custom-call | flops 28185722880 | bytes 58720256 | tf_op jit(solution)/shard_map/experts/pallas_call | solution.py:160
  289.1 0.0 reduce-scatter.2.cloned.1.call-update
  289.1 0.1 slice.129
  289.2 0.8 fusion.77
  290.7 172.6 %reduce-scatter.2.cloned.1.call-done = bf16[256,3584]{1,0:T(8,128)(2,1)} async-done(((bf16[4096,3584]{1,0:T(8,128)(2,1)}), bf16[256,3584]{1,0:T(8,128)(2,1)}) %reduce-scatter.2.cloned.1.call-update) | async-done | bytes 1835024 | tf_op jit(solution)/shard_map/reduce_scatter | solution.py:209
  463.3 2.4 dynamic-slice_bitcast_fusion.2
  465.7 0.5 collective-permute-start.5
  466.1 2.6 collective-permute-start.4
  468.7 1.9 collective-permute-start.3
  470.6 7.7 %collective-permute-done.5 = bf16[64,3584]{1,0:T(8,128)(2,1)S(1)} collective-permute-done((bf16[64,3584]{1,0:T(8,128)(2,1)}, bf16[64,3584]{1,0:T(8,128)(2,1)S(1)}, u32[]{:S(2)}, u32[]{:S(2)}) %collective-permute-start.5) | collective-permute-done | bytes 458784 | tf_op jit(solution)/shard_map/ppermute | solution.py:217
  478.3 10.6 %collective-permute-done.4 = bf16[64,3584]{1,0:T(8,128)(2,1)S(1)} collective-permute-done((bf16[64,3584]{1,0:T(8,128)(2,1)}, bf16[64,3584]{1,0:T(8,128)(2,1)S(1)}, u32[]{:S(2)}, u32[]{:S(2)}) %collective-permute-start.4) | collective-permute-done | bytes 458784 | tf_op jit(solution)/shard_map/ppermute | solution.py:217
  488.9 0.8 collective-permute-done.3
  489.8 1.7 fusion.73
  491.4 0.5 fusion.70
  492.0 0.9 fusion.72
  492.9 0.0 copy-start.1
  492.9 0.2 pad_maximum_fusion
  493.1 2.6 copy.23
  495.8 0.0 copy-done.1
  (29 shorter events, 0.8 us)
Async XLA Ops:
  6.5 7.2 %copy-start = (bf16[24,14336]{1,0:T(8,128)(2,1)S(1)}, bf16[24,14336]{1,0:T(8,128)(2,1)}, u32[]{:S(2)}) copy-start(bf16[24,14336]{1,0:T(8,128)(2,1)} %param.10) | copy-start | bytes 2064388
  6.5 3.1 copy-start.2
  6.5 162.0 %all-gather.2.cloned.1.call-start = ((), (), s32[]{:S(2)}) async-start(), calls=%async_computation.1 | async-start | bytes 30883840 | tf_op jit(solution)/shard_map/all_gather | solution.py:204
  12.3 0.7 copy-start.5
  12.3 0.7 copy-start.3
  13.7 2.1 copy-start.4
  16.0 0.9 copy-start.6
  18.3 445.0 %reduce-scatter.2.cloned.1.call-start = ((), (), s32[]{:S(2)}) async-start(), calls=%async_computation.2 | async-start | bytes 31195136 | tf_op jit(solution)/shard_map/reduce_scatter | solution.py:209
  18.3 6.8 %collective-permute-start = (bf16[3584,512]{1,0:T(8,128)(2,1)}, bf16[3584,512]{1,0:T(8,128)(2,1)}, u32[]{:S(2)}, u32[]{:S(2)}) collective-permute-start(bf16[3584,512]{1,0:T(8,128)(2,1)} %bitcast.133), channel_id=1, source_target_pairs={{0,1},{1,0},{2,3},{3,2},{4,5},{5,4},{6,7},{7,6},{8,9},{9,8},{10,11... | collective-permute-start | bytes 11010056 | tf_op jit(solution)/shard_map/ppermute | solution.py:199
  18.4 12.0 %collective-permute-start.1 = (bf16[3584,512]{1,0:T(8,128)(2,1)}, bf16[3584,512]{1,0:T(8,128)(2,1)}, u32[]{:S(2)}, u32[]{:S(2)}) collective-permute-start(bf16[3584,512]{1,0:T(8,128)(2,1)} %bitcast.135), channel_id=1, source_target_pairs={{0,1},{1,0},{2,3},{3,2},{4,5},{5,4},{6,7},{7,6},{8,9},{9,8},{10,11... | collective-permute-start | bytes 11010056 | tf_op jit(solution)/shard_map/ppermute | solution.py:199
  18.9 16.7 %collective-permute-start.2 = (bf16[512,3584]{1,0:T(8,128)(2,1)}, bf16[512,3584]{1,0:T(8,128)(2,1)}, u32[]{:S(2)}, u32[]{:S(2)}) collective-permute-start(bf16[512,3584]{1,0:T(8,128)(2,1)} %bitcast.137), channel_id=1, source_target_pairs={{0,1},{1,0},{2,3},{3,2},{4,5},{5,4},{6,7},{7,6},{8,9},{9,8},{10,11... | collective-permute-start | bytes 11010056 | tf_op jit(solution)/shard_map/ppermute | solution.py:199
  465.7 12.6 %collective-permute-start.5 = (bf16[64,3584]{1,0:T(8,128)(2,1)}, bf16[64,3584]{1,0:T(8,128)(2,1)S(1)}, u32[]{:S(2)}, u32[]{:S(2)}) collective-permute-start(bf16[64,3584]{1,0:T(8,128)(2,1)} %get-tuple-element.15), channel_id=1, source_target_pairs={{0,96},{32,0},{64,32},{96,64},{1,97},{33,1},{65,33},{97,65},{2,98}... | collective-permute-start | bytes 1376264 | tf_op jit(solution)/shard_map/ppermute | solution.py:217
  466.1 22.8 %collective-permute-start.4 = (bf16[64,3584]{1,0:T(8,128)(2,1)}, bf16[64,3584]{1,0:T(8,128)(2,1)S(1)}, u32[]{:S(2)}, u32[]{:S(2)}) collective-permute-start(bf16[64,3584]{1,0:T(8,128)(2,1)} %get-tuple-element.16), channel_id=1, source_target_pairs={{0,64},{32,96},{64,0},{96,32},{1,65},{33,97},{65,1},{97,33},{2,66}... | collective-permute-start | bytes 1376264 | tf_op jit(solution)/shard_map/ppermute | solution.py:217
  468.7 21.0 %collective-permute-start.3 = (bf16[64,3584]{1,0:T(8,128)(2,1)}, bf16[64,3584]{1,0:T(8,128)(2,1)S(1)}, u32[]{:S(2)}, u32[]{:S(2)}) collective-permute-start(bf16[64,3584]{1,0:T(8,128)(2,1)} %get-tuple-element.14), channel_id=1, source_target_pairs={{0,32},{32,64},{64,96},{96,0},{1,33},{33,65},{65,97},{97,1},{2,34}... | collective-permute-start | bytes 1376264 | tf_op jit(solution)/shard_map/ppermute | solution.py:217
  492.9 2.9 copy-start.1
Sparse Core Ops, SparseCore 0:
  18.4 150.1 all-gather.1
  289.2 174.0 reduce-scatter.1

commit v2 on v1

v2 whole, which is shorter than its diff:
```python
import functools

import jax
import jax.numpy as jnp
from jax import lax
from jax.experimental import pallas as pl
from jax.experimental.pallas import tpu as pltpu
from jax.sharding import Mesh, PartitionSpec as P

BALANCE_SWEEPS = 20
EXPERTS = 32
CAP = 20
TOK = 64
GROUP = 256
SLOTS = GROUP // TOK * CAP
GATE_LANES = 128
RING = 4
PLANE_COLS = 1280


def mix_coefficients(streams, phi_matrix, mix_scale, mix_bias):
    count = streams.shape[1]
    flat = streams.astype(jnp.float32).reshape(streams.shape[0], -1)
    normed = flat * lax.rsqrt(jnp.mean(flat * flat, axis=1, keepdims=True) + 1e-06)
    normed = normed.astype(jnp.bfloat16)
    coeffs = lax.dot_general(
        normed, phi_matrix, (((1,), (1,)), ((), ())), preferred_element_type=jnp.float32
    )
    pre = jax.nn.sigmoid(mix_scale[0] * coeffs[:, :count] + mix_bias[:count])
    post = 2.0 * jax.nn.sigmoid(
        mix_scale[1] * coeffs[:, count : 2 * count] + mix_bias[count : 2 * count]
    )
    logits = mix_scale[2] * coeffs[:, 2 * count :] + mix_bias[2 * count :]
    mixing = jnp.exp(logits).reshape(-1, count, count)
    for sweep_step in range(BALANCE_SWEEPS):
        mixing = mixing / jnp.sum(mixing, axis=2, keepdims=True)
        mixing = mixing / jnp.sum(mixing, axis=1, keepdims=True)
    return (pre, post, mixing)


def mix_input(streams, pre):
    total = pre[:, 0, None] * streams[:, 0, :].astype(jnp.float32)
    for stream in range(1, streams.shape[1]):
        total = total + pre[:, stream, None] * streams[:, stream, :].astype(jnp.float32)
    return total.astype(jnp.bfloat16)


def mix_output(streams, mixing, post, moe_out):
    rows = []
    for target in range(streams.shape[1]):
        total = mixing[:, target, 0, None] * streams[:, 0, :].astype(jnp.float32)
        for source in range(1, streams.shape[1]):
            total = total + mixing[:, target, source, None] * streams[:, source, :].astype(
                jnp.float32
            )
        rows.append(total + post[:, target, None] * moe_out)
    return jnp.stack(rows, axis=1).astype(jnp.bfloat16)


def dense_gates(layer_in, router, expert_index_table):
    logits = lax.dot_general(
        layer_in, router, (((1,), (1,)), ((), ())), preferred_element_type=jnp.float32
    )
    affinity = jax.nn.sigmoid(logits)
    experts = lax.iota(jnp.int32, EXPERTS)
    named = jnp.any(expert_index_table[:, :, None] == experts[None, None, :], axis=1)
    chosen = jnp.where(named, affinity, 0.0)
    gates = 2.5 * chosen / jnp.sum(chosen, axis=1, keepdims=True)
    high = lax.reduce_precision(gates, 8, 7)
    low = gates - high
    pad = jnp.zeros((gates.shape[0], GATE_LANES - 2 * EXPERTS), jnp.float32)
    return jnp.concatenate([high, low, pad], axis=1).astype(jnp.bfloat16)


def slots_of_group(ids, gates, before):
    lane = lax.broadcasted_iota(jnp.int32, (GROUP, GATE_LANES), 1)
    block = lax.broadcasted_iota(jnp.int32, (GROUP, 1), 0) // TOK
    slot_of = lax.broadcasted_iota(jnp.int32, (GROUP, GROUP), 1)
    hit = (gates.astype(jnp.float32) != 0.0).astype(jnp.float32)
    rank = jnp.dot(before, hit.astype(jnp.bfloat16), preferred_element_type=jnp.float32)
    slots = []
    for e in range(2):
        mine = lane == ids[e]
        rank_e = jnp.sum(jnp.where(mine, rank, 0.0), axis=1, keepdims=True)
        hit_e = jnp.sum(jnp.where(mine, hit, 0.0), axis=1, keepdims=True)
        place = rank_e.astype(jnp.int32) + block * CAP + e * SLOTS
        slots.append(jnp.where(hit_e > 0.0, place, -1))
    return ((slot_of == slots[0]) | (slot_of == slots[1])).astype(jnp.float32)


def hidden_kernel(
    ids, gates_ref, x_ref, wg0, wu0, wg1, wu1, hid_ref, st_ref, pick_ref, gate_ref, rows_ref, acc_ref
):
    step, steps = pl.program_id(0), pl.num_programs(0)
    groups = gates_ref.shape[0] // GROUP
    chunk = rows_ref.shape[1] // 4

    @pl.when(step == 0)
    def _():
        acc_ref[...] = jnp.zeros_like(acc_ref)
        row = lax.broadcasted_iota(jnp.int32, (GROUP, GROUP), 0)
        col = lax.broadcasted_iota(jnp.int32, (GROUP, GROUP), 1)
        before = (col < row) & (col // TOK == row // TOK)
        before = before.astype(jnp.float32).astype(jnp.bfloat16)
        slot_lane = lax.broadcasted_iota(jnp.int32, (SLOTS, GATE_LANES), 1)

        @pl.loop(0, groups)
        def _(g):
            gates = gates_ref[pl.ds(pl.multiple_of(g * GROUP, GROUP), GROUP), :]
            st = slots_of_group(ids, gates, before)
            st_ref[g] = st[:, : 2 * SLOTS].astype(jnp.bfloat16)
            pick = jnp.transpose(st)[: 2 * SLOTS].astype(jnp.bfloat16)
            pick_ref[g] = pick
            picked = jnp.dot(pick, gates, preferred_element_type=jnp.float32)
            for e in range(2):
                own = picked[e * SLOTS : (e + 1) * SLOTS]
                wanted = (slot_lane == ids[e]) | (slot_lane == ids[e] + EXPERTS)
                own = jnp.sum(jnp.where(wanted, own, 0.0), axis=1, keepdims=True)
                gate_ref[e, pl.ds(pl.multiple_of(g * SLOTS, 16), SLOTS), :] = jnp.broadcast_to(
                    own, (SLOTS, GATE_LANES)
                )

    @pl.loop(0, groups)
    def _(g):
        x = x_ref[pl.ds(pl.multiple_of(g * GROUP, GROUP), GROUP), :]
        rows = jnp.dot(pick_ref[g], x, preferred_element_type=jnp.float32).astype(jnp.bfloat16)
        for e in range(2):
            rows_ref[e, pl.ds(pl.multiple_of(g * SLOTS, 16), SLOTS), :] = rows[
                e * SLOTS : (e + 1) * SLOTS
            ]

    for e, pair in enumerate(((wg0, wu0), (wg1, wu1))):
        for which, w in enumerate(pair):

            @pl.loop(0, rows_ref.shape[1] // chunk)
            def _(m):
                part = pl.ds(pl.multiple_of(m * chunk, 16), chunk)
                acc_ref[e, which, part, :] += jnp.dot(
                    rows_ref[e, part, :], w[...], preferred_element_type=jnp.float32
                )

    @pl.when(step == steps - 1)
    def _():
        for e in range(2):

            @pl.loop(0, rows_ref.shape[1] // chunk)
            def _(m):
                part = pl.ds(pl.multiple_of(m * chunk, 16), chunk)
                gate_part = acc_ref[e, 0, part, :]
                hidden = gate_part / (1.0 + jnp.exp(-gate_part)) * acc_ref[e, 1, part, :]
                hid_ref[e, part, :] = (hidden * gate_ref[e, part, 0:1]).astype(jnp.bfloat16)


def hidden_call(ids, gathered, up_weights, width, ff):
    tokens = gathered.shape[0]
    tile = min(512, width)
    groups = tokens // GROUP
    rows = groups * SLOTS
    weight = pl.BlockSpec((tile, ff), lambda n, ids: (n, 0))
    return pl.pallas_call(
        hidden_kernel,
        out_shape=(
            jax.ShapeDtypeStruct((2, rows, ff), jnp.bfloat16),
            jax.ShapeDtypeStruct((groups, GROUP, 2 * SLOTS), jnp.bfloat16),
        ),
        grid_spec=pltpu.PrefetchScalarGridSpec(
            num_scalar_prefetch=1,
            grid=(width // tile,),
            in_specs=[
                pl.BlockSpec((tokens, GATE_LANES), lambda n, ids: (0, width // GATE_LANES)),
                pl.BlockSpec((tokens, tile), lambda n, ids: (0, n)),
                weight, weight, weight, weight,
            ],
            out_specs=(
                pl.BlockSpec((2, rows, ff), lambda n, ids: (0, 0, 0)),
                pl.BlockSpec((groups, GROUP, 2 * SLOTS), lambda n, ids: (0, 0, 0)),
            ),
            scratch_shapes=[
                pltpu.VMEM((groups, 2 * SLOTS, GROUP), jnp.bfloat16),
                pltpu.VMEM((2, rows, GATE_LANES), jnp.float32),
                pltpu.VMEM((2, rows, tile), jnp.bfloat16),
                pltpu.VMEM((2, 2, rows, ff), jnp.float32),
            ],
        ),
        compiler_params=pltpu.CompilerParams(
            dimension_semantics=("arbitrary",), vmem_limit_bytes=52 << 20
        ),
        cost_estimate=pl.CostEstimate(
            flops=8 * rows * width * ff, bytes_accessed=2 * tokens * width, transcendentals=0
        ),
        name="hidden",
    )(ids, gathered, gathered, *up_weights)


def down_kernel(plane_first, plane, hid_ref, st_ref, wd0, wd1, o_ref, y_ref):
    groups = st_ref.shape[0]
    batch = groups // 4
    chunk = batch * SLOTS
    for e, w in enumerate((wd0, wd1)):

        @pl.loop(0, 4)
        def _(m):
            part = jnp.dot(
                hid_ref[e, pl.ds(pl.multiple_of(m * chunk, 16), chunk), :],
                w[...],
                preferred_element_type=jnp.float32,
            ).astype(jnp.bfloat16)
            for j in range(batch):
                y_ref[m * batch + j, e * SLOTS : (e + 1) * SLOTS, :] = part[
                    j * SLOTS : (j + 1) * SLOTS
                ]

    half = pl.program_id(0)

    @pl.loop(0, groups)
    def _(g):
        out = jnp.dot(st_ref[g], y_ref[g], preferred_element_type=jnp.float32)
        out = out.astype(jnp.bfloat16)
        z, y = g // RING, g % RING
        if plane_first:
            ahead, behind = (plane[0] + 3 - z) & 3, (z + 3 - plane[0]) & 3
            stop = jnp.where(half == 0, ahead, behind)
            o_ref[0, stop, pl.ds(pl.multiple_of(y * GROUP, GROUP), GROUP), :] = out
        else:
            for b in range(RING):
                o_ref[y * RING + b, z, :, :] = out[b * TOK : (b + 1) * TOK]


def down_call(plane, hidden, chosen, down_weights, first, tile, count, plane_first):
    rows, ff = hidden.shape[1:]
    groups = chosen.shape[0]
    columns = tile * count
    skip = first // tile
    whole = lambda shape: pl.BlockSpec(
        shape, lambda n, plane: (0, 0, 0), pipeline_mode=pl.Buffered(1)
    )
    weight = pl.BlockSpec((ff, tile), lambda n, plane: (0, n + skip))
    if plane_first:
        shape = (count, RING, RING * GROUP, tile)
        block = pl.BlockSpec((1,) + shape[1:], lambda n, plane: (n, 0, 0, 0))
    else:
        shape = (RING * RING, RING, TOK, columns)
        block = pl.BlockSpec(shape[:3] + (tile,), lambda n, plane: (0, 0, 0, n))
    return pl.pallas_call(
        functools.partial(down_kernel, plane_first),
        out_shape=jax.ShapeDtypeStruct(shape, jnp.bfloat16),
        grid_spec=pltpu.PrefetchScalarGridSpec(
            num_scalar_prefetch=1,
            grid=(count,),
            in_specs=[
                whole(hidden.shape), whole(chosen.shape), weight, weight,
            ],
            out_specs=block,
            scratch_shapes=[pltpu.VMEM((groups, 2 * SLOTS, tile), jnp.bfloat16)],
        ),
        compiler_params=pltpu.CompilerParams(
            dimension_semantics=("arbitrary",), vmem_limit_bytes=40 << 20
        ),
        cost_estimate=pl.CostEstimate(
            flops=4 * rows * columns * ff,
            bytes_accessed=2 * groups * GROUP * columns,
            transcendentals=0,
        ),
        name="down_plane" if plane_first else "down",
    )(plane, hidden, chosen, *down_weights)


def add_rounded(a, b):
    return (a.astype(jnp.float32) + b.astype(jnp.float32)).astype(jnp.bfloat16)


def body(
    streams, phi_matrix, mix_scale, mix_bias, router, expert_index_table, w_gate, w_up, down_weight
):
    width, ff = w_gate.shape[1], w_gate.shape[2]
    swap = [(0, 1), (1, 0)]
    own = (w_gate[0], w_up[0], down_weight[0])
    other = tuple(lax.ppermute(w, "c", swap) for w in own)
    pre, post, mixing = mix_coefficients(streams, phi_matrix, mix_scale, mix_bias)
    layer_in = mix_input(streams, pre)
    gates = dense_gates(layer_in, router, expert_index_table)
    packed = jnp.concatenate([layer_in, gates], axis=1)
    gathered = lax.all_gather(packed, ("z", "y", "x"), axis=0, tiled=True)
    core = lax.axis_index("c")
    pair = 2 * (lax.axis_index("y") * RING + lax.axis_index("x"))
    ids = jnp.stack([pair + core, pair + 1 - core]).astype(jnp.int32)
    plane = lax.axis_index("z")
    planes = plane.reshape(1).astype(jnp.int32)
    ups, downs = own[:2] + other[:2], (own[2], other[2])
    hidden, chosen = hidden_call(ids, gathered, ups, width, ff)
    late = width - PLANE_COLS
    dense = down_call(planes, hidden, chosen, downs, PLANE_COLS, 256, late // 256, False)
    summed = lax.psum_scatter(
        dense.reshape(-1, late), ("y", "x"), scatter_dimension=0, tiled=True
    ).reshape(RING, TOK, late)
    halves = down_call(planes, hidden, chosen, downs, 0, PLANE_COLS // 2, 2, True)
    travel = [halves[0, 0], halves[1, 0]]
    for stop in range(1, RING):
        for way, turn in ((0, 1), (1, RING - 1)):
            ring = [(i, (i + turn) % RING) for i in range(RING)]
            travel[way] = add_rounded(lax.ppermute(travel[way], "z", ring), halves[way, stop])
    early_out = lax.psum_scatter(
        jnp.concatenate(travel, axis=1), ("y", "x"), scatter_dimension=0, tiled=True
    ).astype(jnp.float32)
    late_out = lax.dynamic_index_in_dim(summed, plane, 0, keepdims=False).astype(jnp.float32)
    for shift in range(1, RING):
        away = lax.dynamic_index_in_dim(summed, (plane + shift) % RING, 0, keepdims=False)
        ring = [(i, (i + shift) % RING) for i in range(RING)]
        late_out = late_out + lax.ppermute(away, "z", ring).astype(jnp.float32)
    moe_out = jnp.concatenate([early_out, late_out], axis=1)
    return mix_output(streams, mixing, post, moe_out)


def solution(mesh):
    torus = Mesh(mesh.devices.reshape(RING, RING, RING, 2), ("z", "y", "x", "c"))
    tokens, experts = ("z", "y", "x", "c"), ("y", "x", "c")
    in_specs = (
        P(tokens, None, None),
        P(),
        P(),
        P(),
        P(),
        P(tokens, None),
        P(experts, None, "z"),
        P(experts, None, "z"),
        P(experts, "z", None),
    )
    out_specs = P(tokens, None, None)
    return jax.shard_map(
        body, mesh=torus, in_specs=in_specs, out_specs=out_specs, check_vma=False
    )
```

time: 508 us -> 515 us (1.014)
  waiting for transfers between devices: 341 us -> 303 us
  Pallas kernels: 120 us -> 144 us
  local copies, waits for them, and re-layouts: 10.4 us -> 19.9 us
  starting transfers between devices: 5.58 us -> 13 us
  other arithmetic: 10.8 us -> 17.5 us
    reduce_scatter x1 -> x2, waiting for transfers between devices: 173 us -> 68.1 us  [the longest x1 68 us: body(): lax.psum_scatter(jnp.concatenate(travel, axis=1), ('y', 'x'), scatter_dim...]
    ppermute x3 -> x9, waiting for transfers between devices: 19.2 us -> 85.5 us  [the longest x6 85.5 us: body(): lax.ppermute(travel[way], 'z', ring)]
    pallas_call x1 -> x3, Pallas kernels: 120 us -> 144 us  [the longest x1 79.1 us: hidden_call(): pl.pallas_call(hidden_kernel, out_shape=(jax.ShapeDtypeStruct((2, rows, f...]
    unnamed x16 -> x38, local copies, waits for them, and re-layouts: 0.95 us -> 9.3 us
    ppermute x3 -> x9, starting transfers between devices: 4.86 us -> 12.3 us  [the longest x6 6.61 us: body(): lax.ppermute(travel[way], 'z', ring)]
    all_gather x1, waiting for transfers between devices: 133 us -> 138 us  [body(): gathered = lax.all_gather(packed, ('z', 'y', 'x'), axis=0, tiled=True)]
  transfers between devices with their start and end apart: 8 -> 15, of which waited for: 8 -> 10; matrix products, arithmetic and copies ran while one was open for 0% -> 2% of each run, Pallas kernels for 0% -> 19%
where the time goes in v2:
time: 515 us; the launch traced here: 512 us
  waiting for transfers between devices  303 us (59%)
  Pallas kernels  144 us (28%)
  local copies, waits for them, and re-layouts  19.9 us (4%)
  other arithmetic  17.5 us (3%)
  between operations  13.5 us (3%)
  starting transfers between devices  13 us (3%)
    all_gather x1, waiting for transfers between devices, body(): gathered = lax.all_gather(packed, ('z', 'y', 'x'), axis=0, tiled=True)  138 us
    ppermute x6, waiting for transfers between devices, body(): lax.ppermute(travel[way], 'z', ring)  85.5 us
    pallas_call x1, Pallas kernels, hidden_call(): pl.pallas_call(hidden_kernel, out_shape=(jax.ShapeDtypeStruct((2, rows, f...  79.1 us
    reduce_scatter x1, waiting for transfers between devices, body(): lax.psum_scatter(jnp.concatenate(travel, axis=1), ('y', 'x'), scatter_dim...  68 us
    pallas_call x2, Pallas kernels, down_call(): pl.pallas_call(functools.partial(down_kernel, plane_first), out_shape=jax...  64.7 us
    ppermute x3, waiting for transfers between devices, body(): other = tuple((lax.ppermute(w, 'c', swap) for w in own))  11.3 us
  transfers between devices with their start and end apart: 15, of which 10 were waited for; matrix products, arithmetic and copies ran while one was open for 2% of the time, Pallas kernels for 19%

profile of v2, /device:TPU:44, one launch (start us, length us, event | category | flops | bytes accessed | tf_op | source)
XLA Modules:
  0.0 511.8 jit_solution(744886940291873389)
XLA Ops:
  6.5 3.1 multiply_reduce_fusion
  9.6 2.7 fusion.115
  12.3 0.5 copy.29
  12.8 0.1 copy-done.16
  13.0 0.1 fusion.117
  13.1 0.7 fusion.116
  13.7 0.7 fusion.25
  14.4 1.4 fusion.95
  15.9 0.1 copy.22
  16.0 1.8 fusion.74
  17.8 0.4 fusion.118
  18.1 0.1 fusion.82
  18.3 0.9 concatenate.46
  19.1 0.0 all-gather.2.cloned.1.call-update
  19.1 0.0 reduce-scatter.5.cloned.1.call-start
  19.2 0.1 collective-permute-start
  19.3 0.5 collective-permute-start.1
  19.8 0.1 collective-permute-start.2
  19.9 0.1 pad_add_fusion.ids
  20.0 6.1 %collective-permute-done.wg1 = bf16[3584,512]{1,0:T(8,128)(2,1)} collective-permute-done((bf16[3584,512]{1,0:T(8,128)(2,1)}, bf16[3584,512]{1,0:T(8,128)(2,1)}, u32[]{:S(2)}, u32[]{:S(2)}) %collective-permute-start) | collective-permute-done | bytes 3670048 | tf_op jit(solution)/shard_map/ppermute | solution.py:278
  26.0 5.2 %collective-permute-done.1.wu1 = bf16[3584,512]{1,0:T(8,128)(2,1)} collective-permute-done((bf16[3584,512]{1,0:T(8,128)(2,1)}, bf16[3584,512]{1,0:T(8,128)(2,1)}, u32[]{:S(2)}, u32[]{:S(2)}) %collective-permute-start.1) | collective-permute-done | bytes 3670048 | tf_op jit(solution)/shard_map/ppermute | solution.py:278
  31.3 138.2 %all-gather.2.cloned.1.call-done.gates_ref.x_ref = bf16[4096,3712]{1,0:T(8,128)(2,1)} async-done(((bf16[64,3712]{1,0:T(8,128)(2,1)}), bf16[4096,3712]{1,0:T(8,128)(2,1)}) %all-gather.2.cloned.1.call-update) | async-done | bytes 30408720 | tf_op jit(solution)/shard_map/all_gather | solution.py:283
  169.4 79.1 %hidden.1 = (bf16[2,1280,512]{2,1,0:T(8,128)(2,1)}, bf16[16,256,160]{2,1,0:T(8,128)(2,1)}) custom-call(s32[2]{0:T(128)S(1)} %pad_add_fusion.ids, bf16[4096,3712]{1,0:T(8,128)(2,1)} %all-gather.2.cloned.1.call-done.gates_ref.x_ref, bf16[4096,3712]{1,0:T(8,128)(2,1)} %all-gather.2.cloned.1.call-done.gates_ref.x_ref, bf16[3584,512]{1,0:T(8,128)(2,1)} %bitcast.155, ...), custom_call_target="tpu_custom_call" | custom-call | flops 18790481920 | bytes 29360128 | tf_op jit(solution)/shard_map/hidden/pallas_call | solution.py:160
  248.5 1.7 copy-done.4
  250.2 1.6 copy-done.6
  251.8 46.2 %down.1 = bf16[16,4,64,2304]{3,2,1,0:T(8,128)(2,1)} custom-call(s32[1]{0:T(128)} %bitcast.8.plane, bf16[2,1280,512]{2,1,0:T(8,128)(2,1)S(1)} %copy-done.4, bf16[16,256,160]{2,1,0:T(8,128)(2,1)S(1)} %copy-done.6, bf16[512,3584]{1,0:T(8,128)(2,1)S(1)} %bitcast.149, bf16[512,3584]{1,0:T(8,128)(2,1)} %collective-permute-done.2.wd1), custom_call_target="tpu_custom_call" | custom-call | flops 6039797760 | bytes 18874368 | tf_op jit(solution)/shard_map/down/pallas_call | solution.py:244
  298.0 0.0 reduce-scatter.5.cloned.1.call-update
  298.1 0.0 reduce-scatter.3.cloned.1.call-start
  298.1 1.7 copy-done.5
  299.8 2.0 copy-done.3
  301.8 1.6 copy-done.7
  303.4 18.5 %down_plane.1 = bf16[2,4,1024,640]{3,2,1,0:T(8,128)(2,1)} custom-call(s32[1]{0:T(128)} %bitcast.8.plane, bf16[2,1280,512]{2,1,0:T(8,128)(2,1)S(1)} %copy-done.5, bf16[16,256,160]{2,1,0:T(8,128)(2,1)S(1)} %copy-done.7, bf16[512,3584]{1,0:T(8,128)(2,1)S(1)} %bitcast.150, bf16[512,3584]{1,0:T(8,128)(2,1)} %collective-permute-done.2.wd1), custom_call_target="tpu_custom_call" | custom-call | flops 3355443200 | bytes 10485760 | tf_op jit(solution)/shard_map/down_plane/pallas_call | solution.py:244
  321.9 2.1 slice_bitcast_fusion.7
  324.0 1.3 collective-permute-start.3
  325.3 0.8 collective-permute-start.6
  326.1 28.4 %collective-permute-done.3 = bf16[1024,640]{1,0:T(8,128)(2,1)S(1)} collective-permute-done((bf16[1024,640]{1,0:T(8,128)(2,1)S(1)}, bf16[1024,640]{1,0:T(8,128)(2,1)S(1)}, u32[]{:S(2)}, u32[]{:S(2)}) %collective-permute-start.3) | collective-permute-done | bytes 1310752 | tf_op jit(solution)/shard_map/ppermute | solution.py:301
  354.5 0.9 collective-permute-done.6
  355.4 2.4 fusion.24
  357.8 1.5 collective-permute-start.4
  359.3 0.9 collective-permute-start.7
  360.3 27.4 %collective-permute-done.4 = bf16[1024,640]{1,0:T(8,128)(2,1)S(1)} collective-permute-done((bf16[1024,640]{1,0:T(8,128)(2,1)S(1)}, bf16[1024,640]{1,0:T(8,128)(2,1)S(1)}, u32[]{:S(2)}, u32[]{:S(2)}) %collective-permute-start.4) | collective-permute-done | bytes 1310752 | tf_op jit(solution)/shard_map/ppermute | solution.py:301
  387.7 1.8 collective-permute-done.7
  389.5 0.6 fusion.23
  390.1 1.8 collective-permute-start.5
  392.0 0.3 collective-permute-start.8
  392.2 0.1 slice.161
  392.3 0.7 fusion.84
  393.0 25.5 %collective-permute-done.5 = bf16[1024,640]{1,0:T(8,128)(2,1)S(1)} collective-permute-done((bf16[1024,640]{1,0:T(8,128)(2,1)S(1)}, bf16[1024,640]{1,0:T(8,128)(2,1)S(1)}, u32[]{:S(2)}, u32[]{:S(2)}) %collective-permute-start.5) | collective-permute-done | bytes 1310752 | tf_op jit(solution)/shard_map/ppermute | solution.py:301
  418.5 1.4 collective-permute-done.8
  420.0 0.6 fusion.22
  420.6 1.7 pad_maximum_fusion
  422.3 0.0 reduce-scatter.3.cloned.1.call-update
  423.2 0.0 reduce-scatter.5.cloned.1.call-done
  423.3 1.3 dynamic-slice_bitcast_fusion.2
  424.6 1.2 collective-permute-start.11
  425.8 2.0 collective-permute-start.10
  427.9 2.4 collective-permute-start.9
  430.3 68.0 %reduce-scatter.3.cloned.1.call-done = bf16[64,1280]{1,0:T(8,128)(2,1)} async-done(((bf16[1024,1280]{1,0:T(8,128)(2,1)}), bf16[64,1280]{1,0:T(8,128)(2,1)}) %reduce-scatter.3.cloned.1.call-update) | async-done | bytes 163856 | tf_op jit(solution)/shard_map/reduce_scatter | solution.py:302
  498.3 0.9 bitcast_convert_fusion
  499.3 1.2 fusion.80
  500.5 0.9 fusion.59
  501.4 0.9 fusion.54
  502.3 0.2 pad_maximum_fusion.1
  502.6 2.6 copy.23
  (64 shorter events, 0.9 us)
Async XLA Ops:
  6.5 7.2 %copy-start = (bf16[24,14336]{1,0:T(8,128)(2,1)S(1)}, bf16[24,14336]{1,0:T(8,128)(2,1)}, u32[]{:S(2)}) copy-start(bf16[24,14336]{1,0:T(8,128)(2,1)} %param.10) | copy-start | bytes 2064388
  6.5 3.1 copy-start.9
  6.5 162.9 %all-gather.2.cloned.1.call-start = ((), (), s32[]{:S(2)}) async-start(), calls=%async_computation.2 | async-start | bytes 30883840 | tf_op jit(solution)/shard_map/all_gather | solution.py:283
  12.3 0.7 copy-start.16
  12.3 0.7 copy-start.14
  13.7 2.1 copy-start.15
  16.0 1.8 copy-start.17
  19.1 404.1 %reduce-scatter.5.cloned.1.call-start = ((), (), s32[]{:S(2)}) async-start(), calls=%async_computation.4 | async-start | bytes 20054016 | tf_op jit(solution)/shard_map/reduce_scatter | solution.py:293
  19.2 6.8 %collective-permute-start = (bf16[3584,512]{1,0:T(8,128)(2,1)}, bf16[3584,512]{1,0:T(8,128)(2,1)}, u32[]{:S(2)}, u32[]{:S(2)}) collective-permute-start(bf16[3584,512]{1,0:T(8,128)(2,1)} %bitcast.154), channel_id=1, source_target_pairs={{0,1},{1,0},{2,3},{3,2},{4,5},{5,4},{6,7},{7,6},{8,9},{9,8},{10,11... | collective-permute-start | bytes 11010056 | tf_op jit(solution)/shard_map/ppermute | solution.py:278
  19.3 12.0 %collective-permute-start.1 = (bf16[3584,512]{1,0:T(8,128)(2,1)}, bf16[3584,512]{1,0:T(8,128)(2,1)}, u32[]{:S(2)}, u32[]{:S(2)}) collective-permute-start(bf16[3584,512]{1,0:T(8,128)(2,1)} %bitcast.156), channel_id=1, source_target_pairs={{0,1},{1,0},{2,3},{3,2},{4,5},{5,4},{6,7},{7,6},{8,9},{9,8},{10,11... | collective-permute-start | bytes 11010056 | tf_op jit(solution)/shard_map/ppermute | solution.py:278
  19.8 228.7 %collective-permute-start.2 = (bf16[512,3584]{1,0:T(8,128)(2,1)}, bf16[512,3584]{1,0:T(8,128)(2,1)}, u32[]{:S(2)}, u32[]{:S(2)}) collective-permute-start(bf16[512,3584]{1,0:T(8,128)(2,1)} %bitcast.148), channel_id=1, source_target_pairs={{0,1},{1,0},{2,3},{3,2},{4,5},{5,4},{6,7},{7,6},{8,9},{9,8},{10,11... | collective-permute-start | bytes 11010056 | tf_op jit(solution)/shard_map/ppermute | solution.py:278
  169.4 79.1 %copy-start.2 = (bf16[1,512,3584]{2,1,0:T(8,128)(2,1)S(1)}, bf16[1,512,3584]{2,1,0:T(8,128)(2,1)}, u32[]{:S(2)}) copy-start(bf16[1,512,3584]{2,1,0:T(8,128)(2,1)} %param.17) | copy-start | bytes 11010052
  248.5 1.7 copy-start.4
  250.2 1.6 copy-start.6
  298.0 1.7 copy-start.5
  298.1 200.2 %reduce-scatter.3.cloned.1.call-start = ((), (), s32[]{:S(2)}) async-start(), calls=%async_computation.3 | async-start | bytes 2785280 | tf_op jit(solution)/shard_map/reduce_scatter | solution.py:302
  299.8 2.0 copy-start.3
  301.8 1.6 copy-start.7
  321.9 67.6 %copy-start.8 = (bf16[2,4,1024,640]{3,2,1,0:T(8,128)(2,1)S(1)}, bf16[2,4,1024,640]{3,2,1,0:T(8,128)(2,1)}, u32[]{:S(2)}) copy-start(bf16[2,4,1024,640]{3,2,1,0:T(8,128)(2,1)} %down_plane.1) | copy-start | bytes 31457284
  324.0 30.5 %collective-permute-start.3 = (bf16[1024,640]{1,0:T(8,128)(2,1)S(1)}, bf16[1024,640]{1,0:T(8,128)(2,1)S(1)}, u32[]{:S(2)}, u32[]{:S(2)}) collective-permute-start(bf16[1024,640]{1,0:T(8,128)(2,1)S(1)} %get-tuple-element.20), channel_id=1, source_target_pairs={{0,32},{32,64},{64,96},{96,0},{1,33},{33,65},{65,97},{97,1},{2,34}... | collective-permute-start | bytes 3932168 | tf_op jit(solution)/shard_map/ppermute | solution.py:301
  325.3 30.1 %collective-permute-start.6 = (bf16[1024,640]{1,0:T(8,128)(2,1)S(1)}, bf16[1024,640]{1,0:T(8,128)(2,1)S(1)}, u32[]{:S(2)}, u32[]{:S(2)}) collective-permute-start(bf16[1024,640]{1,0:T(8,128)(2,1)S(1)} %get-tuple-element.21), channel_id=1, source_target_pairs={{0,96},{32,0},{64,32},{96,64},{1,97},{33,1},{65,33},{97,65},{2,98}... | collective-permute-start | bytes 3932168 | tf_op jit(solution)/shard_map/ppermute | solution.py:301
  357.8 29.9 %collective-permute-start.4 = (bf16[1024,640]{1,0:T(8,128)(2,1)S(1)}, bf16[1024,640]{1,0:T(8,128)(2,1)S(1)}, u32[]{:S(2)}, u32[]{:S(2)}) collective-permute-start(bf16[1024,640]{1,0:T(8,128)(2,1)S(1)} %get-tuple-element.18), channel_id=1, source_target_pairs={{0,32},{32,64},{64,96},{96,0},{1,33},{33,65},{65,97},{97,1},{2,34}... | collective-permute-start | bytes 3932168 | tf_op jit(solution)/shard_map/ppermute | solution.py:301
  359.3 30.2 %collective-permute-start.7 = (bf16[1024,640]{1,0:T(8,128)(2,1)S(1)}, bf16[1024,640]{1,0:T(8,128)(2,1)S(1)}, u32[]{:S(2)}, u32[]{:S(2)}) collective-permute-start(bf16[1024,640]{1,0:T(8,128)(2,1)S(1)} %get-tuple-element.19), channel_id=1, source_target_pairs={{0,96},{32,0},{64,32},{96,64},{1,97},{33,1},{65,33},{97,65},{2,98}... | collective-permute-start | bytes 3932168 | tf_op jit(solution)/shard_map/ppermute | solution.py:301
  390.1 28.4 %collective-permute-start.5 = (bf16[1024,640]{1,0:T(8,128)(2,1)S(1)}, bf16[1024,640]{1,0:T(8,128)(2,1)S(1)}, u32[]{:S(2)}, u32[]{:S(2)}) collective-permute-start(bf16[1024,640]{1,0:T(8,128)(2,1)S(1)} %get-tuple-element.16), channel_id=1, source_target_pairs={{0,32},{32,64},{64,96},{96,0},{1,33},{33,65},{65,97},{97,1},{2,34}... | collective-permute-start | bytes 3932168 | tf_op jit(solution)/shard_map/ppermute | solution.py:301
  392.0 28.0 %collective-permute-start.8 = (bf16[1024,640]{1,0:T(8,128)(2,1)S(1)}, bf16[1024,640]{1,0:T(8,128)(2,1)S(1)}, u32[]{:S(2)}, u32[]{:S(2)}) collective-permute-start(bf16[1024,640]{1,0:T(8,128)(2,1)S(1)} %get-tuple-element.17), channel_id=1, source_target_pairs={{0,96},{32,0},{64,32},{96,64},{1,97},{33,1},{65,33},{97,65},{2,98}... | collective-permute-start | bytes 3932168 | tf_op jit(solution)/shard_map/ppermute | solution.py:301
  423.2 77.2 %copy-start.10 = (bf16[64,1,3584]{2,0,1:T(8,128)(2,1)S(1)}, bf16[64,1,3584]{2,0,1:T(8,128)(2,1)}, u32[]{:S(2)}) copy-start(bf16[64,1,3584]{2,0,1:T(8,128)(2,1)} %get-tuple-element.10) | copy-start | bytes 1376260
  423.2 77.2 %copy-start.11 = (bf16[64,1,3584]{2,0,1:T(8,128)(2,1)S(1)}, bf16[64,1,3584]{2,0,1:T(8,128)(2,1)}, u32[]{:S(2)}) copy-start(bf16[64,1,3584]{2,0,1:T(8,128)(2,1)} %get-tuple-element.11) | copy-start | bytes 1376260
  423.3 77.2 %copy-start.12 = (bf16[64,1,3584]{2,0,1:T(8,128)(2,1)S(1)}, bf16[64,1,3584]{2,0,1:T(8,128)(2,1)}, u32[]{:S(2)}) copy-start(bf16[64,1,3584]{2,0,1:T(8,128)(2,1)} %get-tuple-element.12) | copy-start | bytes 1376260
  423.3 77.2 %copy-start.13 = (bf16[64,1,3584]{2,0,1:T(8,128)(2,1)S(1)}, bf16[64,1,3584]{2,0,1:T(8,128)(2,1)}, u32[]{:S(2)}) copy-start(bf16[64,1,3584]{2,0,1:T(8,128)(2,1)} %get-tuple-element.13) | copy-start | bytes 1376260
  424.6 74.6 %collective-permute-start.11 = (bf16[64,2304]{1,0:T(8,128)(2,1)S(1)}, bf16[64,2304]{1,0:T(8,128)(2,1)S(1)}, u32[]{:S(2)}, u32[]{:S(2)}) collective-permute-start(bf16[64,2304]{1,0:T(8,128)(2,1)S(1)} %get-tuple-element.31), channel_id=1, source_target_pairs={{0,96},{32,0},{64,32},{96,64},{1,97},{33,1},{65,33},{97,65},{2,98}... | collective-permute-start | bytes 884744 | tf_op jit(solution)/shard_map/ppermute | solution.py:309
  425.8 73.4 %collective-permute-start.10 = (bf16[64,2304]{1,0:T(8,128)(2,1)S(1)}, bf16[64,2304]{1,0:T(8,128)(2,1)S(1)}, u32[]{:S(2)}, u32[]{:S(2)}) collective-permute-start(bf16[64,2304]{1,0:T(8,128)(2,1)S(1)} %get-tuple-element.32), channel_id=1, source_target_pairs={{0,64},{32,96},{64,0},{96,32},{1,65},{33,97},{65,1},{97,33},{2,66}... | collective-permute-start | bytes 884744 | tf_op jit(solution)/shard_map/ppermute | solution.py:309
  427.9 71.4 %collective-permute-start.9 = (bf16[64,2304]{1,0:T(8,128)(2,1)S(1)}, bf16[64,2304]{1,0:T(8,128)(2,1)}, u32[]{:S(2)}, u32[]{:S(2)}) collective-permute-start(bf16[64,2304]{1,0:T(8,128)(2,1)S(1)} %get-tuple-element.30), channel_id=1, source_target_pairs={{0,32},{32,64},{64,96},{96,0},{1,33},{33,65},{65,97},{97,1},{2,34}... | collective-permute-start | bytes 884744 | tf_op jit(solution)/shard_map/ppermute | solution.py:309
  502.3 2.9 copy-start.1
Sparse Core Ops, SparseCore 0:
  19.3 150.1 all-gather.1
  298.2 120.6 reduce-scatter.4
  422.4 75.8 reduce-scatter.2

commit v3 on v1

v3 whole, which is shorter than its diff:
```python
import functools

import jax
import jax.numpy as jnp
from jax import lax
from jax.experimental import pallas as pl
from jax.experimental.pallas import tpu as pltpu
from jax.sharding import Mesh, PartitionSpec as P

BALANCE_SWEEPS = 20
EXPERTS = 32
CAP = 20
TOK = 64
GROUP = 256
SLOTS = GROUP // TOK * CAP
GATE_LANES = 128
RING = 4
PLANE_COLS = 1280


def balance_kernel(logits_ref, out_ref):
    cells = tuple(jnp.exp(logits_ref[i : i + 1, :]) for i in range(16))

    def sweep(step, cells):
        rows = [cells[4 * n] + cells[4 * n + 1] + cells[4 * n + 2] + cells[4 * n + 3] for n in range(4)]
        cells = [cells[i] / rows[i // 4] for i in range(16)]
        cols = [cells[m] + cells[4 + m] + cells[8 + m] + cells[12 + m] for m in range(4)]
        return tuple(cells[i] / cols[i % 4] for i in range(16))

    cells = lax.fori_loop(0, BALANCE_SWEEPS, sweep, cells)
    for i in range(16):
        out_ref[i : i + 1, :] = cells[i]


def balance_call(logits):
    return pl.pallas_call(
        balance_kernel,
        out_shape=jax.ShapeDtypeStruct(logits.shape, jnp.float32),
        in_specs=[pl.BlockSpec(memory_space=pltpu.VMEM)],
        out_specs=pl.BlockSpec(memory_space=pltpu.VMEM),
        cost_estimate=pl.CostEstimate(flops=100000, bytes_accessed=8192, transcendentals=1024),
        name="balance",
    )(logits)


def mix_coefficients(streams, phi_matrix, mix_scale, mix_bias):
    count = streams.shape[1]
    flat = streams.astype(jnp.float32).reshape(streams.shape[0], -1)
    normed = flat * lax.rsqrt(jnp.mean(flat * flat, axis=1, keepdims=True) + 1e-06)
    normed = normed.astype(jnp.bfloat16)
    coeffs = lax.dot_general(
        normed, phi_matrix, (((1,), (1,)), ((), ())), preferred_element_type=jnp.float32
    )
    pre = jax.nn.sigmoid(mix_scale[0] * coeffs[:, :count] + mix_bias[:count])
    post = 2.0 * jax.nn.sigmoid(
        mix_scale[1] * coeffs[:, count : 2 * count] + mix_bias[count : 2 * count]
    )
    logits = mix_scale[2] * coeffs[:, 2 * count :] + mix_bias[2 * count :]
    mixing = balance_call(logits.T).T.reshape(-1, count, count)
    return (pre, post, mixing)


def mix_input(streams, pre):
    total = pre[:, 0, None] * streams[:, 0, :].astype(jnp.float32)
    for stream in range(1, streams.shape[1]):
        total = total + pre[:, stream, None] * streams[:, stream, :].astype(jnp.float32)
    return total.astype(jnp.bfloat16)


def mix_output(streams, mixing, post, moe_out):
    rows = []
    for target in range(streams.shape[1]):
        total = mixing[:, target, 0, None] * streams[:, 0, :].astype(jnp.float32)
        for source in range(1, streams.shape[1]):
            total = total + mixing[:, target, source, None] * streams[:, source, :].astype(
                jnp.float32
            )
        rows.append(total + post[:, target, None] * moe_out)
    return jnp.stack(rows, axis=1).astype(jnp.bfloat16)


def dense_gates(layer_in, router, expert_index_table):
    logits = lax.dot_general(
        layer_in, router, (((1,), (1,)), ((), ())), preferred_element_type=jnp.float32
    )
    affinity = jax.nn.sigmoid(logits)
    experts = lax.iota(jnp.int32, EXPERTS)
    named = jnp.any(expert_index_table[:, :, None] == experts[None, None, :], axis=1)
    chosen = jnp.where(named, affinity, 0.0)
    gates = 2.5 * chosen / jnp.sum(chosen, axis=1, keepdims=True)
    high = lax.reduce_precision(gates, 8, 7)
    low = gates - high
    pad = jnp.zeros((gates.shape[0], GATE_LANES - 2 * EXPERTS), jnp.float32)
    return jnp.concatenate([high, low, pad], axis=1).astype(jnp.bfloat16)


def slot_tables(ids):
    slot = lax.broadcasted_iota(jnp.int32, (2 * SLOTS, GATE_LANES), 0)
    lane = lax.broadcasted_iota(jnp.int32, (2 * SLOTS, GATE_LANES), 1)
    expert = jnp.where(slot < SLOTS, ids[0], ids[1])
    return lane == expert, lane == expert + EXPERTS


def place_of(slot, token):
    inner = lax.rem(slot, SLOTS)
    return jnp.where(inner // CAP == token // TOK, lax.rem(inner, CAP) + 1, -1)


def pick_kernel(ids, x_ref, rows_ref, gate_ref, st_ref):
    width = rows_ref.shape[-1]
    tile = min(512, width)
    gates = x_ref[:, width : width + GATE_LANES]
    hit = (gates.astype(jnp.float32) != 0.0).astype(jnp.float32)
    row = lax.broadcasted_iota(jnp.int32, (GROUP, GROUP), 0)
    col = lax.broadcasted_iota(jnp.int32, (GROUP, GROUP), 1)
    upto = ((col <= row) & (col // TOK == row // TOK)).astype(jnp.float32).astype(jnp.bfloat16)
    count = jnp.dot(upto, hit.astype(jnp.bfloat16), preferred_element_type=jnp.float32)
    count = (count * hit).astype(jnp.bfloat16)
    high, low = slot_tables(ids)
    table = high.astype(jnp.float32).astype(jnp.bfloat16)
    across = (((1,), (1,)), ((), ()))
    by_slot = lax.dot_general(table, count, across, preferred_element_type=jnp.float32)
    slot = lax.broadcasted_iota(jnp.int32, (2 * SLOTS, GROUP), 0)
    token = lax.broadcasted_iota(jnp.int32, (2 * SLOTS, GROUP), 1)
    pick = by_slot == place_of(slot, token).astype(jnp.float32)
    pick = pick.astype(jnp.float32).astype(jnp.bfloat16)
    by_token = lax.dot_general(count, table, across, preferred_element_type=jnp.float32)
    token = lax.broadcasted_iota(jnp.int32, (GROUP, 2 * SLOTS), 0)
    slot = lax.broadcasted_iota(jnp.int32, (GROUP, 2 * SLOTS), 1)
    put = by_token == place_of(slot, token).astype(jnp.float32)
    st_ref[0] = put.astype(jnp.float32).astype(jnp.bfloat16)
    for n in range(width // tile):
        cols = slice(n * tile, (n + 1) * tile)
        rows = jnp.dot(pick, x_ref[:, cols], preferred_element_type=jnp.float32)
        rows = rows.astype(jnp.bfloat16)
        rows_ref[0, :, cols] = rows[:SLOTS]
        rows_ref[1, :, cols] = rows[SLOTS:]
    picked = jnp.dot(pick, gates, preferred_element_type=jnp.float32)
    own = jnp.sum(jnp.where(high | low, picked, 0.0), axis=1, keepdims=True)
    own = jnp.broadcast_to(own, (2 * SLOTS, GATE_LANES))
    gate_ref[0] = own[:SLOTS]
    gate_ref[1] = own[SLOTS:]


def pick_call(ids, gathered, width):
    groups = gathered.shape[0] // GROUP
    return pl.pallas_call(
        pick_kernel,
        out_shape=(
            jax.ShapeDtypeStruct((2, groups * SLOTS, width), jnp.bfloat16),
            jax.ShapeDtypeStruct((2, groups * SLOTS, GATE_LANES), jnp.float32),
            jax.ShapeDtypeStruct((groups, GROUP, 2 * SLOTS), jnp.bfloat16),
        ),
        grid_spec=pltpu.PrefetchScalarGridSpec(
            num_scalar_prefetch=1,
            grid=(groups,),
            in_specs=[pl.BlockSpec((GROUP, width + GATE_LANES), lambda g, ids: (g, 0))],
            out_specs=(
                pl.BlockSpec((2, SLOTS, width), lambda g, ids: (0, g, 0)),
                pl.BlockSpec((2, SLOTS, GATE_LANES), lambda g, ids: (0, g, 0)),
                pl.BlockSpec((1, GROUP, 2 * SLOTS), lambda g, ids: (g, 0, 0)),
            ),
        ),
        compiler_params=pltpu.CompilerParams(
            dimension_semantics=("arbitrary",), vmem_limit_bytes=24 << 20
        ),
        cost_estimate=pl.CostEstimate(
            flops=4 * groups * SLOTS * GROUP * width,
            bytes_accessed=4 * groups * GROUP * width,
            transcendentals=0,
        ),
        name="pick",
    )(ids, gathered)


def put_kernel(halves, plane, st_ref, y0_ref, y1_ref, *outs):
    columns = y0_ref.shape[-1]
    tile = columns // halves if halves > 1 else min(256, columns)
    for n in range(columns // tile):
        cols = slice(n * tile, (n + 1) * tile)
        y = jnp.concatenate([y0_ref[:, cols], y1_ref[:, cols]], axis=0)
        out = jnp.dot(st_ref[0], y, preferred_element_type=jnp.float32).astype(jnp.bfloat16)
        if halves > 1:
            outs[n][0] = out
        else:
            for b in range(RING):
                outs[0][b, 0, :, cols] = out[b * TOK : (b + 1) * TOK]


def put_call(plane, chosen, y0, y1, halves):
    groups = chosen.shape[0]
    columns = y0.shape[1]
    if halves > 1:
        half = columns // halves
        shape = jax.ShapeDtypeStruct((RING, RING * GROUP, half), jnp.bfloat16)
        out_shape = (shape, shape)
        out_specs = (
            pl.BlockSpec(
                (1, GROUP, half), lambda g, plane: ((plane[0] + 3 - g // RING) & 3, g % RING, 0)
            ),
            pl.BlockSpec(
                (1, GROUP, half), lambda g, plane: ((g // RING + 3 - plane[0]) & 3, g % RING, 0)
            ),
        )
    else:
        out_shape = jax.ShapeDtypeStruct((RING * RING, RING, TOK, columns), jnp.bfloat16)
        out_specs = pl.BlockSpec(
            (RING, 1, TOK, columns), lambda g, plane: (g % RING, g // RING, 0, 0)
        )
    return pl.pallas_call(
        functools.partial(put_kernel, halves),
        out_shape=out_shape,
        grid_spec=pltpu.PrefetchScalarGridSpec(
            num_scalar_prefetch=1,
            grid=(groups,),
            in_specs=[
                pl.BlockSpec((1, GROUP, 2 * SLOTS), lambda g, plane: (g, 0, 0)),
                pl.BlockSpec((SLOTS, columns), lambda g, plane: (g, 0)),
                pl.BlockSpec((SLOTS, columns), lambda g, plane: (g, 0)),
            ],
            out_specs=out_specs,
        ),
        compiler_params=pltpu.CompilerParams(
            dimension_semantics=("arbitrary",), vmem_limit_bytes=24 << 20
        ),
        cost_estimate=pl.CostEstimate(
            flops=4 * groups * GROUP * SLOTS * columns,
            bytes_accessed=3 * groups * GROUP * columns,
            transcendentals=0,
        ),
        name="put_halves" if halves > 1 else "put",
    )(plane, chosen, y0, y1)


def run_hidden(rows, gate, w_gate, w_up):
    gate_part = jnp.dot(rows, w_gate, preferred_element_type=jnp.float32)
    up_part = jnp.dot(rows, w_up, preferred_element_type=jnp.float32)
    return (jax.nn.silu(gate_part) * up_part * gate[:, :1]).astype(jnp.bfloat16)


def run_down(hidden, down_weight):
    return jnp.dot(hidden, down_weight, preferred_element_type=jnp.float32).astype(jnp.bfloat16)


def add_rounded(a, b):
    return (a.astype(jnp.float32) + b.astype(jnp.float32)).astype(jnp.bfloat16)


def body(
    streams, phi_matrix, mix_scale, mix_bias, router, expert_index_table, w_gate, w_up, down_weight
):
    width, ff = w_gate.shape[1], w_gate.shape[2]
    swap = [(0, 1), (1, 0)]
    own = (w_gate[0], w_up[0], down_weight[0])
    other = tuple(lax.ppermute(w, "c", swap) for w in own)
    pre, post, mixing = mix_coefficients(streams, phi_matrix, mix_scale, mix_bias)
    layer_in = mix_input(streams, pre)
    gates = dense_gates(layer_in, router, expert_index_table)
    packed = jnp.concatenate([layer_in, gates], axis=1)
    gathered = lax.all_gather(packed, ("z", "y", "x"), axis=0, tiled=True)
    core = lax.axis_index("c")
    pair = 2 * (lax.axis_index("y") * RING + lax.axis_index("x"))
    ids = jnp.stack([pair + core, pair + 1 - core]).astype(jnp.int32)
    plane = lax.axis_index("z")
    planes = plane.reshape(1).astype(jnp.int32)
    rows, gate, chosen = pick_call(ids, gathered, width)
    hidden = [run_hidden(rows[e], gate[e], *w[:2]) for e, w in enumerate((own, other))]
    hidden = lax.optimization_barrier(hidden)
    downs = (own[2], other[2])
    late = width - PLANE_COLS
    late_parts = [run_down(h, w[:, :late]) for h, w in zip(hidden, downs)]
    dense = put_call(planes, chosen, *late_parts, 1)
    summed = lax.psum_scatter(
        dense.reshape(-1, late), ("y", "x"), scatter_dimension=0, tiled=True
    ).reshape(RING, TOK, late)
    early_parts = [run_down(h, w[:, late:]) for h, w in zip(hidden, downs)]
    halves = put_call(planes, chosen, *early_parts, 2)
    travel = [half[0] for half in halves]
    for stop in range(1, RING):
        for way, turn in ((0, 1), (1, RING - 1)):
            ring = [(i, (i + turn) % RING) for i in range(RING)]
            travel[way] = add_rounded(lax.ppermute(travel[way], "z", ring), halves[way][stop])
    shares = jnp.concatenate(travel, axis=1).reshape(RING * RING, TOK, PLANE_COLS)
    shares = lax.all_to_all(shares, ("y", "x"), split_axis=0, concat_axis=0, tiled=True)
    early_out = jnp.sum(shares.astype(jnp.float32), axis=0)
    late_out = lax.dynamic_index_in_dim(summed, plane, 0, keepdims=False).astype(jnp.float32)
    for shift in range(1, RING):
        away = lax.dynamic_index_in_dim(summed, (plane + shift) % RING, 0, keepdims=False)
        ring = [(i, (i + shift) % RING) for i in range(RING)]
        late_out = late_out + lax.ppermute(away, "z", ring).astype(jnp.float32)
    moe_out = jnp.concatenate([late_out, early_out], axis=1)
    return mix_output(streams, mixing, post, moe_out)


def solution(mesh):
    torus = Mesh(mesh.devices.reshape(RING, RING, RING, 2), ("z", "y", "x", "c"))
    tokens, experts = ("z", "y", "x", "c"), ("y", "x", "c")
    in_specs = (
        P(tokens, None, None),
        P(),
        P(),
        P(),
        P(),
        P(tokens, None),
        P(experts, None, "z"),
        P(experts, None, "z"),
        P(experts, "z", None),
    )
    out_specs = P(tokens, None, None)
    return jax.shard_map(
        body, mesh=torus, in_specs=in_specs, out_specs=out_specs, check_vma=False
    )
```

time: 508 us -> 428 us (0.84)
  waiting for transfers between devices: 341 us -> 262 us
  Pallas kernels: 120 us -> 42.1 us
  matrix products: 1.03 us -> 49.4 us
  starting transfers between devices: 5.58 us -> 30 us
  other arithmetic: 10.8 us -> 16.6 us
    reduce_scatter x1, waiting for transfers between devices: 173 us -> 15.2 us  [body(): lax.psum_scatter(dense.reshape(-1, late), ('y', 'x'), scatter_dimension=0...]
    pallas_call x1 -> x4, Pallas kernels: 120 us -> 42.1 us  [the longest x1 21.6 us: pick_call(): pl.pallas_call(pick_kernel, out_shape=(jax.ShapeDtypeStruct((2, groups *...]
    ppermute x3 -> x9, waiting for transfers between devices: 19.2 us -> 96.9 us  [the longest x6 85 us: body(): lax.ppermute(travel[way], 'z', ring)]
    dot_general x0 -> x8, matrix products: none -> 48.4 us  [the longest x2 17.5 us: run_hidden(): gate_part = jnp.dot(rows, w_gate, preferred_element_type=jnp.float32)]
    ppermute x3 -> x9, starting transfers between devices: 4.86 us -> 21.9 us  [the longest x3 15.6 us: body(): late_out = late_out + lax.ppermute(away, 'z', ring).astype(jnp.float32)]
    all_gather x1, waiting for transfers between devices: 133 us -> 149 us  [body(): gathered = lax.all_gather(packed, ('z', 'y', 'x'), axis=0, tiled=True)]
    ppermute x3, waiting for transfers between devices: 16 us -> 0.01 us  [body(): other = tuple((lax.ppermute(w, 'c', swap) for w in own))]
    all_to_all x0 -> x1, starting transfers between devices: none -> 7.29 us  [body(): lax.all_to_all(shares, ('y', 'x'), split_axis=0, concat_axis=0, tiled=True)]
  transfers between devices with their start and end apart: 8 -> 15, of which waited for: 8 -> 11; matrix products, arithmetic and copies ran while one was open for 0% -> 12% of each run, Pallas kernels for 0% -> 7%
where the time goes in v3:
time: 428 us; the launch traced here: 425 us
  waiting for transfers between devices  262 us (61%)
  matrix products  49.4 us (12%)
  Pallas kernels  42.1 us (10%)
  starting transfers between devices  30 us (7%)
  other arithmetic  16.6 us (4%)
  between operations  13.8 us (3%)
  local copies, waits for them, and re-layouts  11.3 us (3%)
    all_gather x1, waiting for transfers between devices, body(): gathered = lax.all_gather(packed, ('z', 'y', 'x'), axis=0, tiled=True)  149 us
    ppermute x6, waiting for transfers between devices, body(): lax.ppermute(travel[way], 'z', ring)  85 us
    pallas_call x1, Pallas kernels, pick_call(): pl.pallas_call(pick_kernel, out_shape=(jax.ShapeDtypeStruct((2, groups *...  21.6 us
    pallas_call x2, Pallas kernels, put_call(): pl.pallas_call(functools.partial(put_kernel, halves), out_shape=out_shape...  18.7 us
    dot_general x2, matrix products, run_hidden(): gate_part = jnp.dot(rows, w_gate, preferred_element_type=jnp.float32)  17.5 us
    ppermute x3, starting transfers between devices, body(): late_out = late_out + lax.ppermute(away, 'z', ring).astype(jnp.float32)  15.6 us
    dot_general x2, matrix products, run_hidden(): up_part = jnp.dot(rows, w_up, preferred_element_type=jnp.float32)  15.5 us
    dot_general x4, matrix products, run_down(): jnp.dot(hidden, down_weight, preferred_element_type=jnp.float32)  15.4 us
  transfers between devices with their start and end apart: 15, of which 11 were waited for; matrix products, arithmetic and copies ran while one was open for 12% of the time, Pallas kernels for 7%

profile of v3, /device:TPU:44, one launch (start us, length us, event | category | flops | bytes accessed | tf_op | source)
XLA Modules:
  0.0 425.3 jit_solution(8121746651372480488)
XLA Ops:
  6.5 3.1 multiply_reduce_fusion
  9.6 2.7 fusion.85
  12.3 0.5 copy.36
  12.8 0.1 copy-done.9
  13.1 0.6 fusion.86
  13.6 0.7 fusion.29
  14.3 1.3 fusion.82
  15.7 0.1 copy.29
  15.8 1.8 fusion.61
  17.6 0.4 fusion.88
  18.0 0.1 fusion.69
  18.1 0.9 concatenate.44
  19.0 0.1 collective-permute-start
  19.1 0.5 collective-permute-start.1
  19.6 0.1 collective-permute-start.2
  19.8 149.5 %all-gather.2.cloned.1.call-done.x_ref = bf16[4096,3712]{1,0:T(8,128)(2,1)} async-done(((bf16[64,3712]{1,0:T(8,128)(2,1)}), bf16[4096,3712]{1,0:T(8,128)(2,1)}) %all-gather.2.cloned.1.call-update) | async-done | bytes 30408720 | tf_op jit(solution)/shard_map/all_gather | solution.py:260
  169.2 21.6 %pick.1 = (bf16[2,1280,3584]{2,1,0:T(8,128)(2,1)S(1)}, f32[2,1280,128]{2,1,0:T(8,128)S(1)}, bf16[16,256,160]{2,1,0:T(8,128)(2,1)S(1)}) custom-call(s32[2]{0:T(128)S(1)} %pad_add_fusion.ids, bf16[4096,3712]{1,0:T(8,128)(2,1)} %all-gather.2.cloned.1.call-done.x_ref), custom_call_target="tpu_custom_call" | custom-call | flops 4697620480 | bytes 58720256 | tf_op jit(solution)/shard_map/pick/pallas_call | solution.py:147
  191.0 0.4 slice_reduce_fusion
  191.4 8.6 %fusion.6 = f32[1280,512]{1,0:T(8,128)} fusion(bf16[2,1280,3584]{2,1,0:T(8,128)(2,1)S(1)} %get-tuple-element.13, bf16[1,3584,512]{2,1,0:T(8,128)(2,1)} %param.15), kind=kOutput, calls=%fused_computation.8 | convolution fusion | flops 4697620480 | bytes 15466496 | tf_op jit(solution)/shard_map/dot_general | solution.py:236
  200.0 6.7 %fusion.18 = bf16[1280,512]{1,0:T(8,128)(2,1)S(1)} fusion(bf16[2,1280,3584]{2,1,0:T(8,128)(2,1)S(1)} %get-tuple-element.13, f32[1280,512]{1,0:T(8,128)} %fusion.6, f32[1280]{0:T(1024)S(1)} %get-tuple-element.73, bf16[1,3584,512]{2,1,0:T(8,128)(2,1)S(1)} %copy-done.10), kind=kOutput, calls=%fused_computation.21 | convolution fusion | flops 4702208000 | bytes 16785408 | tf_op jit(solution)/shard_map/dot_general | solution.py:237
  206.7 8.9 %fusion.2 = f32[1280,512]{1,0:T(8,128)} fusion(bf16[3584,512]{1,0:T(8,128)(2,1)} %collective-permute-done, bf16[2,1280,3584]{2,1,0:T(8,128)(2,1)S(1)} %get-tuple-element.13), kind=kOutput, calls=%fused_computation.4 | convolution fusion | flops 4697620480 | bytes 15466496 | tf_op jit(solution)/shard_map/dot_general | solution.py:236
  215.7 8.8 %multiply_convert_fusion.1 = bf16[1280,512]{1,0:T(8,128)(2,1)} fusion(f32[1280,512]{1,0:T(8,128)} %fusion.2, f32[1280]{0:T(1024)S(1)} %get-tuple-element.72, bf16[3584,512]{1,0:T(8,128)(2,1)} %collective-permute-done.1, bf16[2,1280,3584]{2,1,0:T(8,128)(2,1)S(1)} %get-tuple-element.13), kind=kOutput, calls=%fused_computation.35 | convolution fusion | flops 4702208000 | bytes 16785408 | tf_op jit(solution)/shard_map/dot_general | solution.py:237
  224.5 3.4 convolution_convert_fusion.1.y0_ref
  227.9 5.1 %convolution_convert_fusion.y1_ref = bf16[1280,2304]{1,0:T(8,128)(2,1)S(1)} fusion(bf16[1280,512]{1,0:T(8,128)(2,1)S(1)} %copy-done.14, bf16[512,3584]{1,0:T(8,128)(2,1)} %collective-permute-done.2), kind=kOutput, calls=%fused_computation | convolution fusion | flops 3022848000 | bytes 9568256 | tf_op jit(solution)/shard_map/dot_general | solution.py:242
  233.0 12.8 %put.1 = bf16[16,4,64,2304]{3,2,1,0:T(8,128)(2,1)} custom-call(s32[1]{0:T(128)} %bitcast.11.plane, bf16[16,256,160]{2,1,0:T(8,128)(2,1)S(1)} %get-tuple-element.12.st_ref, bf16[1280,2304]{1,0:T(8,128)(2,1)S(1)} %convolution_convert_fusion.1.y0_ref, bf16[1280,2304]{1,0:T(8,128)(2,1)S(1)} %convolution_convert_fusion.y1_ref), custom_call_target="tpu_custom_call" | custom-call | flops 3019898880 | bytes 28311552 | tf_op jit(solution)/shard_map/put/pallas_call | solution.py:210
  245.9 3.7 convolution_convert_fusion.3.y0_ref
  249.6 3.2 convolution_convert_fusion.2.y1_ref
  252.8 5.9 %put_halves.1 = (bf16[4,1024,640]{2,1,0:T(8,128)(2,1)S(1)}, bf16[4,1024,640]{2,1,0:T(8,128)(2,1)S(1)}) custom-call(s32[1]{0:T(128)} %bitcast.11.plane, bf16[16,256,160]{2,1,0:T(8,128)(2,1)S(1)} %get-tuple-element.12.st_ref, bf16[1280,1280]{1,0:T(8,128)(2,1)S(1)} %convolution_convert_fusion.3.y0_ref, bf16[1280,1280]{1,0:T(8,128)(2,1)S(1)} %convolution_convert_fusion.2.y1_ref), custom_call_target="tpu_custom_call" | custom-call | flops 1677721600 | bytes 15728640 | tf_op jit(solution)/shard_map/put_halves/pallas_call | solution.py:210
  258.7 0.1 slice_bitcast_fusion
  258.8 1.9 collective-permute-start.9
  260.7 0.1 slice_bitcast_fusion.1
  260.8 0.2 collective-permute-start.6
  261.1 28.1 %collective-permute-done.9 = bf16[1024,640]{1,0:T(8,128)(2,1)S(1)} collective-permute-done((bf16[1024,640]{1,0:T(8,128)(2,1)S(1)}, bf16[1024,640]{1,0:T(8,128)(2,1)S(1)}, u32[]{:S(2)}, u32[]{:S(2)}) %collective-permute-start.9) | collective-permute-done | bytes 1310752 | tf_op jit(solution)/shard_map/ppermute | solution.py:282
  289.2 0.3 fusion.23
  289.5 1.9 collective-permute-start.10
  291.5 0.3 fusion.26
  291.8 0.2 collective-permute-start.7
  292.0 27.2 %collective-permute-done.10 = bf16[1024,640]{1,0:T(8,128)(2,1)S(1)} collective-permute-done((bf16[1024,640]{1,0:T(8,128)(2,1)S(1)}, bf16[1024,640]{1,0:T(8,128)(2,1)S(1)}, u32[]{:S(2)}, u32[]{:S(2)}) %collective-permute-start.10) | collective-permute-done | bytes 1310752 | tf_op jit(solution)/shard_map/ppermute | solution.py:282
  319.2 0.3 fusion.22
  319.5 1.9 collective-permute-start.11
  321.5 0.3 collective-permute-done.7
  321.7 0.3 fusion.25
  322.2 26.5 %collective-permute-done.11 = bf16[1024,640]{1,0:T(8,128)(2,1)S(1)} collective-permute-done((bf16[1024,640]{1,0:T(8,128)(2,1)S(1)}, bf16[1024,640]{1,0:T(8,128)(2,1)S(1)}, u32[]{:S(2)}, u32[]{:S(2)}) %collective-permute-start.11) | collective-permute-done | bytes 1310752 | tf_op jit(solution)/shard_map/ppermute | solution.py:282
  348.7 0.3 fusion.21
  349.0 3.0 collective-permute-done.8
  352.0 0.3 fusion.24
  352.3 1.7 pad_maximum_fusion
  354.0 7.3 %all-to-all-start = ((bf16[16,64,1280]{2,1,0:T(8,128)(2,1)}), bf16[16,64,1280]{2,1,0:T(8,128)(2,1)S(1)}, u32[]{:S(2)}, u32[]{:S(2)}) async-start(bf16[16,64,1280]{2,1,0:T(8,128)(2,1)} %bitcast.170), calls=%async_computation.1 | async-start | bytes 5242880 | tf_op jit(solution)/shard_map/all_to_all | solution.py:284
  361.4 1.2 fusion.71.logits_ref
  362.6 1.8 balance.1
  364.4 0.8 slice_bitcast_fusion.19
  365.2 15.2 %reduce-scatter.2.cloned.1.call-done = bf16[256,2304]{1,0:T(8,128)(2,1)} async-done(((bf16[4096,2304]{1,0:T(8,128)(2,1)}), bf16[256,2304]{1,0:T(8,128)(2,1)}) %reduce-scatter.2.cloned.1.call-update) | async-done | bytes 1179664 | tf_op jit(solution)/shard_map/reduce_scatter | solution.py:273
  380.5 2.1 dynamic-slice_bitcast_fusion.2
  382.5 15.6 %collective-permute-start.4 = (bf16[64,2304]{1,0:T(8,128)(2,1)}, bf16[64,2304]{1,0:T(8,128)(2,1)}, u32[]{:S(2)}, u32[]{:S(2)}) collective-permute-start(bf16[64,2304]{1,0:T(8,128)(2,1)} %get-tuple-element.36), channel_id=1, source_target_pairs={{0,64},{32,96},{64,0},{96,32},{1,65},{33,97},{65,1},{97,33},{2,66}... | collective-permute-start | bytes 884744 | tf_op jit(solution)/shard_map/ppermute | solution.py:290
  398.1 0.5 all-to-all-done
  398.6 0.4 convert_reduce_fusion
  399.0 4.9 %collective-permute-done.5 = bf16[64,2304]{1,0:T(8,128)(2,1)} collective-permute-done((bf16[64,2304]{1,0:T(8,128)(2,1)}, bf16[64,2304]{1,0:T(8,128)(2,1)}, u32[]{:S(2)}, u32[]{:S(2)}) %collective-permute-start.5) | collective-permute-done | bytes 294944 | tf_op jit(solution)/shard_map/ppermute | solution.py:290
  403.9 6.3 %collective-permute-done.4 = bf16[64,2304]{1,0:T(8,128)(2,1)} collective-permute-done((bf16[64,2304]{1,0:T(8,128)(2,1)}, bf16[64,2304]{1,0:T(8,128)(2,1)}, u32[]{:S(2)}, u32[]{:S(2)}) %collective-permute-start.4) | collective-permute-done | bytes 294944 | tf_op jit(solution)/shard_map/ppermute | solution.py:290
  410.2 0.7 collective-permute-done.3
  410.9 1.4 fusion.67
  412.2 2.3 fusion.46
  414.6 0.9 fusion.41
  415.6 0.2 pad_maximum_fusion.1
  415.8 2.6 copy.30
  (51 shorter events, 0.6 us)
Async XLA Ops:
  6.5 7.1 %copy-start = (bf16[24,14336]{1,0:T(8,128)(2,1)S(1)}, bf16[24,14336]{1,0:T(8,128)(2,1)}, u32[]{:S(2)}) copy-start(bf16[24,14336]{1,0:T(8,128)(2,1)} %param.10) | copy-start | bytes 2064388
  6.5 3.1 copy-start.2
  6.5 162.7 %all-gather.2.cloned.1.call-start = ((), (), s32[]{:S(2)}) async-start(), calls=%async_computation.2 | async-start | bytes 30883840 | tf_op jit(solution)/shard_map/all_gather | solution.py:260
  12.3 0.7 copy-start.9
  12.3 0.7 copy-start.7
  12.8 2.8 copy-start.8
  15.8 1.8 copy-start.12
  19.0 361.5 %reduce-scatter.2.cloned.1.call-start = ((), (), s32[]{:S(2)}) async-start(), calls=%async_computation.3 | async-start | bytes 20054016 | tf_op jit(solution)/shard_map/reduce_scatter | solution.py:273
  19.0 187.7 %collective-permute-start = (bf16[3584,512]{1,0:T(8,128)(2,1)}, bf16[3584,512]{1,0:T(8,128)(2,1)}, u32[]{:S(2)}, u32[]{:S(2)}) collective-permute-start(bf16[3584,512]{1,0:T(8,128)(2,1)} %bitcast.176), channel_id=1, source_target_pairs={{0,1},{1,0},{2,3},{3,2},{4,5},{5,4},{6,7},{7,6},{8,9},{9,8},{10,11... | collective-permute-start | bytes 11010056 | tf_op jit(solution)/shard_map/ppermute | solution.py:255
  19.1 196.6 %collective-permute-start.1 = (bf16[3584,512]{1,0:T(8,128)(2,1)}, bf16[3584,512]{1,0:T(8,128)(2,1)}, u32[]{:S(2)}, u32[]{:S(2)}) collective-permute-start(bf16[3584,512]{1,0:T(8,128)(2,1)} %bitcast.177), channel_id=1, source_target_pairs={{0,1},{1,0},{2,3},{3,2},{4,5},{5,4},{6,7},{7,6},{8,9},{9,8},{10,11... | collective-permute-start | bytes 11010056 | tf_op jit(solution)/shard_map/ppermute | solution.py:255
  19.6 208.3 %collective-permute-start.2 = (bf16[512,3584]{1,0:T(8,128)(2,1)}, bf16[512,3584]{1,0:T(8,128)(2,1)}, u32[]{:S(2)}, u32[]{:S(2)}) collective-permute-start(bf16[512,3584]{1,0:T(8,128)(2,1)} %bitcast.178), channel_id=1, source_target_pairs={{0,1},{1,0},{2,3},{3,2},{4,5},{5,4},{6,7},{7,6},{8,9},{9,8},{10,11... | collective-permute-start | bytes 11010056 | tf_op jit(solution)/shard_map/ppermute | solution.py:255
  191.4 8.6 %copy-start.10 = (bf16[1,3584,512]{2,1,0:T(8,128)(2,1)S(1)}, bf16[1,3584,512]{2,1,0:T(8,128)(2,1)}, u32[]{:S(2)}) copy-start(bf16[1,3584,512]{2,1,0:T(8,128)(2,1)} %param.16) | copy-start | bytes 11010052
  206.7 17.8 %copy-start.13 = (bf16[1280,512]{1,0:T(8,128)(2,1)}, bf16[1280,512]{1,0:T(8,128)(2,1)S(1)}, u32[]{:S(2)}) copy-start(bf16[1280,512]{1,0:T(8,128)(2,1)S(1)} %fusion.18) | copy-start | bytes 3932164
  215.7 8.8 %copy-start.11 = (bf16[1,512,3584]{2,1,0:T(8,128)(2,1)S(1)}, bf16[1,512,3584]{2,1,0:T(8,128)(2,1)}, u32[]{:S(2)}) copy-start(bf16[1,512,3584]{2,1,0:T(8,128)(2,1)} %param.17) | copy-start | bytes 11010052
  224.5 3.5 copy-start.14
  245.9 3.7 copy-start.15
  258.8 30.4 %collective-permute-start.9 = (bf16[1024,640]{1,0:T(8,128)(2,1)S(1)}, bf16[1024,640]{1,0:T(8,128)(2,1)S(1)}, u32[]{:S(2)}, u32[]{:S(2)}) collective-permute-start(bf16[1024,640]{1,0:T(8,128)(2,1)S(1)} %slice_bitcast_fusion), channel_id=1, source_target_pairs={{0,96},{32,0},{64,32},{96,64},{1,97},{33,1},{65,33},{97,65},{2,98}... | collective-permute-start | bytes 3932168 | tf_op jit(solution)/shard_map/ppermute | solution.py:282
  260.8 30.6 %collective-permute-start.6 = (bf16[1024,640]{1,0:T(8,128)(2,1)S(1)}, bf16[1024,640]{1,0:T(8,128)(2,1)S(1)}, u32[]{:S(2)}, u32[]{:S(2)}) collective-permute-start(bf16[1024,640]{1,0:T(8,128)(2,1)S(1)} %slice_bitcast_fusion.1), channel_id=1, source_target_pairs={{0,32},{32,64},{64,96},{96,0},{1,33},{33,65},{65,97},{97,1},{2,34}... | collective-permute-start | bytes 3932168 | tf_op jit(solution)/shard_map/ppermute | solution.py:282
  289.5 29.7 %collective-permute-start.10 = (bf16[1024,640]{1,0:T(8,128)(2,1)S(1)}, bf16[1024,640]{1,0:T(8,128)(2,1)S(1)}, u32[]{:S(2)}, u32[]{:S(2)}) collective-permute-start(bf16[1024,640]{1,0:T(8,128)(2,1)S(1)} %fusion.23), channel_id=1, source_target_pairs={{0,96},{32,0},{64,32},{96,64},{1,97},{33,1},{65,33},{97,65},{2,98}... | collective-permute-start | bytes 3932168 | tf_op jit(solution)/shard_map/ppermute | solution.py:282
  291.8 29.9 %collective-permute-start.7 = (bf16[1024,640]{1,0:T(8,128)(2,1)S(1)}, bf16[1024,640]{1,0:T(8,128)(2,1)S(1)}, u32[]{:S(2)}, u32[]{:S(2)}) collective-permute-start(bf16[1024,640]{1,0:T(8,128)(2,1)S(1)} %fusion.26), channel_id=1, source_target_pairs={{0,32},{32,64},{64,96},{96,0},{1,33},{33,65},{65,97},{97,1},{2,34}... | collective-permute-start | bytes 3932168 | tf_op jit(solution)/shard_map/ppermute | solution.py:282
  319.5 29.1 %collective-permute-start.11 = (bf16[1024,640]{1,0:T(8,128)(2,1)S(1)}, bf16[1024,640]{1,0:T(8,128)(2,1)S(1)}, u32[]{:S(2)}, u32[]{:S(2)}) collective-permute-start(bf16[1024,640]{1,0:T(8,128)(2,1)S(1)} %fusion.22), channel_id=1, source_target_pairs={{0,96},{32,0},{64,32},{96,64},{1,97},{33,1},{65,33},{97,65},{2,98}... | collective-permute-start | bytes 3932168 | tf_op jit(solution)/shard_map/ppermute | solution.py:282
  322.1 29.9 %collective-permute-start.8 = (bf16[1024,640]{1,0:T(8,128)(2,1)S(1)}, bf16[1024,640]{1,0:T(8,128)(2,1)S(1)}, u32[]{:S(2)}, u32[]{:S(2)}) collective-permute-start(bf16[1024,640]{1,0:T(8,128)(2,1)S(1)} %fusion.25), channel_id=1, source_target_pairs={{0,32},{32,64},{64,96},{96,0},{1,33},{33,65},{65,97},{97,1},{2,34}... | collective-permute-start | bytes 3932168 | tf_op jit(solution)/shard_map/ppermute | solution.py:282
  354.0 44.6 %all-to-all-start = ((bf16[16,64,1280]{2,1,0:T(8,128)(2,1)}), bf16[16,64,1280]{2,1,0:T(8,128)(2,1)S(1)}, u32[]{:S(2)}, u32[]{:S(2)}) async-start(bf16[16,64,1280]{2,1,0:T(8,128)(2,1)} %bitcast.170), calls=%async_computation.1 | async-start | bytes 5242880 | tf_op jit(solution)/shard_map/all_to_all | solution.py:284
  382.5 21.4 %collective-permute-start.5 = (bf16[64,2304]{1,0:T(8,128)(2,1)}, bf16[64,2304]{1,0:T(8,128)(2,1)}, u32[]{:S(2)}, u32[]{:S(2)}) collective-permute-start(bf16[64,2304]{1,0:T(8,128)(2,1)} %get-tuple-element.35), channel_id=1, source_target_pairs={{0,96},{32,0},{64,32},{96,64},{1,97},{33,1},{65,33},{97,65},{2,98}... | collective-permute-start | bytes 884744 | tf_op jit(solution)/shard_map/ppermute | solution.py:290
  382.5 27.7 %collective-permute-start.4 = (bf16[64,2304]{1,0:T(8,128)(2,1)}, bf16[64,2304]{1,0:T(8,128)(2,1)}, u32[]{:S(2)}, u32[]{:S(2)}) collective-permute-start(bf16[64,2304]{1,0:T(8,128)(2,1)} %get-tuple-element.36), channel_id=1, source_target_pairs={{0,64},{32,96},{64,0},{96,32},{1,65},{33,97},{65,1},{97,33},{2,66}... | collective-permute-start | bytes 884744 | tf_op jit(solution)/shard_map/ppermute | solution.py:290
  398.1 12.7 %collective-permute-start.3 = (bf16[64,2304]{1,0:T(8,128)(2,1)}, bf16[64,2304]{1,0:T(8,128)(2,1)}, u32[]{:S(2)}, u32[]{:S(2)}) collective-permute-start(bf16[64,2304]{1,0:T(8,128)(2,1)} %get-tuple-element.34), channel_id=1, source_target_pairs={{0,32},{32,64},{64,96},{96,0},{1,33},{33,65},{65,97},{97,1},{2,34}... | collective-permute-start | bytes 884744 | tf_op jit(solution)/shard_map/ppermute | solution.py:290
  399.0 15.6 %copy-start.3 = (bf16[64,1,3584]{2,0,1:T(8,128)(2,1)S(1)}, bf16[64,1,3584]{2,0,1:T(8,128)(2,1)}, u32[]{:S(2)}) copy-start(bf16[64,1,3584]{2,0,1:T(8,128)(2,1)} %get-tuple-element.20) | copy-start | bytes 1376260
  399.0 15.6 %copy-start.4 = (bf16[64,1,3584]{2,0,1:T(8,128)(2,1)S(1)}, bf16[64,1,3584]{2,0,1:T(8,128)(2,1)}, u32[]{:S(2)}) copy-start(bf16[64,1,3584]{2,0,1:T(8,128)(2,1)} %get-tuple-element.21) | copy-start | bytes 1376260
  399.0 15.6 %copy-start.5 = (bf16[64,1,3584]{2,0,1:T(8,128)(2,1)S(1)}, bf16[64,1,3584]{2,0,1:T(8,128)(2,1)}, u32[]{:S(2)}) copy-start(bf16[64,1,3584]{2,0,1:T(8,128)(2,1)} %get-tuple-element.22) | copy-start | bytes 1376260
  399.0 15.6 %copy-start.6 = (bf16[64,1,3584]{2,0,1:T(8,128)(2,1)S(1)}, bf16[64,1,3584]{2,0,1:T(8,128)(2,1)}, u32[]{:S(2)}) copy-start(bf16[64,1,3584]{2,0,1:T(8,128)(2,1)} %get-tuple-element.23) | copy-start | bytes 1376260
  415.6 2.9 copy-start.1
Sparse Core Ops, SparseCore 0:
  19.1 150.1 all-gather.1
  246.0 134.4 reduce-scatter.1

commit v4 on v3

--- a/solution.py
+++ b/solution.py
@@ -106,44 +106,55 @@
     return jnp.where(inner // CAP == token // TOK, lax.rem(inner, CAP) + 1, -1)
 
 
-def pick_kernel(ids, x_ref, rows_ref, gate_ref, st_ref):
+def pick_kernel(ids, x_ref, rows_ref, gate_ref, st_ref, upto_ref, want_ref, wanted_ref):
     width = rows_ref.shape[-1]
     tile = min(512, width)
-    gates = x_ref[:, width : width + GATE_LANES]
-    hit = (gates.astype(jnp.float32) != 0.0).astype(jnp.float32)
-    row = lax.broadcasted_iota(jnp.int32, (GROUP, GROUP), 0)
-    col = lax.broadcasted_iota(jnp.int32, (GROUP, GROUP), 1)
-    upto = ((col <= row) & (col // TOK == row // TOK)).astype(jnp.float32).astype(jnp.bfloat16)
-    count = jnp.dot(upto, hit.astype(jnp.bfloat16), preferred_element_type=jnp.float32)
-    count = (count * hit).astype(jnp.bfloat16)
+    across = (((1,), (1,)), ((), ()))
+
+    @pl.when(pl.program_id(0) == 0)
+    def _():
+        row = lax.broadcasted_iota(jnp.int32, (GROUP, GROUP), 0)
+        col = lax.broadcasted_iota(jnp.int32, (GROUP, GROUP), 1)
+        upto = (col <= row) & (col // TOK == row // TOK)
+        upto_ref[...] = upto.astype(jnp.float32).astype(jnp.bfloat16)
+        slot = lax.broadcasted_iota(jnp.int32, (2 * SLOTS, GROUP), 0)
+        token = lax.broadcasted_iota(jnp.int32, (2 * SLOTS, GROUP), 1)
+        want_ref[...] = place_of(slot, token).astype(jnp.float32)
+        token = lax.broadcasted_iota(jnp.int32, (GROUP, 2 * SLOTS), 0)
+        slot = lax.broadcasted_iota(jnp.int32, (GROUP, 2 * SLOTS), 1)
+        wanted_ref[...] = place_of(slot, token).astype(jnp.float32)
+
     high, low = slot_tables(ids)
     table = high.astype(jnp.float32).astype(jnp.bfloat16)
-    across = (((1,), (1,)), ((), ()))
-    by_slot = lax.dot_general(table, count, across, preferred_element_type=jnp.float32)
-    slot = lax.broadcasted_iota(jnp.int32, (2 * SLOTS, GROUP), 0)
-    token = lax.broadcasted_iota(jnp.int32, (2 * SLOTS, GROUP), 1)
-    pick = by_slot == place_of(slot, token).astype(jnp.float32)
-    pick = pick.astype(jnp.float32).astype(jnp.bfloat16)
-    by_token = lax.dot_general(count, table, across, preferred_element_type=jnp.float32)
-    token = lax.broadcasted_iota(jnp.int32, (GROUP, 2 * SLOTS), 0)
-    slot = lax.broadcasted_iota(jnp.int32, (GROUP, 2 * SLOTS), 1)
-    put = by_token == place_of(slot, token).astype(jnp.float32)
-    st_ref[0] = put.astype(jnp.float32).astype(jnp.bfloat16)
-    for n in range(width // tile):
-        cols = slice(n * tile, (n + 1) * tile)
-        rows = jnp.dot(pick, x_ref[:, cols], preferred_element_type=jnp.float32)
-        rows = rows.astype(jnp.bfloat16)
-        rows_ref[0, :, cols] = rows[:SLOTS]
-        rows_ref[1, :, cols] = rows[SLOTS:]
-    picked = jnp.dot(pick, gates, preferred_element_type=jnp.float32)
-    own = jnp.sum(jnp.where(high | low, picked, 0.0), axis=1, keepdims=True)
-    own = jnp.broadcast_to(own, (2 * SLOTS, GATE_LANES))
-    gate_ref[0] = own[:SLOTS]
-    gate_ref[1] = own[SLOTS:]
+    for g in range(x_ref.shape[0] // GROUP):
+        tokens = slice(g * GROUP, (g + 1) * GROUP)
+        mine = slice(g * SLOTS, (g + 1) * SLOTS)
+        gates = x_ref[tokens, width : width + GATE_LANES]
+        hit = (gates.astype(jnp.float32) != 0.0).astype(jnp.float32)
+        count = jnp.dot(
+            upto_ref[...], hit.astype(jnp.bfloat16), preferred_element_type=jnp.float32
+        )
+        count = (count * hit).astype(jnp.bfloat16)
+        by_slot = lax.dot_general(table, count, across, preferred_element_type=jnp.float32)
+        pick = (by_slot == want_ref[...]).astype(jnp.float32).astype(jnp.bfloat16)
+        by_token = lax.dot_general(count, table, across, preferred_element_type=jnp.float32)
+        put = (by_token == wanted_ref[...]).astype(jnp.float32)
+        st_ref[g] = put.astype(jnp.bfloat16)
+        for n in range(width // tile):
+            cols = slice(n * tile, (n + 1) * tile)
+            rows = jnp.dot(pick, x_ref[tokens, cols], preferred_element_type=jnp.float32)
+            rows = rows.astype(jnp.bfloat16)
+            rows_ref[0, mine, cols] = rows[:SLOTS]
+            rows_ref[1, mine, cols] = rows[SLOTS:]
+        picked = jnp.dot(pick, gates, preferred_element_type=jnp.float32)
+        picked = jnp.where(high | low, picked, 0.0)
+        gate_ref[0, mine] = picked[:SLOTS]
+        gate_ref[1, mine] = picked[SLOTS:]
 
 
 def pick_call(ids, gathered, width):
     groups = gathered.shape[0] // GROUP
+    step = 2
     return pl.pallas_call(
         pick_kernel,
         out_shape=(
@@ -153,16 +164,21 @@
         ),
         grid_spec=pltpu.PrefetchScalarGridSpec(
             num_scalar_prefetch=1,
-            grid=(groups,),
-            in_specs=[pl.BlockSpec((GROUP, width + GATE_LANES), lambda g, ids: (g, 0))],
+            grid=(groups // step,),
+            in_specs=[pl.BlockSpec((step * GROUP, width + GATE_LANES), lambda g, ids: (g, 0))],
             out_specs=(
-                pl.BlockSpec((2, SLOTS, width), lambda g, ids: (0, g, 0)),
-                pl.BlockSpec((2, SLOTS, GATE_LANES), lambda g, ids: (0, g, 0)),
-                pl.BlockSpec((1, GROUP, 2 * SLOTS), lambda g, ids: (g, 0, 0)),
+                pl.BlockSpec((2, step * SLOTS, width), lambda g, ids: (0, g, 0)),
+                pl.BlockSpec((2, step * SLOTS, GATE_LANES), lambda g, ids: (0, g, 0)),
+                pl.BlockSpec((step, GROUP, 2 * SLOTS), lambda g, ids: (g, 0, 0)),
             ),
+            scratch_shapes=[
+                pltpu.VMEM((GROUP, GROUP), jnp.bfloat16),
+                pltpu.VMEM((2 * SLOTS, GROUP), jnp.float32),
+                pltpu.VMEM((GROUP, 2 * SLOTS), jnp.float32),
+            ],
         ),
         compiler_params=pltpu.CompilerParams(
-            dimension_semantics=("arbitrary",), vmem_limit_bytes=24 << 20
+            dimension_semantics=("arbitrary",), vmem_limit_bytes=26 << 20
         ),
         cost_estimate=pl.CostEstimate(
             flops=4 * groups * SLOTS * GROUP * width,
@@ -173,55 +189,56 @@
     )(ids, gathered)
 
 
-def put_kernel(halves, plane, st_ref, y0_ref, y1_ref, *outs):
-    columns = y0_ref.shape[-1]
+def put_kernel(halves, plane, st_ref, y_ref, *outs):
+    columns = y_ref.shape[-1]
     tile = columns // halves if halves > 1 else min(256, columns)
-    for n in range(columns // tile):
-        cols = slice(n * tile, (n + 1) * tile)
-        y = jnp.concatenate([y0_ref[:, cols], y1_ref[:, cols]], axis=0)
-        out = jnp.dot(st_ref[0], y, preferred_element_type=jnp.float32).astype(jnp.bfloat16)
-        if halves > 1:
-            outs[n][0] = out
-        else:
-            for b in range(RING):
-                outs[0][b, 0, :, cols] = out[b * TOK : (b + 1) * TOK]
-
-
-def put_call(plane, chosen, y0, y1, halves):
+
+    @pl.loop(0, RING)
+    def _(g):
+        mine = pl.ds(pl.multiple_of(g * SLOTS, 16), SLOTS)
+        for n in range(columns // tile):
+            cols = slice(n * tile, (n + 1) * tile)
+            y = jnp.concatenate([y_ref[0, mine, cols], y_ref[1, mine, cols]], axis=0)
+            out = jnp.dot(st_ref[g], y, preferred_element_type=jnp.float32)
+            out = out.astype(jnp.bfloat16)
+            if halves > 1:
+                outs[n][0, pl.ds(pl.multiple_of(g * GROUP, GROUP), GROUP), :] = out
+            else:
+                for b in range(RING):
+                    outs[0][g * RING + b, 0, :, cols] = out[b * TOK : (b + 1) * TOK]
+
+
+def put_call(plane, chosen, y, halves):
     groups = chosen.shape[0]
-    columns = y0.shape[1]
+    columns = y.shape[-1]
     if halves > 1:
         half = columns // halves
         shape = jax.ShapeDtypeStruct((RING, RING * GROUP, half), jnp.bfloat16)
         out_shape = (shape, shape)
+        block = (1, RING * GROUP, half)
         out_specs = (
-            pl.BlockSpec(
-                (1, GROUP, half), lambda g, plane: ((plane[0] + 3 - g // RING) & 3, g % RING, 0)
-            ),
-            pl.BlockSpec(
-                (1, GROUP, half), lambda g, plane: ((g // RING + 3 - plane[0]) & 3, g % RING, 0)
-            ),
+            pl.BlockSpec(block, lambda z, plane: ((plane[0] + 3 - z) & 3, 0, 0)),
+            pl.BlockSpec(block, lambda z, plane: ((z + 3 - plane[0]) & 3, 0, 0)),
         )
     else:
         out_shape = jax.ShapeDtypeStruct((RING * RING, RING, TOK, columns), jnp.bfloat16)
         out_specs = pl.BlockSpec(
-            (RING, 1, TOK, columns), lambda g, plane: (g % RING, g // RING, 0, 0)
+            (RING * RING, 1, TOK, columns), lambda z, plane: (0, z, 0, 0)
         )
     return pl.pallas_call(
         functools.partial(put_kernel, halves),
         out_shape=out_shape,
         grid_spec=pltpu.PrefetchScalarGridSpec(
             num_scalar_prefetch=1,
-            grid=(groups,),
+            grid=(groups // RING,),
             in_specs=[
-                pl.BlockSpec((1, GROUP, 2 * SLOTS), lambda g, plane: (g, 0, 0)),
-                pl.BlockSpec((SLOTS, columns), lambda g, plane: (g, 0)),
-                pl.BlockSpec((SLOTS, columns), lambda g, plane: (g, 0)),
+                pl.BlockSpec((RING, GROUP, 2 * SLOTS), lambda z, plane: (z, 0, 0)),
+                pl.BlockSpec((2, RING * SLOTS, columns), lambda z, plane: (0, z, 0)),
             ],
             out_specs=out_specs,
         ),
         compiler_params=pltpu.CompilerParams(
-            dimension_semantics=("arbitrary",), vmem_limit_bytes=24 << 20
+            dimension_semantics=("arbitrary",), vmem_limit_bytes=26 << 20
         ),
         cost_estimate=pl.CostEstimate(
             flops=4 * groups * GROUP * SLOTS * columns,
@@ -229,17 +246,19 @@
             transcendentals=0,
         ),
         name="put_halves" if halves > 1 else "put",
-    )(plane, chosen, y0, y1)
+    )(plane, chosen, y)
 
 
 def run_hidden(rows, gate, w_gate, w_up):
-    gate_part = jnp.dot(rows, w_gate, preferred_element_type=jnp.float32)
-    up_part = jnp.dot(rows, w_up, preferred_element_type=jnp.float32)
-    return (jax.nn.silu(gate_part) * up_part * gate[:, :1]).astype(jnp.bfloat16)
+    gate = jnp.sum(gate, axis=2, keepdims=True)
+    gate_part = jnp.einsum("erd,edf->erf", rows, w_gate, preferred_element_type=jnp.float32)
+    up_part = jnp.einsum("erd,edf->erf", rows, w_up, preferred_element_type=jnp.float32)
+    return (jax.nn.silu(gate_part) * up_part * gate).astype(jnp.bfloat16)
 
 
 def run_down(hidden, down_weight):
-    return jnp.dot(hidden, down_weight, preferred_element_type=jnp.float32).astype(jnp.bfloat16)
+    part = jnp.einsum("erf,efd->erd", hidden, down_weight, preferred_element_type=jnp.float32)
+    return part.astype(jnp.bfloat16)
 
 
 def add_rounded(a, b):
@@ -264,17 +283,16 @@
     plane = lax.axis_index("z")
     planes = plane.reshape(1).astype(jnp.int32)
     rows, gate, chosen = pick_call(ids, gathered, width)
-    hidden = [run_hidden(rows[e], gate[e], *w[:2]) for e, w in enumerate((own, other))]
-    hidden = lax.optimization_barrier(hidden)
-    downs = (own[2], other[2])
     late = width - PLANE_COLS
-    late_parts = [run_down(h, w[:, :late]) for h, w in zip(hidden, downs)]
-    dense = put_call(planes, chosen, *late_parts, 1)
+    w_gates, w_ups = (jnp.stack(pair) for pair in zip(own[:2], other[:2]))
+    late_downs = jnp.stack([own[2][:, :late], other[2][:, :late]])
+    early_downs = jnp.stack([own[2][:, late:], other[2][:, late:]])
+    hidden = lax.optimization_barrier(run_hidden(rows, gate, w_gates, w_ups))
+    dense = put_call(planes, chosen, run_down(hidden, late_downs), 1)
     summed = lax.psum_scatter(
         dense.reshape(-1, late), ("y", "x"), scatter_dimension=0, tiled=True
     ).reshape(RING, TOK, late)
-    early_parts = [run_down(h, w[:, late:]) for h, w in zip(hidden, downs)]
-    halves = put_call(planes, chosen, *early_parts, 2)
+    halves = put_call(planes, chosen, run_down(hidden, early_downs), 2)
     travel = [half[0] for half in halves]
     for stop in range(1, RING):
         for way, turn in ((0, 1), (1, RING - 1)):

time: 428 us -> 422 us (0.986)
  local copies, waits for them, and re-layouts: 11.3 us -> 27.8 us
  waiting for transfers between devices: 262 us -> 249 us
  Pallas kernels: 42.1 us -> 36.2 us
    another operation x0 -> x4, local copies, waits for them, and re-layouts: none -> 9.47 us  [the longest x2 6.52 us: body(): late_downs = jnp.stack([own[2][:, :late], other[2][:, :late]])]
    all_gather x1, waiting for transfers between devices: 149 us -> 140 us  [body(): gathered = lax.all_gather(packed, ('z', 'y', 'x'), axis=0, tiled=True)]
    unnamed x33 -> x49, local copies, waits for them, and re-layouts: 0.68 us -> 7.02 us
    ppermute x3, waiting for transfers between devices: 11.8 us -> 6.88 us  [body(): late_out = late_out + lax.ppermute(away, 'z', ring).astype(jnp.float32)]
    dot_general x8 -> x4, matrix products: 48.4 us -> 47.7 us  [the longest x1 18 us: run_hidden(): jnp.einsum('erd,edf->erf', rows, w_up, preferred_element_type=jnp.float32)]
  transfers between devices with their start and end apart: 15 -> 15, of which waited for: 11 -> 12; matrix products, arithmetic and copies ran while one was open for 12% -> 10% of each run, Pallas kernels for 7% -> 6%
where the time goes in v4:
time: 422 us
  waiting for transfers between devices  249 us (59%)
  matrix products  48.7 us (12%)
  Pallas kernels  36.2 us (9%)
  starting transfers between devices  29.4 us (7%)
  local copies, waits for them, and re-layouts  27.8 us (7%)
  other arithmetic  16.6 us (4%)
  between operations  13.9 us (3%)
    all_gather x1, waiting for transfers between devices, body(): gathered = lax.all_gather(packed, ('z', 'y', 'x'), axis=0, tiled=True)  140 us
    ppermute x6, waiting for transfers between devices, body(): lax.ppermute(travel[way], 'z', ring)  84.9 us
    dot_general x1, matrix products, run_hidden(): jnp.einsum('erd,edf->erf', rows, w_up, preferred_element_type=jnp.float32)  18 us
    pallas_call x1, Pallas kernels, pick_call(): pl.pallas_call(pick_kernel, out_shape=(jax.ShapeDtypeStruct((2, groups *...  17.6 us
    dot_general x1, matrix products, run_hidden(): jnp.einsum('erd,edf->erf', rows, w_gate, preferred_element_type=jnp.float32)  17 us
    pallas_call x2, Pallas kernels, put_call(): pl.pallas_call(functools.partial(put_kernel, halves), out_shape=out_shape...  16.8 us
    ppermute x3, starting transfers between devices, body(): late_out = late_out + lax.ppermute(away, 'z', ring).astype(jnp.float32)  15 us
    reduce_scatter x1, waiting for transfers between devices, body(): lax.psum_scatter(dense.reshape(-1, late), ('y', 'x'), scatter_dimension=0...  13.4 us
  transfers between devices with their start and end apart: 15, of which 12 were waited for; matrix products, arithmetic and copies ran while one was open for 10% of the time, Pallas kernels for 6%

profile of v4, /device:TPU:44, one launch (start us, length us, event | category | flops | bytes accessed | tf_op | source)
XLA Modules:
  0.0 421.8 jit_solution(14661892225366867848)
XLA Ops:
  6.5 3.1 multiply_reduce_fusion
  9.6 2.7 fusion.78
  12.3 0.5 copy.29
  12.8 0.1 copy-done.21
  13.1 0.6 fusion.79
  13.7 0.7 fusion.20
  14.3 1.4 fusion.71
  15.9 1.8 fusion.50
  17.7 0.4 fusion.81
  18.2 0.9 concatenate.44
  19.2 0.5 collective-permute-start
  19.7 0.1 collective-permute-start.1
  19.9 3.3 slice_bitcast_fusion.1
  23.1 2.8 collective-permute-done.2
  25.9 3.3 slice_bitcast_fusion
  29.2 140.1 %all-gather.2.cloned.1.call-done.x_ref = bf16[4096,3712]{1,0:T(8,128)(2,1)} async-done(((bf16[64,3712]{1,0:T(8,128)(2,1)}), bf16[4096,3712]{1,0:T(8,128)(2,1)}) %all-gather.2.cloned.1.call-update) | async-done | bytes 30408720 | tf_op jit(solution)/shard_map/all_gather | solution.py:279
  169.3 17.6 %pick.1 = (bf16[2,1280,3584]{2,1,0:T(8,128)(2,1)S(1)}, f32[2,1280,128]{2,1,0:T(8,128)S(1)}, bf16[16,256,160]{2,1,0:T(8,128)(2,1)S(1)}) custom-call(s32[2]{0:T(128)S(1)} %pad_add_fusion.ids, bf16[4096,3712]{1,0:T(8,128)(2,1)} %all-gather.2.cloned.1.call-done.x_ref), custom_call_target="tpu_custom_call" | custom-call | flops 4697620480 | bytes 58720256 | tf_op jit(solution)/shard_map/pick/pallas_call | solution.py:158
  187.0 6.3 %copy-done.2 = bf16[2,1280,3584]{2,1,0:T(8,128)(2,1)} copy-done((bf16[2,1280,3584]{2,1,0:T(8,128)(2,1)}, bf16[2,1280,3584]{2,1,0:T(8,128)(2,1)S(1)}, u32[]{:S(2)}) %copy-start.2) | copy-done | bytes 18350104
  193.3 0.4 reduce_sum.38
  193.7 17.0 %fusion = f32[2,1280,512]{2,1,0:T(8,128)} fusion(bf16[2,1280,3584]{2,1,0:T(8,128)(2,1)} %copy-done.2, bf16[1,3584,512]{2,1,0:T(8,128)(2,1)} %bitcast.24, bf16[1,3584,512]{2,1,0:T(8,128)(2,1)} %param.15), kind=kOutput, calls=%fused_computation.2 | convolution fusion | flops 9398910976 | bytes 30932992 | tf_op jit(solution)/shard_map/erd,edf->erf/dot_general | solution.py:254
  210.8 18.0 %multiply_convert_fusion = bf16[2,1280,512]{2,1,0:T(8,128)(2,1)} fusion(f32[2,1280,512]{2,1,0:T(8,128)} %fusion, f32[2,1280]{1,0:T(2,128)S(1)} %reduce_sum.38, bf16[2,1280,3584]{2,1,0:T(8,128)(2,1)} %copy-done.2, bf16[1,3584,512]{2,1,0:T(8,128)(2,1)} %bitcast.26, bf16[1,3584,512]{2,1,0:T(8,128)(2,1)} %param.16), kind=kOutput, calls=%fused_computation.11 | convolution fusion | flops 9408086016 | bytes 33564672 | tf_op jit(solution)/shard_map/erd,edf->erf/dot_general | solution.py:255
  228.8 8.4 %convolution_convert_fusion.y_ref = bf16[2,1280,2304]{2,1,0:T(8,128)(2,1)S(1)} fusion(bf16[2,1280,512]{2,1,0:T(8,128)(2,1)} %multiply_convert_fusion, bf16[1,512,2304]{2,1,0:T(8,128)(2,1)S(1)} %copy-done.9, bf16[1,512,2304]{2,1,0:T(8,128)(2,1)S(1)} %copy-done.8), kind=kOutput, calls=%fused_computation | convolution fusion | flops 6048055296 | bytes 19136512 | tf_op jit(solution)/shard_map/erf,efd->erd/dot_general | solution.py:260
  237.2 10.5 %put.1 = bf16[16,4,64,2304]{3,2,1,0:T(8,128)(2,1)} custom-call(s32[1]{0:T(128)} %bitcast.11.plane, bf16[16,256,160]{2,1,0:T(8,128)(2,1)S(1)} %get-tuple-element.10.st_ref, bf16[2,1280,2304]{2,1,0:T(8,128)(2,1)S(1)} %convolution_convert_fusion.y_ref), custom_call_target="tpu_custom_call" | custom-call | flops 3019898880 | bytes 28311552 | tf_op jit(solution)/shard_map/put/pallas_call | solution.py:228
  247.8 1.6 slice_bitcast_fusion.3
  249.3 1.4 slice_bitcast_fusion.2
  250.8 4.2 convolution_convert_fusion.1.y_ref
  255.0 6.3 %put_halves.1 = (bf16[4,1024,640]{2,1,0:T(8,128)(2,1)S(1)}, bf16[4,1024,640]{2,1,0:T(8,128)(2,1)S(1)}) custom-call(s32[1]{0:T(128)} %bitcast.11.plane, bf16[16,256,160]{2,1,0:T(8,128)(2,1)S(1)} %get-tuple-element.10.st_ref, bf16[2,1280,1280]{2,1,0:T(8,128)(2,1)S(1)} %convolution_convert_fusion.1.y_ref), custom_call_target="tpu_custom_call" | custom-call | flops 1677721600 | bytes 15728640 | tf_op jit(solution)/shard_map/put_halves/pallas_call | solution.py:228
  261.3 0.1 slice_bitcast_fusion.4
  261.4 1.9 collective-permute-start.9
  263.3 0.1 slice_bitcast_fusion.5
  263.4 0.2 collective-permute-start.6
  263.7 28.1 %collective-permute-done.9 = bf16[1024,640]{1,0:T(8,128)(2,1)S(1)} collective-permute-done((bf16[1024,640]{1,0:T(8,128)(2,1)S(1)}, bf16[1024,640]{1,0:T(8,128)(2,1)S(1)}, u32[]{:S(2)}, u32[]{:S(2)}) %collective-permute-start.9) | collective-permute-done | bytes 1310752 | tf_op jit(solution)/shard_map/ppermute | solution.py:300
  291.8 0.4 fusion.16
  292.2 2.0 collective-permute-start.10
  294.1 0.4 fusion.19
  294.5 0.2 collective-permute-start.7
  294.7 27.1 %collective-permute-done.10 = bf16[1024,640]{1,0:T(8,128)(2,1)S(1)} collective-permute-done((bf16[1024,640]{1,0:T(8,128)(2,1)S(1)}, bf16[1024,640]{1,0:T(8,128)(2,1)S(1)}, u32[]{:S(2)}, u32[]{:S(2)}) %collective-permute-start.10) | collective-permute-done | bytes 1310752 | tf_op jit(solution)/shard_map/ppermute | solution.py:300
  321.8 0.4 fusion.15
  322.2 2.0 collective-permute-start.11
  324.2 0.2 collective-permute-done.7
  324.4 0.4 fusion.18
  324.9 26.5 %collective-permute-done.11 = bf16[1024,640]{1,0:T(8,128)(2,1)S(1)} collective-permute-done((bf16[1024,640]{1,0:T(8,128)(2,1)S(1)}, bf16[1024,640]{1,0:T(8,128)(2,1)S(1)}, u32[]{:S(2)}, u32[]{:S(2)}) %collective-permute-start.11) | collective-permute-done | bytes 1310752 | tf_op jit(solution)/shard_map/ppermute | solution.py:300
  351.4 0.4 fusion.14
  351.7 3.0 collective-permute-done.8
  354.7 0.4 fusion.17
  355.1 1.7 pad_maximum_fusion
  356.8 7.3 %all-to-all-start = ((bf16[16,64,1280]{2,1,0:T(8,128)(2,1)}), bf16[16,64,1280]{2,1,0:T(8,128)(2,1)S(1)}, u32[]{:S(2)}, u32[]{:S(2)}) async-start(bf16[16,64,1280]{2,1,0:T(8,128)(2,1)} %bitcast.152), calls=%async_computation.1 | async-start | bytes 5242880 | tf_op jit(solution)/shard_map/all_to_all | solution.py:302
  364.1 1.2 fusion.60.logits_ref
  365.4 1.8 balance.1
  367.1 1.4 slice_bitcast_fusion.21
  368.6 13.4 %reduce-scatter.2.cloned.1.call-done = bf16[256,2304]{1,0:T(8,128)(2,1)} async-done(((bf16[4096,2304]{1,0:T(8,128)(2,1)}), bf16[256,2304]{1,0:T(8,128)(2,1)}) %reduce-scatter.2.cloned.1.call-update) | async-done | bytes 1179664 | tf_op jit(solution)/shard_map/reduce_scatter | solution.py:292
  382.0 2.1 dynamic-slice_bitcast_fusion.2
  384.0 15.0 %collective-permute-start.4 = (bf16[64,2304]{1,0:T(8,128)(2,1)}, bf16[64,2304]{1,0:T(8,128)(2,1)}, u32[]{:S(2)}, u32[]{:S(2)}) collective-permute-start(bf16[64,2304]{1,0:T(8,128)(2,1)} %get-tuple-element.30), channel_id=1, source_target_pairs={{0,64},{32,96},{64,0},{96,32},{1,65},{33,97},{65,1},{97,33},{2,66}... | collective-permute-start | bytes 884744 | tf_op jit(solution)/shard_map/ppermute | solution.py:308
  399.0 0.6 slice_bitcast_fusion.29
  399.6 1.0 all-to-all-done
  400.6 0.4 convert_reduce_fusion
  401.0 1.5 collective-permute-done.5
  402.6 4.6 %collective-permute-done.4 = bf16[64,2304]{1,0:T(8,128)(2,1)} collective-permute-done((bf16[64,2304]{1,0:T(8,128)(2,1)}, bf16[64,2304]{1,0:T(8,128)(2,1)}, u32[]{:S(2)}, u32[]{:S(2)}) %collective-permute-start.4) | collective-permute-done | bytes 294944 | tf_op jit(solution)/shard_map/ppermute | solution.py:308
  407.2 0.7 collective-permute-done.3
  407.9 1.4 fusion.56
  409.4 1.6 fusion.35
  411.1 0.9 fusion.30
  412.0 0.2 pad_maximum_fusion.1
  412.3 2.6 copy.23
  (66 shorter events, 0.8 us)
Async XLA Ops:
  6.5 7.1 %copy-start = (bf16[24,14336]{1,0:T(8,128)(2,1)S(1)}, bf16[24,14336]{1,0:T(8,128)(2,1)}, u32[]{:S(2)}) copy-start(bf16[24,14336]{1,0:T(8,128)(2,1)} %param.10) | copy-start | bytes 2064388
  6.5 3.1 copy-start.3
  6.5 162.8 %all-gather.2.cloned.1.call-start = ((), (), s32[]{:S(2)}) async-start(), calls=%async_computation.2 | async-start | bytes 30883840 | tf_op jit(solution)/shard_map/all_gather | solution.py:279
  12.3 0.7 copy-start.21
  12.3 0.7 copy-start.10
  12.8 2.9 copy-start.11
  15.9 1.8 copy-start.22
  19.0 362.9 %reduce-scatter.2.cloned.1.call-start = ((), (), s32[]{:S(2)}) async-start(), calls=%async_computation.3 | async-start | bytes 20054016 | tf_op jit(solution)/shard_map/reduce_scatter | solution.py:292
  19.1 6.8 %collective-permute-start.2 = (bf16[512,3584]{1,0:T(8,128)(2,1)}, bf16[512,3584]{1,0:T(8,128)(2,1)}, u32[]{:S(2)}, u32[]{:S(2)}) collective-permute-start(bf16[512,3584]{1,0:T(8,128)(2,1)} %bitcast.153), channel_id=1, source_target_pairs={{0,1},{1,0},{2,3},{3,2},{4,5},{5,4},{6,7},{7,6},{8,9},{9,8},{10,11... | collective-permute-start | bytes 11010056 | tf_op jit(solution)/shard_map/ppermute | solution.py:274
  19.2 174.5 %collective-permute-start = (bf16[3584,512]{1,0:T(8,128)(2,1)}, bf16[3584,512]{1,0:T(8,128)(2,1)}, u32[]{:S(2)}, u32[]{:S(2)}) collective-permute-start(bf16[3584,512]{1,0:T(8,128)(2,1)} %bitcast.161), channel_id=1, source_target_pairs={{0,1},{1,0},{2,3},{3,2},{4,5},{5,4},{6,7},{7,6},{8,9},{9,8},{10,11... | collective-permute-start | bytes 11010056 | tf_op jit(solution)/shard_map/ppermute | solution.py:274
  19.7 191.1 %collective-permute-start.1 = (bf16[3584,512]{1,0:T(8,128)(2,1)}, bf16[3584,512]{1,0:T(8,128)(2,1)}, u32[]{:S(2)}, u32[]{:S(2)}) collective-permute-start(bf16[3584,512]{1,0:T(8,128)(2,1)} %bitcast.162), channel_id=1, source_target_pairs={{0,1},{1,0},{2,3},{3,2},{4,5},{5,4},{6,7},{7,6},{8,9},{9,8},{10,11... | collective-permute-start | bytes 11010056 | tf_op jit(solution)/shard_map/ppermute | solution.py:274
  187.0 6.3 %copy-start.2 = (bf16[2,1280,3584]{2,1,0:T(8,128)(2,1)}, bf16[2,1280,3584]{2,1,0:T(8,128)(2,1)S(1)}, u32[]{:S(2)}) copy-start(bf16[2,1280,3584]{2,1,0:T(8,128)(2,1)S(1)} %get-tuple-element.11) | copy-start | bytes 55050244
  210.7 18.0 %copy-start.8 = (bf16[1,512,2304]{2,1,0:T(8,128)(2,1)S(1)}, bf16[1,512,2304]{2,1,0:T(8,128)(2,1)}, u32[]{:S(2)}) copy-start(bf16[1,512,2304]{2,1,0:T(8,128)(2,1)} %slice_bitcast_fusion.1) | copy-start | bytes 7077892
  210.7 18.0 %copy-start.9 = (bf16[1,512,2304]{2,1,0:T(8,128)(2,1)S(1)}, bf16[1,512,2304]{2,1,0:T(8,128)(2,1)}, u32[]{:S(2)}) copy-start(bf16[1,512,2304]{2,1,0:T(8,128)(2,1)} %slice_bitcast_fusion) | copy-start | bytes 7077892
  247.8 3.0 copy-start.23
  261.4 30.4 %collective-permute-start.9 = (bf16[1024,640]{1,0:T(8,128)(2,1)S(1)}, bf16[1024,640]{1,0:T(8,128)(2,1)S(1)}, u32[]{:S(2)}, u32[]{:S(2)}) collective-permute-start(bf16[1024,640]{1,0:T(8,128)(2,1)S(1)} %slice_bitcast_fusion.4), channel_id=1, source_target_pairs={{0,96},{32,0},{64,32},{96,64},{1,97},{33,1},{65,33},{97,65},{2,98}... | collective-permute-start | bytes 3932168 | tf_op jit(solution)/shard_map/ppermute | solution.py:300
  263.4 30.7 %collective-permute-start.6 = (bf16[1024,640]{1,0:T(8,128)(2,1)S(1)}, bf16[1024,640]{1,0:T(8,128)(2,1)S(1)}, u32[]{:S(2)}, u32[]{:S(2)}) collective-permute-start(bf16[1024,640]{1,0:T(8,128)(2,1)S(1)} %slice_bitcast_fusion.5), channel_id=1, source_target_pairs={{0,32},{32,64},{64,96},{96,0},{1,33},{33,65},{65,97},{97,1},{2,34}... | collective-permute-start | bytes 3932168 | tf_op jit(solution)/shard_map/ppermute | solution.py:300
  292.2 29.7 %collective-permute-start.10 = (bf16[1024,640]{1,0:T(8,128)(2,1)S(1)}, bf16[1024,640]{1,0:T(8,128)(2,1)S(1)}, u32[]{:S(2)}, u32[]{:S(2)}) collective-permute-start(bf16[1024,640]{1,0:T(8,128)(2,1)S(1)} %fusion.16), channel_id=1, source_target_pairs={{0,96},{32,0},{64,32},{96,64},{1,97},{33,1},{65,33},{97,65},{2,98}... | collective-permute-start | bytes 3932168 | tf_op jit(solution)/shard_map/ppermute | solution.py:300
  294.5 29.9 %collective-permute-start.7 = (bf16[1024,640]{1,0:T(8,128)(2,1)S(1)}, bf16[1024,640]{1,0:T(8,128)(2,1)S(1)}, u32[]{:S(2)}, u32[]{:S(2)}) collective-permute-start(bf16[1024,640]{1,0:T(8,128)(2,1)S(1)} %fusion.19), channel_id=1, source_target_pairs={{0,32},{32,64},{64,96},{96,0},{1,33},{33,65},{65,97},{97,1},{2,34}... | collective-permute-start | bytes 3932168 | tf_op jit(solution)/shard_map/ppermute | solution.py:300
  322.2 29.1 %collective-permute-start.11 = (bf16[1024,640]{1,0:T(8,128)(2,1)S(1)}, bf16[1024,640]{1,0:T(8,128)(2,1)S(1)}, u32[]{:S(2)}, u32[]{:S(2)}) collective-permute-start(bf16[1024,640]{1,0:T(8,128)(2,1)S(1)} %fusion.15), channel_id=1, source_target_pairs={{0,96},{32,0},{64,32},{96,64},{1,97},{33,1},{65,33},{97,65},{2,98}... | collective-permute-start | bytes 3932168 | tf_op jit(solution)/shard_map/ppermute | solution.py:300
  324.8 29.9 %collective-permute-start.8 = (bf16[1024,640]{1,0:T(8,128)(2,1)S(1)}, bf16[1024,640]{1,0:T(8,128)(2,1)S(1)}, u32[]{:S(2)}, u32[]{:S(2)}) collective-permute-start(bf16[1024,640]{1,0:T(8,128)(2,1)S(1)} %fusion.18), channel_id=1, source_target_pairs={{0,32},{32,64},{64,96},{96,0},{1,33},{33,65},{65,97},{97,1},{2,34}... | collective-permute-start | bytes 3932168 | tf_op jit(solution)/shard_map/ppermute | solution.py:300
  356.8 43.8 %all-to-all-start = ((bf16[16,64,1280]{2,1,0:T(8,128)(2,1)}), bf16[16,64,1280]{2,1,0:T(8,128)(2,1)S(1)}, u32[]{:S(2)}, u32[]{:S(2)}) async-start(bf16[16,64,1280]{2,1,0:T(8,128)(2,1)} %bitcast.152), calls=%async_computation.1 | async-start | bytes 5242880 | tf_op jit(solution)/shard_map/all_to_all | solution.py:302
  384.0 25.3 %copy-start.4 = (bf16[64,1,3584]{2,0,1:T(8,128)(2,1)S(1)}, bf16[64,1,3584]{2,0,1:T(8,128)(2,1)}, u32[]{:S(2)}) copy-start(bf16[64,1,3584]{2,0,1:T(8,128)(2,1)} %get-tuple-element.16) | copy-start | bytes 1376260
  384.0 25.3 %copy-start.5 = (bf16[64,1,3584]{2,0,1:T(8,128)(2,1)S(1)}, bf16[64,1,3584]{2,0,1:T(8,128)(2,1)}, u32[]{:S(2)}) copy-start(bf16[64,1,3584]{2,0,1:T(8,128)(2,1)} %get-tuple-element.17) | copy-start | bytes 1376260
  384.0 18.5 %collective-permute-start.5 = (bf16[64,2304]{1,0:T(8,128)(2,1)}, bf16[64,2304]{1,0:T(8,128)(2,1)}, u32[]{:S(2)}, u32[]{:S(2)}) collective-permute-start(bf16[64,2304]{1,0:T(8,128)(2,1)} %get-tuple-element.29), channel_id=1, source_target_pairs={{0,96},{32,0},{64,32},{96,64},{1,97},{33,1},{65,33},{97,65},{2,98}... | collective-permute-start | bytes 884744 | tf_op jit(solution)/shard_map/ppermute | solution.py:308
  384.0 23.2 %collective-permute-start.4 = (bf16[64,2304]{1,0:T(8,128)(2,1)}, bf16[64,2304]{1,0:T(8,128)(2,1)}, u32[]{:S(2)}, u32[]{:S(2)}) collective-permute-start(bf16[64,2304]{1,0:T(8,128)(2,1)} %get-tuple-element.30), channel_id=1, source_target_pairs={{0,64},{32,96},{64,0},{96,32},{1,65},{33,97},{65,1},{97,33},{2,66}... | collective-permute-start | bytes 884744 | tf_op jit(solution)/shard_map/ppermute | solution.py:308
  399.0 8.9 %collective-permute-start.3 = (bf16[64,2304]{1,0:T(8,128)(2,1)}, bf16[64,2304]{1,0:T(8,128)(2,1)}, u32[]{:S(2)}, u32[]{:S(2)}) collective-permute-start(bf16[64,2304]{1,0:T(8,128)(2,1)} %get-tuple-element.28), channel_id=1, source_target_pairs={{0,32},{32,64},{64,96},{96,0},{1,33},{33,65},{65,97},{97,1},{2,34}... | collective-permute-start | bytes 884744 | tf_op jit(solution)/shard_map/ppermute | solution.py:308
  400.6 8.7 %copy-start.6 = (bf16[64,1,3584]{2,0,1:T(8,128)(2,1)S(1)}, bf16[64,1,3584]{2,0,1:T(8,128)(2,1)}, u32[]{:S(2)}) copy-start(bf16[64,1,3584]{2,0,1:T(8,128)(2,1)} %get-tuple-element.18) | copy-start | bytes 1376260
  400.6 8.7 %copy-start.7 = (bf16[64,1,3584]{2,0,1:T(8,128)(2,1)S(1)}, bf16[64,1,3584]{2,0,1:T(8,128)(2,1)}, u32[]{:S(2)}) copy-start(bf16[64,1,3584]{2,0,1:T(8,128)(2,1)} %get-tuple-element.19) | copy-start | bytes 1376260
  400.6 8.7 %copy-start.19 = (f32[64]{0:T(128)S(1)}, f32[64]{0:T(128)}, u32[]{:S(2)}) copy-start(f32[64]{0:T(128)} %get-tuple-element.52) | copy-start | bytes 772
  400.6 8.7 %copy-start.20 = (f32[64]{0:T(128)S(1)}, f32[64]{0:T(128)}, u32[]{:S(2)}) copy-start(f32[64]{0:T(128)} %get-tuple-element.54) | copy-start | bytes 772
  401.0 10.0 %copy-start.12 = (f32[64]{0:T(128)S(1)}, f32[64]{0:T(128)}, u32[]{:S(2)}) copy-start(f32[64]{0:T(128)} %get-tuple-element.42) | copy-start | bytes 772
  401.0 10.0 %copy-start.13 = (f32[64]{0:T(128)S(1)}, f32[64]{0:T(128)}, u32[]{:S(2)}) copy-start(f32[64]{0:T(128)} %get-tuple-element.43) | copy-start | bytes 772
  401.0 10.0 %copy-start.14 = (f32[64]{0:T(128)S(1)}, f32[64]{0:T(128)}, u32[]{:S(2)}) copy-start(f32[64]{0:T(128)} %get-tuple-element.48) | copy-start | bytes 772
  401.0 10.0 %copy-start.15 = (f32[64]{0:T(128)S(1)}, f32[64]{0:T(128)}, u32[]{:S(2)}) copy-start(f32[64]{0:T(128)} %get-tuple-element.49) | copy-start | bytes 772
  401.0 10.0 %copy-start.16 = (f32[64]{0:T(128)S(1)}, f32[64]{0:T(128)}, u32[]{:S(2)}) copy-start(f32[64]{0:T(128)} %get-tuple-element.50) | copy-start | bytes 772
  401.0 10.0 %copy-start.17 = (f32[64]{0:T(128)S(1)}, f32[64]{0:T(128)}, u32[]{:S(2)}) copy-start(f32[64]{0:T(128)} %get-tuple-element.51) | copy-start | bytes 772
  401.0 10.0 %copy-start.18 = (f32[64]{0:T(128)S(1)}, f32[64]{0:T(128)}, u32[]{:S(2)}) copy-start(f32[64]{0:T(128)} %get-tuple-element.53) | copy-start | bytes 772
  412.0 2.9 copy-start.1
Sparse Core Ops, SparseCore 0:
  19.2 150.1 all-gather.1
  247.9 134.0 reduce-scatter.1

commit v5 on v4

--- a/solution.py
+++ b/solution.py
@@ -15,7 +15,8 @@
 SLOTS = GROUP // TOK * CAP
 GATE_LANES = 128
 RING = 4
-PLANE_COLS = 1280
+PLANE_COLS = 1536
+CHUNKS = 2
 
 
 def balance_kernel(logits_ref, out_ref):
@@ -126,9 +127,11 @@
 
     high, low = slot_tables(ids)
     table = high.astype(jnp.float32).astype(jnp.bfloat16)
-    for g in range(x_ref.shape[0] // GROUP):
-        tokens = slice(g * GROUP, (g + 1) * GROUP)
-        mine = slice(g * SLOTS, (g + 1) * SLOTS)
+
+    @pl.loop(0, x_ref.shape[0] // GROUP)
+    def _(g):
+        tokens = pl.ds(pl.multiple_of(g * GROUP, GROUP), GROUP)
+        mine = pl.ds(pl.multiple_of(g * SLOTS, 16), SLOTS)
         gates = x_ref[tokens, width : width + GATE_LANES]
         hit = (gates.astype(jnp.float32) != 0.0).astype(jnp.float32)
         count = jnp.dot(
@@ -178,7 +181,7 @@
             ],
         ),
         compiler_params=pltpu.CompilerParams(
-            dimension_semantics=("arbitrary",), vmem_limit_bytes=26 << 20
+            dimension_semantics=("arbitrary",), vmem_limit_bytes=50 << 20
         ),
         cost_estimate=pl.CostEstimate(
             flops=4 * groups * SLOTS * GROUP * width,
@@ -214,12 +217,12 @@
     if halves > 1:
         half = columns // halves
         shape = jax.ShapeDtypeStruct((RING, RING * GROUP, half), jnp.bfloat16)
-        out_shape = (shape, shape)
+        out_shape = (shape,) * halves
         block = (1, RING * GROUP, half)
         out_specs = (
             pl.BlockSpec(block, lambda z, plane: ((plane[0] + 3 - z) & 3, 0, 0)),
             pl.BlockSpec(block, lambda z, plane: ((z + 3 - plane[0]) & 3, 0, 0)),
-        )
+        ) * (halves // 2)
     else:
         out_shape = jax.ShapeDtypeStruct((RING * RING, RING, TOK, columns), jnp.bfloat16)
         out_specs = pl.BlockSpec(
@@ -282,31 +285,38 @@
     ids = jnp.stack([pair + core, pair + 1 - core]).astype(jnp.int32)
     plane = lax.axis_index("z")
     planes = plane.reshape(1).astype(jnp.int32)
-    rows, gate, chosen = pick_call(ids, gathered, width)
     late = width - PLANE_COLS
     w_gates, w_ups = (jnp.stack(pair) for pair in zip(own[:2], other[:2]))
     late_downs = jnp.stack([own[2][:, :late], other[2][:, :late]])
     early_downs = jnp.stack([own[2][:, late:], other[2][:, late:]])
+    gathered, late_downs, early_downs = lax.optimization_barrier(
+        (gathered, late_downs, early_downs)
+    )
+    rows, gate, chosen = pick_call(ids, gathered, width)
     hidden = lax.optimization_barrier(run_hidden(rows, gate, w_gates, w_ups))
     dense = put_call(planes, chosen, run_down(hidden, late_downs), 1)
     summed = lax.psum_scatter(
         dense.reshape(-1, late), ("y", "x"), scatter_dimension=0, tiled=True
     ).reshape(RING, TOK, late)
-    halves = put_call(planes, chosen, run_down(hidden, early_downs), 2)
+    halves = put_call(planes, chosen, run_down(hidden, early_downs), 2 * CHUNKS)
     travel = [half[0] for half in halves]
     for stop in range(1, RING):
-        for way, turn in ((0, 1), (1, RING - 1)):
+        for part in range(2 * CHUNKS):
+            turn = (1, RING - 1)[part % 2]
             ring = [(i, (i + turn) % RING) for i in range(RING)]
-            travel[way] = add_rounded(lax.ppermute(travel[way], "z", ring), halves[way][stop])
-    shares = jnp.concatenate(travel, axis=1).reshape(RING * RING, TOK, PLANE_COLS)
-    shares = lax.all_to_all(shares, ("y", "x"), split_axis=0, concat_axis=0, tiled=True)
-    early_out = jnp.sum(shares.astype(jnp.float32), axis=0)
+            travel[part] = add_rounded(lax.ppermute(travel[part], "z", ring), halves[part][stop])
+    early_out = []
+    for chunk in range(CHUNKS):
+        shares = jnp.concatenate(travel[2 * chunk : 2 * chunk + 2], axis=1)
+        shares = shares.reshape(RING * RING, TOK, PLANE_COLS // CHUNKS)
+        shares = lax.all_to_all(shares, ("y", "x"), split_axis=0, concat_axis=0, tiled=True)
+        early_out.append(jnp.sum(shares.astype(jnp.float32), axis=0))
     late_out = lax.dynamic_index_in_dim(summed, plane, 0, keepdims=False).astype(jnp.float32)
     for shift in range(1, RING):
         away = lax.dynamic_index_in_dim(summed, (plane + shift) % RING, 0, keepdims=False)
         ring = [(i, (i + shift) % RING) for i in range(RING)]
         late_out = late_out + lax.ppermute(away, "z", ring).astype(jnp.float32)
-    moe_out = jnp.concatenate([late_out, early_out], axis=1)
+    moe_out = jnp.concatenate([late_out] + early_out, axis=1)
     return mix_output(streams, mixing, post, moe_out)
 
 

time: 422 us -> 423 us (level); the launches traced: 422 us -> 416 us
  waiting for transfers between devices: 249 us -> 225 us
  other arithmetic: 16.6 us -> 28.6 us
  local copies, waits for them, and re-layouts: 27.8 us -> 16.7 us
  starting transfers between devices: 29.4 us -> 38.2 us
  Pallas kernels: 36.2 us -> 42.4 us
    reduce_scatter x1, waiting for transfers between devices: 13.4 us -> 0.02 us  [body(): lax.psum_scatter(dense.reshape(-1, late), ('y', 'x'), scatter_dimension=0...]
    ppermute x6 -> x12, starting transfers between devices: 6.37 us -> 16.9 us  [body(): lax.ppermute(travel[part], 'z', ring)]
    ppermute x3, starting transfers between devices: 15 us -> 6.05 us  [body(): late_out = late_out + lax.ppermute(away, 'z', ring).astype(jnp.float32)]
    all_to_all x1 -> x2, starting transfers between devices: 7.3 us -> 14.6 us  [body(): lax.all_to_all(shares, ('y', 'x'), split_axis=0, concat_axis=0, tiled=True)]
    ppermute x3, waiting for transfers between devices: 6.88 us -> 0.01 us  [body(): late_out = late_out + lax.ppermute(away, 'z', ring).astype(jnp.float32)]
    unnamed x49 -> x31, local copies, waits for them, and re-layouts: 7.02 us -> 0.67 us
    pallas_call x1, Pallas kernels: 17.6 us -> 23.6 us  [pick_call(): pl.pallas_call(pick_kernel, out_shape=(jax.ShapeDtypeStruct((2, groups *...]
    convert_element_type x6 -> x12, other arithmetic: 2.22 us -> 6.81 us  [add_rounded(): return (a.astype(jnp.float32) + b.astype(jnp.float32)).astype(jnp.bfloat16)]
  transfers between devices with their start and end apart: 15 -> 22, of which waited for: 12 -> 11; matrix products, arithmetic and copies ran while one was open for 10% -> 12% of each run, Pallas kernels for 6% -> 8%
where the time goes in v5:
time: 423 us; the launch traced here: 416 us
  waiting for transfers between devices  225 us (53%)
  matrix products  50.6 us (12%)
  Pallas kernels  42.4 us (10%)
  starting transfers between devices  38.2 us (9%)
  other arithmetic  28.6 us (7%)
  local copies, waits for them, and re-layouts  16.7 us (4%)
  between operations  13.8 us (3%)
    all_gather x1, waiting for transfers between devices, body(): gathered = lax.all_gather(packed, ('z', 'y', 'x'), axis=0, tiled=True)  136 us
    ppermute x12, waiting for transfers between devices, body(): lax.ppermute(travel[part], 'z', ring)  82.6 us
    pallas_call x1, Pallas kernels, pick_call(): pl.pallas_call(pick_kernel, out_shape=(jax.ShapeDtypeStruct((2, groups *...  23.6 us
    dot_general x1, matrix products, run_hidden(): jnp.einsum('erd,edf->erf', rows, w_up, preferred_element_type=jnp.float32)  18 us
    dot_general x1, matrix products, run_hidden(): jnp.einsum('erd,edf->erf', rows, w_gate, preferred_element_type=jnp.float32)  17.1 us
    pallas_call x2, Pallas kernels, put_call(): pl.pallas_call(functools.partial(put_kernel, halves), out_shape=out_shape...  17.1 us
    ppermute x12, starting transfers between devices, body(): lax.ppermute(travel[part], 'z', ring)  16.9 us
    all_to_all x2, starting transfers between devices, body(): lax.all_to_all(shares, ('y', 'x'), split_axis=0, concat_axis=0, tiled=True)  14.6 us
  transfers between devices with their start and end apart: 22, of which 11 were waited for; matrix products, arithmetic and copies ran while one was open for 12% of the time, Pallas kernels for 8%

profile of v5, /device:TPU:44, one launch (start us, length us, event | category | flops | bytes accessed | tf_op | source)
XLA Modules:
  0.0 415.5 jit_solution(3280674451567907792)
XLA Ops:
  6.5 3.1 multiply_reduce_fusion
  9.6 2.7 fusion.76
  12.3 0.5 copy.29
  13.1 0.7 fusion.77
  13.7 0.7 fusion.8
  14.4 1.3 fusion.71
  15.9 1.8 fusion.50
  18.2 0.9 concatenate.49
  19.2 0.5 collective-permute-start.1
  19.9 1.7 slice_bitcast_fusion.1
  21.6 1.5 slice_bitcast_fusion.3
  23.1 2.8 collective-permute-done
  26.0 1.7 slice_bitcast_fusion
  27.7 1.5 slice_bitcast_fusion.2
  29.2 2.3 pad_maximum_fusion
  31.5 2.0 pad_maximum_fusion.1
  33.5 135.9 %all-gather.2.cloned.1.call-done.x_ref = bf16[4096,3712]{1,0:T(8,128)(2,1)} async-done(((bf16[64,3712]{1,0:T(8,128)(2,1)}), bf16[4096,3712]{1,0:T(8,128)(2,1)}) %all-gather.2.cloned.1.call-update) | async-done | bytes 30408720 | tf_op jit(solution)/shard_map/all_gather | solution.py:282
  169.4 23.6 %pick.1 = (bf16[2,1280,3584]{2,1,0:T(8,128)(2,1)}, f32[2,1280,128]{2,1,0:T(8,128)S(1)}, bf16[16,256,160]{2,1,0:T(8,128)(2,1)S(1)}) custom-call(s32[2]{0:T(128)S(1)} %pad_add_fusion.ids, bf16[4096,3712]{1,0:T(8,128)(2,1)} %all-gather.2.cloned.1.call-done.x_ref), custom_call_target="tpu_custom_call" | custom-call | flops 4697620480 | bytes 58720256 | tf_op jit(solution)/shard_map/pick/pallas_call | solution.py:161
  192.9 0.4 reduce_sum.47
  193.4 17.1 %fusion = f32[2,1280,512]{2,1,0:T(8,128)} fusion(bf16[2,1280,3584]{2,1,0:T(8,128)(2,1)} %get-tuple-element.17, bf16[1,3584,512]{2,1,0:T(8,128)(2,1)} %bitcast.29, bf16[1,3584,512]{2,1,0:T(8,128)(2,1)} %param.15), kind=kOutput, calls=%fused_computation.2 | convolution fusion | flops 9398910976 | bytes 30932992 | tf_op jit(solution)/shard_map/erd,edf->erf/dot_general | solution.py:257
  210.4 18.0 %multiply_convert_fusion = bf16[2,1280,512]{2,1,0:T(8,128)(2,1)} fusion(f32[2,1280,512]{2,1,0:T(8,128)} %fusion, f32[2,1280]{1,0:T(2,128)S(1)} %reduce_sum.47, bf16[2,1280,3584]{2,1,0:T(8,128)(2,1)} %get-tuple-element.17, bf16[1,3584,512]{2,1,0:T(8,128)(2,1)} %bitcast.31, bf16[1,3584,512]{2,1,0:T(8,128)(2,1)} %param.16), kind=kOutput, calls=%fused_computation.10 | convolution fusion | flops 9408086016 | bytes 33564672 | tf_op jit(solution)/shard_map/erd,edf->erf/dot_general | solution.py:258
  228.4 7.6 %convolution_convert_fusion.y_ref = bf16[2,1280,2048]{2,1,0:T(8,128)(2,1)S(1)} fusion(bf16[2,1280,512]{2,1,0:T(8,128)(2,1)} %multiply_convert_fusion, bf16[2,512,2048]{2,1,0:T(8,128)(2,1)S(1)} %copy-done.10), kind=kOutput, calls=%fused_computation | convolution fusion | flops 5373952000 | bytes 17301504 | tf_op jit(solution)/shard_map/erf,efd->erd/dot_general | solution.py:263
  236.0 9.6 %put.1 = bf16[16,4,64,2048]{3,2,1,0:T(8,128)(2,1)} custom-call(s32[1]{0:T(128)} %bitcast.11.plane, bf16[16,256,160]{2,1,0:T(8,128)(2,1)S(1)} %get-tuple-element.16.st_ref, bf16[2,1280,2048]{2,1,0:T(8,128)(2,1)S(1)} %convolution_convert_fusion.y_ref), custom_call_target="tpu_custom_call" | custom-call | flops 2684354560 | bytes 25165824 | tf_op jit(solution)/shard_map/put/pallas_call | solution.py:231
  245.6 6.9 %convolution_convert_fusion.1.y_ref = bf16[2,1280,1536]{2,1,0:T(8,128)(2,1)S(1)} fusion(bf16[2,1280,512]{2,1,0:T(8,128)(2,1)} %multiply_convert_fusion, bf16[2,512,1536]{2,1,0:T(8,128)(2,1)} %pad_maximum_fusion.1), kind=kOutput, calls=%fused_computation.1 | convolution fusion | flops 4030464000 | bytes 13631488 | tf_op jit(solution)/shard_map/erf,efd->erd/dot_general | solution.py:263
  252.6 7.5 %put_halves.1 = (bf16[4,1024,384]{2,1,0:T(8,128)(2,1)S(1)}, bf16[4,1024,384]{2,1,0:T(8,128)(2,1)S(1)}, bf16[4,1024,384]{2,1,0:T(8,128)(2,1)S(1)}, bf16[4,1024,384]{2,1,0:T(8,128)(2,1)S(1)}) custom-call(s32[1]{0:T(128)} %bitcast.11.plane, bf16[16,256,160]{2,1,0:T(8,128)(2,1)S(1)} %get-tuple-element.16.st_ref, ...), custom_call_target="tpu_custom_call" | custom-call | flops 2013265920 | bytes 18874368 | tf_op jit(solution)/shard_map/put_halves/pallas_call | solution.py:231
  260.2 1.9 collective-permute-start.15
  262.5 1.9 collective-permute-start.9
  264.4 16.2 %collective-permute-done.15 = bf16[1024,384]{1,0:T(8,128)(2,1)S(1)} collective-permute-done((bf16[1024,384]{1,0:T(8,128)(2,1)S(1)}, bf16[1024,384]{1,0:T(8,128)(2,1)S(1)}, u32[]{:S(2)}, u32[]{:S(2)}) %collective-permute-start.15) | collective-permute-done | bytes 786464 | tf_op jit(solution)/shard_map/ppermute | solution.py:307
  280.9 2.0 collective-permute-start.16
  283.3 1.7 collective-permute-start.6
  285.0 12.5 %collective-permute-done.9 = bf16[1024,384]{1,0:T(8,128)(2,1)S(1)} collective-permute-done((bf16[1024,384]{1,0:T(8,128)(2,1)S(1)}, bf16[1024,384]{1,0:T(8,128)(2,1)S(1)}, u32[]{:S(2)}, u32[]{:S(2)}) %collective-permute-start.9) | collective-permute-done | bytes 786464 | tf_op jit(solution)/shard_map/ppermute | solution.py:307
  297.7 2.0 collective-permute-start.10
  299.7 14.7 %collective-permute-done.16 = bf16[1024,384]{1,0:T(8,128)(2,1)S(1)} collective-permute-done((bf16[1024,384]{1,0:T(8,128)(2,1)S(1)}, bf16[1024,384]{1,0:T(8,128)(2,1)S(1)}, u32[]{:S(2)}, u32[]{:S(2)}) %collective-permute-start.16) | collective-permute-done | bytes 786464 | tf_op jit(solution)/shard_map/ppermute | solution.py:307
  314.6 2.0 collective-permute-start.17
  317.2 1.1 fusion.21
  318.3 1.4 collective-permute-start.7
  319.7 11.5 %collective-permute-done.10 = bf16[1024,384]{1,0:T(8,128)(2,1)S(1)} collective-permute-done((bf16[1024,384]{1,0:T(8,128)(2,1)S(1)}, bf16[1024,384]{1,0:T(8,128)(2,1)S(1)}, u32[]{:S(2)}, u32[]{:S(2)}) %collective-permute-start.10) | collective-permute-done | bytes 786464 | tf_op jit(solution)/shard_map/ppermute | solution.py:307
  331.2 1.1 fusion.17
  332.3 1.9 collective-permute-start.11
  334.2 13.9 %collective-permute-done.17 = bf16[1024,384]{1,0:T(8,128)(2,1)S(1)} collective-permute-done((bf16[1024,384]{1,0:T(8,128)(2,1)S(1)}, bf16[1024,384]{1,0:T(8,128)(2,1)S(1)}, u32[]{:S(2)}, u32[]{:S(2)}) %collective-permute-start.17) | collective-permute-done | bytes 786464 | tf_op jit(solution)/shard_map/ppermute | solution.py:307
  348.5 1.3 pad_maximum_fusion.4
  349.8 7.3 %all-to-all-start.1 = ((bf16[16,64,768]{2,1,0:T(8,128)(2,1)}), bf16[16,64,768]{2,1,0:T(8,128)(2,1)}, u32[]{:S(2)}, u32[]{:S(2)}) async-start(bf16[16,64,768]{2,1,0:T(8,128)(2,1)} %bitcast.178), calls=%async_computation.2 | async-start | bytes 3145728 | tf_op jit(solution)/shard_map/all_to_all | solution.py:312
  357.1 1.3 fusion.20
  358.5 1.4 collective-permute-start.8
  359.9 3.8 collective-permute-done.11
  363.7 1.6 fusion.16
  365.2 9.9 %collective-permute-done.8 = bf16[1024,384]{1,0:T(8,128)(2,1)S(1)} collective-permute-done((bf16[1024,384]{1,0:T(8,128)(2,1)S(1)}, bf16[1024,384]{1,0:T(8,128)(2,1)S(1)}, u32[]{:S(2)}, u32[]{:S(2)}) %collective-permute-start.8) | collective-permute-done | bytes 786464 | tf_op jit(solution)/shard_map/ppermute | solution.py:307
  375.3 1.3 pad_maximum_fusion.3
  376.6 7.2 %all-to-all-start = ((bf16[16,64,768]{2,1,0:T(8,128)(2,1)}), bf16[16,64,768]{2,1,0:T(8,128)(2,1)}, u32[]{:S(2)}, u32[]{:S(2)}) async-start(bf16[16,64,768]{2,1,0:T(8,128)(2,1)} %bitcast.47), calls=%async_computation.1 | async-start | bytes 3145728 | tf_op jit(solution)/shard_map/all_to_all | solution.py:312
  383.9 1.4 fusion.60.logits_ref
  385.3 1.8 balance.1
  387.1 0.8 slice_bitcast_fusion.23
  388.0 1.3 dynamic-slice_bitcast_fusion.2
  389.3 3.3 collective-permute-start.5
  392.8 2.5 collective-permute-start.3
  395.3 1.6 convert_reduce_fusion
  397.0 3.9 all-to-all-done
  400.8 1.6 convert_reduce_fusion.1
  402.5 1.2 fusion.56
  403.7 0.5 fusion.45
  404.2 0.5 fusion.40
  404.8 0.5 fusion.35
  405.3 0.5 fusion.30
  406.0 2.6 copy.23
  (76 shorter events, 4.6 us)
Async XLA Ops:
  6.5 7.2 %copy-start = (bf16[24,14336]{1,0:T(8,128)(2,1)S(1)}, bf16[24,14336]{1,0:T(8,128)(2,1)}, u32[]{:S(2)}) copy-start(bf16[24,14336]{1,0:T(8,128)(2,1)} %param.10) | copy-start | bytes 2064388
  6.5 3.1 copy-start.5
  6.5 162.8 %all-gather.2.cloned.1.call-start = ((), (), s32[]{:S(2)}) async-start(), calls=%async_computation.3 | async-start | bytes 30883840 | tf_op jit(solution)/shard_map/all_gather | solution.py:282
  12.3 0.7 copy-start.13
  12.3 0.7 copy-start.11
  12.8 2.9 copy-start.12
  14.4 3.3 copy-start.14
  19.1 368.8 %reduce-scatter.2.cloned.1.call-start = ((), (), s32[]{:S(2)}) async-start(), calls=%async_computation.4 | async-start | bytes 17825792 | tf_op jit(solution)/shard_map/reduce_scatter | solution.py:298
  19.1 6.8 %collective-permute-start = (bf16[512,3584]{1,0:T(8,128)(2,1)}, bf16[512,3584]{1,0:T(8,128)(2,1)}, u32[]{:S(2)}, u32[]{:S(2)}) collective-permute-start(bf16[512,3584]{1,0:T(8,128)(2,1)} %bitcast.187), channel_id=1, source_target_pairs={{0,1},{1,0},{2,3},{3,2},{4,5},{5,4},{6,7},{7,6},{8,9},{9,8},{10,11... | collective-permute-start | bytes 11010056 | tf_op jit(solution)/shard_map/ppermute | solution.py:277
  19.2 174.1 %collective-permute-start.1 = (bf16[3584,512]{1,0:T(8,128)(2,1)}, bf16[3584,512]{1,0:T(8,128)(2,1)}, u32[]{:S(2)}, u32[]{:S(2)}) collective-permute-start(bf16[3584,512]{1,0:T(8,128)(2,1)} %bitcast.193), channel_id=1, source_target_pairs={{0,1},{1,0},{2,3},{3,2},{4,5},{5,4},{6,7},{7,6},{8,9},{9,8},{10,11... | collective-permute-start | bytes 11010056 | tf_op jit(solution)/shard_map/ppermute | solution.py:277
  19.7 190.7 %collective-permute-start.2 = (bf16[3584,512]{1,0:T(8,128)(2,1)}, bf16[3584,512]{1,0:T(8,128)(2,1)}, u32[]{:S(2)}, u32[]{:S(2)}) collective-permute-start(bf16[3584,512]{1,0:T(8,128)(2,1)} %bitcast.194), channel_id=1, source_target_pairs={{0,1},{1,0},{2,3},{3,2},{4,5},{5,4},{6,7},{7,6},{8,9},{9,8},{10,11... | collective-permute-start | bytes 11010056 | tf_op jit(solution)/shard_map/ppermute | solution.py:277
  210.4 18.0 %copy-start.10 = (bf16[2,512,2048]{2,1,0:T(8,128)(2,1)S(1)}, bf16[2,512,2048]{2,1,0:T(8,128)(2,1)}, u32[]{:S(2)}) copy-start(bf16[2,512,2048]{2,1,0:T(8,128)(2,1)} %pad_maximum_fusion) | copy-start | bytes 12582916
  260.0 57.1 %copy-start.2 = (bf16[4,1024,384]{2,1,0:T(8,128)(2,1)}, bf16[4,1024,384]{2,1,0:T(8,128)(2,1)S(1)}, u32[]{:S(2)}) copy-start(bf16[4,1024,384]{2,1,0:T(8,128)(2,1)S(1)} %get-tuple-element.21) | copy-start | bytes 9437188
  260.1 71.1 %copy-start.4 = (bf16[4,1024,384]{2,1,0:T(8,128)(2,1)}, bf16[4,1024,384]{2,1,0:T(8,128)(2,1)S(1)}, u32[]{:S(2)}) copy-start(bf16[4,1024,384]{2,1,0:T(8,128)(2,1)S(1)} %get-tuple-element.22) | copy-start | bytes 9437188
  260.2 20.5 %collective-permute-start.15 = (bf16[1024,384]{1,0:T(8,128)(2,1)S(1)}, bf16[1024,384]{1,0:T(8,128)(2,1)S(1)}, u32[]{:S(2)}, u32[]{:S(2)}) collective-permute-start(bf16[1024,384]{1,0:T(8,128)(2,1)S(1)} %slice_bitcast_fusion.4), channel_id=1, source_target_pairs={{0,96},{32,0},{64,32},{96,64},{1,97},{33,1},{65,33},{97,65},{2,98}... | collective-permute-start | bytes 2359304 | tf_op jit(solution)/shard_map/ppermute | solution.py:307
  262.2 20.6 %collective-permute-start.12 = (bf16[1024,384]{1,0:T(8,128)(2,1)S(1)}, bf16[1024,384]{1,0:T(8,128)(2,1)S(1)}, u32[]{:S(2)}, u32[]{:S(2)}) collective-permute-start(bf16[1024,384]{1,0:T(8,128)(2,1)S(1)} %slice_bitcast_fusion.5), channel_id=1, source_target_pairs={{0,32},{32,64},{64,96},{96,0},{1,33},{33,65},{65,97},{97,1},{2,34}... | collective-permute-start | bytes 2359304 | tf_op jit(solution)/shard_map/ppermute | solution.py:307
  262.5 35.0 %collective-permute-start.9 = (bf16[1024,384]{1,0:T(8,128)(2,1)S(1)}, bf16[1024,384]{1,0:T(8,128)(2,1)S(1)}, u32[]{:S(2)}, u32[]{:S(2)}) collective-permute-start(bf16[1024,384]{1,0:T(8,128)(2,1)S(1)} %slice_bitcast_fusion.6), channel_id=1, source_target_pairs={{0,96},{32,0},{64,32},{96,64},{1,97},{33,1},{65,33},{97,65},{2,98}... | collective-permute-start | bytes 2359304 | tf_op jit(solution)/shard_map/ppermute | solution.py:307
  280.9 33.5 %collective-permute-start.16 = (bf16[1024,384]{1,0:T(8,128)(2,1)S(1)}, bf16[1024,384]{1,0:T(8,128)(2,1)S(1)}, u32[]{:S(2)}, u32[]{:S(2)}) collective-permute-start(bf16[1024,384]{1,0:T(8,128)(2,1)S(1)} %fusion.12), channel_id=1, source_target_pairs={{0,96},{32,0},{64,32},{96,64},{1,97},{33,1},{65,33},{97,65},{2,98}... | collective-permute-start | bytes 2359304 | tf_op jit(solution)/shard_map/ppermute | solution.py:307
  283.0 33.5 %collective-permute-start.13 = (bf16[1024,384]{1,0:T(8,128)(2,1)S(1)}, bf16[1024,384]{1,0:T(8,128)(2,1)S(1)}, u32[]{:S(2)}, u32[]{:S(2)}) collective-permute-start(bf16[1024,384]{1,0:T(8,128)(2,1)S(1)} %fusion.15), channel_id=1, source_target_pairs={{0,32},{32,64},{64,96},{96,0},{1,33},{33,65},{65,97},{97,1},{2,34}... | collective-permute-start | bytes 2359304 | tf_op jit(solution)/shard_map/ppermute | solution.py:307
  283.3 33.8 %collective-permute-start.6 = (bf16[1024,384]{1,0:T(8,128)(2,1)S(1)}, bf16[1024,384]{1,0:T(8,128)(2,1)S(1)}, u32[]{:S(2)}, u32[]{:S(2)}) collective-permute-start(bf16[1024,384]{1,0:T(8,128)(2,1)S(1)} %slice_bitcast_fusion.7), channel_id=1, source_target_pairs={{0,32},{32,64},{64,96},{96,0},{1,33},{33,65},{65,97},{97,1},{2,34}... | collective-permute-start | bytes 2359304 | tf_op jit(solution)/shard_map/ppermute | solution.py:307
  297.7 33.5 %collective-permute-start.10 = (bf16[1024,384]{1,0:T(8,128)(2,1)S(1)}, bf16[1024,384]{1,0:T(8,128)(2,1)S(1)}, u32[]{:S(2)}, u32[]{:S(2)}) collective-permute-start(bf16[1024,384]{1,0:T(8,128)(2,1)S(1)} %fusion.18), channel_id=1, source_target_pairs={{0,96},{32,0},{64,32},{96,64},{1,97},{33,1},{65,33},{97,65},{2,98}... | collective-permute-start | bytes 2359304 | tf_op jit(solution)/shard_map/ppermute | solution.py:307
  314.6 33.5 %collective-permute-start.17 = (bf16[1024,384]{1,0:T(8,128)(2,1)S(1)}, bf16[1024,384]{1,0:T(8,128)(2,1)S(1)}, u32[]{:S(2)}, u32[]{:S(2)}) collective-permute-start(bf16[1024,384]{1,0:T(8,128)(2,1)S(1)} %fusion.11), channel_id=1, source_target_pairs={{0,96},{32,0},{64,32},{96,64},{1,97},{33,1},{65,33},{97,65},{2,98}... | collective-permute-start | bytes 2359304 | tf_op jit(solution)/shard_map/ppermute | solution.py:307
  316.7 31.5 %collective-permute-start.14 = (bf16[1024,384]{1,0:T(8,128)(2,1)S(1)}, bf16[1024,384]{1,0:T(8,128)(2,1)S(1)}, u32[]{:S(2)}, u32[]{:S(2)}) collective-permute-start(bf16[1024,384]{1,0:T(8,128)(2,1)S(1)} %fusion.14), channel_id=1, source_target_pairs={{0,32},{32,64},{64,96},{96,0},{1,33},{33,65},{65,97},{97,1},{2,34}... | collective-permute-start | bytes 2359304 | tf_op jit(solution)/shard_map/ppermute | solution.py:307
  318.3 38.9 %collective-permute-start.7 = (bf16[1024,384]{1,0:T(8,128)(2,1)}, bf16[1024,384]{1,0:T(8,128)(2,1)}, u32[]{:S(2)}, u32[]{:S(2)}) collective-permute-start(bf16[1024,384]{1,0:T(8,128)(2,1)} %fusion.21), channel_id=1, source_target_pairs={{0,32},{32,64},{64,96},{96,0},{1,33},{33,65},{65,97},{97,1},{2,34}... | collective-permute-start | bytes 2359304 | tf_op jit(solution)/shard_map/ppermute | solution.py:307
  332.3 31.4 %collective-permute-start.11 = (bf16[1024,384]{1,0:T(8,128)(2,1)}, bf16[1024,384]{1,0:T(8,128)(2,1)}, u32[]{:S(2)}, u32[]{:S(2)}) collective-permute-start(bf16[1024,384]{1,0:T(8,128)(2,1)} %fusion.17), channel_id=1, source_target_pairs={{0,96},{32,0},{64,32},{96,64},{1,97},{33,1},{65,33},{97,65},{2,98}... | collective-permute-start | bytes 2359304 | tf_op jit(solution)/shard_map/ppermute | solution.py:307
  348.5 8.6 %copy-start.3 = (bf16[4,1024,384]{2,1,0:T(8,128)(2,1)S(1)}, bf16[4,1024,384]{2,1,0:T(8,128)(2,1)}, u32[]{:S(2)}) copy-start(bf16[4,1024,384]{2,1,0:T(8,128)(2,1)} %copy-done.2) | copy-start | bytes 9437188
  349.8 26.8 %all-to-all-start.1 = ((bf16[16,64,768]{2,1,0:T(8,128)(2,1)}), bf16[16,64,768]{2,1,0:T(8,128)(2,1)}, u32[]{:S(2)}, u32[]{:S(2)}) async-start(bf16[16,64,768]{2,1,0:T(8,128)(2,1)} %bitcast.178), calls=%async_computation.2 | async-start | bytes 3145728 | tf_op jit(solution)/shard_map/all_to_all | solution.py:312
  358.5 16.7 %collective-permute-start.8 = (bf16[1024,384]{1,0:T(8,128)(2,1)S(1)}, bf16[1024,384]{1,0:T(8,128)(2,1)S(1)}, u32[]{:S(2)}, u32[]{:S(2)}) collective-permute-start(bf16[1024,384]{1,0:T(8,128)(2,1)S(1)} %fusion.20), channel_id=1, source_target_pairs={{0,32},{32,64},{64,96},{96,0},{1,33},{33,65},{65,97},{97,1},{2,34}... | collective-permute-start | bytes 2359304 | tf_op jit(solution)/shard_map/ppermute | solution.py:307
  376.6 24.2 %all-to-all-start = ((bf16[16,64,768]{2,1,0:T(8,128)(2,1)}), bf16[16,64,768]{2,1,0:T(8,128)(2,1)}, u32[]{:S(2)}, u32[]{:S(2)}) async-start(bf16[16,64,768]{2,1,0:T(8,128)(2,1)} %bitcast.47), calls=%async_computation.1 | async-start | bytes 3145728 | tf_op jit(solution)/shard_map/all_to_all | solution.py:312
  387.9 15.7 %copy-start.6 = (bf16[64,1,3584]{2,0,1:T(8,128)(2,1)S(1)}, bf16[64,1,3584]{2,0,1:T(8,128)(2,1)}, u32[]{:S(2)}) copy-start(bf16[64,1,3584]{2,0,1:T(8,128)(2,1)} %get-tuple-element.26) | copy-start | bytes 1376260
  387.9 15.7 %copy-start.7 = (bf16[64,1,3584]{2,0,1:T(8,128)(2,1)S(1)}, bf16[64,1,3584]{2,0,1:T(8,128)(2,1)}, u32[]{:S(2)}) copy-start(bf16[64,1,3584]{2,0,1:T(8,128)(2,1)} %get-tuple-element.27) | copy-start | bytes 1376260
  388.0 15.7 %copy-start.8 = (bf16[64,1,3584]{2,0,1:T(8,128)(2,1)S(1)}, bf16[64,1,3584]{2,0,1:T(8,128)(2,1)}, u32[]{:S(2)}) copy-start(bf16[64,1,3584]{2,0,1:T(8,128)(2,1)} %get-tuple-element.28) | copy-start | bytes 1376260
  388.0 15.7 %copy-start.9 = (bf16[64,1,3584]{2,0,1:T(8,128)(2,1)S(1)}, bf16[64,1,3584]{2,0,1:T(8,128)(2,1)}, u32[]{:S(2)}) copy-start(bf16[64,1,3584]{2,0,1:T(8,128)(2,1)} %get-tuple-element.29) | copy-start | bytes 1376260
  389.3 13.2 %collective-permute-start.5 = (bf16[64,2048]{1,0:T(8,128)(2,1)S(1)}, bf16[64,2048]{1,0:T(8,128)(2,1)S(1)}, u32[]{:S(2)}, u32[]{:S(2)}) collective-permute-start(bf16[64,2048]{1,0:T(8,128)(2,1)S(1)} %get-tuple-element.35), channel_id=1, source_target_pairs={{0,96},{32,0},{64,32},{96,64},{1,97},{33,1},{65,33},{97,65},{2,98}... | collective-permute-start | bytes 786440 | tf_op jit(solution)/shard_map/ppermute | solution.py:318
  392.6 9.9 %collective-permute-start.4 = (bf16[64,2048]{1,0:T(8,128)(2,1)S(1)}, bf16[64,2048]{1,0:T(8,128)(2,1)S(1)}, u32[]{:S(2)}, u32[]{:S(2)}) collective-permute-start(bf16[64,2048]{1,0:T(8,128)(2,1)S(1)} %get-tuple-element.36), channel_id=1, source_target_pairs={{0,64},{32,96},{64,0},{96,32},{1,65},{33,97},{65,1},{97,33},{2,66}... | collective-permute-start | bytes 786440 | tf_op jit(solution)/shard_map/ppermute | solution.py:318
  392.8 9.7 %collective-permute-start.3 = (bf16[64,2048]{1,0:T(8,128)(2,1)S(1)}, bf16[64,2048]{1,0:T(8,128)(2,1)}, u32[]{:S(2)}, u32[]{:S(2)}) collective-permute-start(bf16[64,2048]{1,0:T(8,128)(2,1)S(1)} %get-tuple-element.34), channel_id=1, source_target_pairs={{0,32},{32,64},{64,96},{96,0},{1,33},{33,65},{65,97},{97,1},{2,34}... | collective-permute-start | bytes 786440 | tf_op jit(solution)/shard_map/ppermute | solution.py:318
  405.3 3.4 copy-start.1
Sparse Core Ops, SparseCore 0:
  19.2 150.1 all-gather.1
  245.8 110.0 reduce-scatter.1

commit v6 on v5

--- a/solution.py
+++ b/solution.py
@@ -15,8 +15,7 @@
 SLOTS = GROUP // TOK * CAP
 GATE_LANES = 128
 RING = 4
-PLANE_COLS = 1536
-CHUNKS = 2
+CHUNKS = (512, 768)
 
 
 def balance_kernel(logits_ref, out_ref):
@@ -181,7 +180,7 @@
             ],
         ),
         compiler_params=pltpu.CompilerParams(
-            dimension_semantics=("arbitrary",), vmem_limit_bytes=50 << 20
+            dimension_semantics=("arbitrary",), vmem_limit_bytes=26 << 20
         ),
         cost_estimate=pl.CostEstimate(
             flops=4 * groups * SLOTS * GROUP * width,
@@ -192,51 +191,53 @@
     )(ids, gathered)
 
 
-def put_kernel(halves, plane, st_ref, y_ref, *outs):
-    columns = y_ref.shape[-1]
-    tile = columns // halves if halves > 1 else min(256, columns)
+def put_kernel(widths, plane, st_ref, y0_ref, y1_ref, *outs):
+    columns = y0_ref.shape[-1]
+    tile = min(256, columns)
+    cuts = widths or (tile,) * (columns // tile)
 
     @pl.loop(0, RING)
     def _(g):
         mine = pl.ds(pl.multiple_of(g * SLOTS, 16), SLOTS)
-        for n in range(columns // tile):
-            cols = slice(n * tile, (n + 1) * tile)
-            y = jnp.concatenate([y_ref[0, mine, cols], y_ref[1, mine, cols]], axis=0)
+        for n, cut in enumerate(cuts):
+            cols = slice(sum(cuts[:n]), sum(cuts[: n + 1]))
+            y = jnp.concatenate([y0_ref[mine, cols], y1_ref[mine, cols]], axis=0)
             out = jnp.dot(st_ref[g], y, preferred_element_type=jnp.float32)
             out = out.astype(jnp.bfloat16)
-            if halves > 1:
+            if widths:
                 outs[n][0, pl.ds(pl.multiple_of(g * GROUP, GROUP), GROUP), :] = out
             else:
                 for b in range(RING):
                     outs[0][g * RING + b, 0, :, cols] = out[b * TOK : (b + 1) * TOK]
 
 
-def put_call(plane, chosen, y, halves):
+def put_call(plane, chosen, y0, y1, widths=()):
     groups = chosen.shape[0]
-    columns = y.shape[-1]
-    if halves > 1:
-        half = columns // halves
-        shape = jax.ShapeDtypeStruct((RING, RING * GROUP, half), jnp.bfloat16)
-        out_shape = (shape,) * halves
-        block = (1, RING * GROUP, half)
-        out_specs = (
-            pl.BlockSpec(block, lambda z, plane: ((plane[0] + 3 - z) & 3, 0, 0)),
-            pl.BlockSpec(block, lambda z, plane: ((z + 3 - plane[0]) & 3, 0, 0)),
-        ) * (halves // 2)
+    columns = y0.shape[-1]
+    turns = (lambda z, plane: ((plane[0] + 3 - z) & 3, 0, 0)), (
+        lambda z, plane: ((z + 3 - plane[0]) & 3, 0, 0)
+    )
+    if widths:
+        out_shape = tuple(
+            jax.ShapeDtypeStruct((RING, RING * GROUP, cut), jnp.bfloat16) for cut in widths
+        )
+        out_specs = tuple(
+            pl.BlockSpec((1, RING * GROUP, cut), turns[n % 2]) for n, cut in enumerate(widths)
+        )
     else:
         out_shape = jax.ShapeDtypeStruct((RING * RING, RING, TOK, columns), jnp.bfloat16)
         out_specs = pl.BlockSpec(
             (RING * RING, 1, TOK, columns), lambda z, plane: (0, z, 0, 0)
         )
+    rows = pl.BlockSpec((RING * SLOTS, columns), lambda z, plane: (z, 0))
     return pl.pallas_call(
-        functools.partial(put_kernel, halves),
+        functools.partial(put_kernel, widths),
         out_shape=out_shape,
         grid_spec=pltpu.PrefetchScalarGridSpec(
             num_scalar_prefetch=1,
             grid=(groups // RING,),
             in_specs=[
-                pl.BlockSpec((RING, GROUP, 2 * SLOTS), lambda z, plane: (z, 0, 0)),
-                pl.BlockSpec((2, RING * SLOTS, columns), lambda z, plane: (0, z, 0)),
+                pl.BlockSpec((RING, GROUP, 2 * SLOTS), lambda z, plane: (z, 0, 0)), rows, rows,
             ],
             out_specs=out_specs,
         ),
@@ -248,20 +249,22 @@
             bytes_accessed=3 * groups * GROUP * columns,
             transcendentals=0,
         ),
-        name="put_halves" if halves > 1 else "put",
-    )(plane, chosen, y)
+        name="put_halves" if widths else "put",
+    )(plane, chosen, y0, y1)
 
 
 def run_hidden(rows, gate, w_gate, w_up):
-    gate = jnp.sum(gate, axis=2, keepdims=True)
-    gate_part = jnp.einsum("erd,edf->erf", rows, w_gate, preferred_element_type=jnp.float32)
-    up_part = jnp.einsum("erd,edf->erf", rows, w_up, preferred_element_type=jnp.float32)
+    gate = jnp.sum(gate, axis=1, keepdims=True)
+    gate_part = jnp.dot(rows, w_gate, preferred_element_type=jnp.float32)
+    up_part = jnp.dot(rows, w_up, preferred_element_type=jnp.float32)
     return (jax.nn.silu(gate_part) * up_part * gate).astype(jnp.bfloat16)
 
 
-def run_down(hidden, down_weight):
-    part = jnp.einsum("erf,efd->erd", hidden, down_weight, preferred_element_type=jnp.float32)
-    return part.astype(jnp.bfloat16)
+def run_down(hidden, down_weights):
+    return [
+        jnp.dot(h, w, preferred_element_type=jnp.float32).astype(jnp.bfloat16)
+        for h, w in zip(hidden, down_weights)
+    ]
 
 
 def add_rounded(a, b):
@@ -285,30 +288,31 @@
     ids = jnp.stack([pair + core, pair + 1 - core]).astype(jnp.int32)
     plane = lax.axis_index("z")
     planes = plane.reshape(1).astype(jnp.int32)
-    late = width - PLANE_COLS
-    w_gates, w_ups = (jnp.stack(pair) for pair in zip(own[:2], other[:2]))
-    late_downs = jnp.stack([own[2][:, :late], other[2][:, :late]])
-    early_downs = jnp.stack([own[2][:, late:], other[2][:, late:]])
+    late = width - sum(CHUNKS)
+    downs = (own[2], other[2])
+    late_downs, early_downs = [w[:, :late] for w in downs], [w[:, late:] for w in downs]
     gathered, late_downs, early_downs = lax.optimization_barrier(
         (gathered, late_downs, early_downs)
     )
     rows, gate, chosen = pick_call(ids, gathered, width)
-    hidden = lax.optimization_barrier(run_hidden(rows, gate, w_gates, w_ups))
-    dense = put_call(planes, chosen, run_down(hidden, late_downs), 1)
+    hidden = [run_hidden(rows[e], gate[e], *w[:2]) for e, w in enumerate((own, other))]
+    hidden = lax.optimization_barrier(hidden)
+    dense = put_call(planes, chosen, *run_down(hidden, late_downs))
     summed = lax.psum_scatter(
         dense.reshape(-1, late), ("y", "x"), scatter_dimension=0, tiled=True
     ).reshape(RING, TOK, late)
-    halves = put_call(planes, chosen, run_down(hidden, early_downs), 2 * CHUNKS)
+    widths = tuple(cut // 2 for cut in CHUNKS for way in range(2))
+    halves = put_call(planes, chosen, *run_down(hidden, early_downs), widths)
     travel = [half[0] for half in halves]
     for stop in range(1, RING):
-        for part in range(2 * CHUNKS):
+        for part in range(len(widths)):
             turn = (1, RING - 1)[part % 2]
             ring = [(i, (i + turn) % RING) for i in range(RING)]
             travel[part] = add_rounded(lax.ppermute(travel[part], "z", ring), halves[part][stop])
     early_out = []
-    for chunk in range(CHUNKS):
+    for chunk, cut in enumerate(CHUNKS):
         shares = jnp.concatenate(travel[2 * chunk : 2 * chunk + 2], axis=1)
-        shares = shares.reshape(RING * RING, TOK, PLANE_COLS // CHUNKS)
+        shares = shares.reshape(RING * RING, TOK, cut)
         shares = lax.all_to_all(shares, ("y", "x"), split_axis=0, concat_axis=0, tiled=True)
         early_out.append(jnp.sum(shares.astype(jnp.float32), axis=0))
     late_out = lax.dynamic_index_in_dim(summed, plane, 0, keepdims=False).astype(jnp.float32)

time: 423 us -> 417 us (0.986); the launches traced: 416 us -> 414 us
  waiting for transfers between devices: 225 us -> 237 us
  other arithmetic: 28.6 us -> 21.4 us
  Pallas kernels: 42.4 us -> 36 us
  local copies, waits for them, and re-layouts: 16.7 us -> 22.3 us
    ppermute x12, waiting for transfers between devices: 82.6 us -> 61 us  [body(): lax.ppermute(travel[part], 'z', ring)]
    reduce_scatter x1, waiting for transfers between devices: 0.02 us -> 18.5 us  [body(): lax.psum_scatter(dense.reshape(-1, late), ('y', 'x'), scatter_dimension=0...]
    ppermute x3, waiting for transfers between devices: 0.01 us -> 12.1 us  [body(): late_out = late_out + lax.ppermute(away, 'z', ring).astype(jnp.float32)]
    slice x0 -> x4, local copies, waits for them, and re-layouts: none -> 11.5 us  [the longest x2 6.5 us: body(): w[:, :late]]
    another operation x4 -> x0, local copies, waits for them, and re-layouts: 6.48 us -> none  [the longest x2 3.45 us: body(): late_downs = jnp.stack([own[2][:, :late], other[2][:, :late]])]
    pallas_call x1, Pallas kernels: 23.6 us -> 18.5 us  [pick_call(): pl.pallas_call(pick_kernel, out_shape=(jax.ShapeDtypeStruct((2, groups *...]
    another operation x7 -> x5, other arithmetic: 6.45 us -> 2.16 us  [the longest x1 2.3 us: body(): late_downs = jnp.stack([own[2][:, :late], other[2][:, :late]])]
    dot_general x4 -> x8, matrix products: 49.6 us -> 45.8 us  [the longest x2 16.3 us: run_hidden(): up_part = jnp.dot(rows, w_up, preferred_element_type=jnp.float32)]
  transfers between devices with their start and end apart: 22 -> 22, of which waited for: 11 -> 19; matrix products, arithmetic and copies ran while one was open for 12% -> 13% of each run, Pallas kernels for 8% -> 6%
where the time goes in v6:
time: 417 us; the launch traced here: 414 us
  waiting for transfers between devices  237 us (57%)
  matrix products  46.9 us (11%)
  starting transfers between devices  36.8 us (9%)
  Pallas kernels  36 us (9%)
  local copies, waits for them, and re-layouts  22.3 us (5%)
  other arithmetic  21.4 us (5%)
  between operations  13.8 us (3%)
    all_gather x1, waiting for transfers between devices, body(): gathered = lax.all_gather(packed, ('z', 'y', 'x'), axis=0, tiled=True)  138 us
    ppermute x12, waiting for transfers between devices, body(): lax.ppermute(travel[part], 'z', ring)  61 us
    pallas_call x1, Pallas kernels, pick_call(): pl.pallas_call(pick_kernel, out_shape=(jax.ShapeDtypeStruct((2, groups *...  18.5 us
    reduce_scatter x1, waiting for transfers between devices, body(): lax.psum_scatter(dense.reshape(-1, late), ('y', 'x'), scatter_dimension=0...  18.5 us
    all_to_all x2, starting transfers between devices, body(): lax.all_to_all(shares, ('y', 'x'), split_axis=0, concat_axis=0, tiled=True)  16.6 us
    dot_general x2, matrix products, run_hidden(): up_part = jnp.dot(rows, w_up, preferred_element_type=jnp.float32)  16.3 us
    ppermute x12, starting transfers between devices, body(): lax.ppermute(travel[part], 'z', ring)  15.8 us
    pallas_call x2, Pallas kernels, put_call(): pl.pallas_call(functools.partial(put_kernel, widths), out_shape=out_shape...  15.7 us
  transfers between devices with their start and end apart: 22, of which 19 were waited for; matrix products, arithmetic and copies ran while one was open for 13% of the time, Pallas kernels for 6%

profile of v6, /device:TPU:44, one launch (start us, length us, event | category | flops | bytes accessed | tf_op | source)
XLA Modules:
  0.0 414.0 jit_solution(13927133916824543171)
XLA Ops:
  6.5 3.1 multiply_reduce_fusion
  9.6 2.7 fusion.87
  14.4 1.4 fusion.84
  16.0 1.6 fusion.63
  18.1 0.9 concatenate.49
  19.7 3.3 slice.279
  23.0 2.5 slice.281
  25.8 3.2 slice.280
  29.1 2.5 slice.282
  31.6 137.7 %all-gather.2.cloned.1.call-done.x_ref = bf16[4096,3712]{1,0:T(8,128)(2,1)} async-done(((bf16[64,3712]{1,0:T(8,128)(2,1)}), bf16[4096,3712]{1,0:T(8,128)(2,1)}) %all-gather.2.cloned.1.call-update) | async-done | bytes 30408720 | tf_op jit(solution)/shard_map/all_gather | solution.py:285
  169.3 18.5 %pick.1 = (bf16[2,1280,3584]{2,1,0:T(8,128)(2,1)S(1)}, f32[2,1280,128]{2,1,0:T(8,128)S(1)}, bf16[16,256,160]{2,1,0:T(8,128)(2,1)S(1)}) custom-call(s32[2]{0:T(128)S(1)} %pad_add_fusion.ids, bf16[4096,3712]{1,0:T(8,128)(2,1)} %all-gather.2.cloned.1.call-done.x_ref), custom_call_target="tpu_custom_call" | custom-call | flops 4697620480 | bytes 58720256 | tf_op jit(solution)/shard_map/pick/pallas_call | solution.py:160
  188.2 6.5 %fusion.6 = f32[1280,512]{1,0:T(8,128)} fusion(bf16[2,1280,3584]{2,1,0:T(8,128)(2,1)S(1)} %get-tuple-element.21, bf16[1,3584,512]{2,1,0:T(8,128)(2,1)S(1)} %copy-done.14), kind=kOutput, calls=%fused_computation.8 | convolution fusion | flops 4697620480 | bytes 15466496 | tf_op jit(solution)/shard_map/dot_general | solution.py:258
  194.7 8.6 %fusion.2 = f32[1280,512]{1,0:T(8,128)} fusion(bf16[3584,512]{1,0:T(8,128)(2,1)} %collective-permute-done.1, bf16[2,1280,3584]{2,1,0:T(8,128)(2,1)S(1)} %get-tuple-element.21), kind=kOutput, calls=%fused_computation.4 | convolution fusion | flops 4697620480 | bytes 15466496 | tf_op jit(solution)/shard_map/dot_general | solution.py:258
  203.3 7.5 %fusion.18 = bf16[1280,512]{1,0:T(8,128)(2,1)} fusion(bf16[2,1280,3584]{2,1,0:T(8,128)(2,1)S(1)} %get-tuple-element.21, f32[1280,512]{1,0:T(8,128)} %fusion.6, f32[1280]{0:T(1024)S(1)} %get-tuple-element.34, bf16[1,3584,512]{2,1,0:T(8,128)(2,1)S(1)} %copy-done.15), kind=kOutput, calls=%fused_computation.21 | convolution fusion | flops 4702208000 | bytes 16785408 | tf_op jit(solution)/shard_map/dot_general | solution.py:259
  210.8 8.8 %multiply_convert_fusion.1 = bf16[1280,512]{1,0:T(8,128)(2,1)} fusion(f32[1280,512]{1,0:T(8,128)} %fusion.2, f32[1280]{0:T(1024)S(1)} %get-tuple-element.33, bf16[3584,512]{1,0:T(8,128)(2,1)} %collective-permute-done.2, bf16[2,1280,3584]{2,1,0:T(8,128)(2,1)S(1)} %get-tuple-element.21), kind=kOutput, calls=%fused_computation.22 | convolution fusion | flops 4702208000 | bytes 16785408 | tf_op jit(solution)/shard_map/dot_general | solution.py:259
  219.6 5.3 %convolution_convert_fusion.1.y0_ref = bf16[1280,2304]{1,0:T(8,128)(2,1)S(1)} fusion(bf16[1280,512]{1,0:T(8,128)(2,1)} %fusion.18, bf16[512,2304]{1,0:T(8,128)(2,1)S(1)} %copy-done.8), kind=kOutput, calls=%fused_computation.1 | convolution fusion | flops 3022848000 | bytes 9568256 | tf_op jit(solution)/shard_map/dot_general | solution.py:265
  224.9 3.6 convolution_convert_fusion.y1_ref
  228.5 9.9 %put.1 = bf16[16,4,64,2304]{3,2,1,0:T(8,128)(2,1)} custom-call(s32[1]{0:T(128)} %bitcast.11.plane, bf16[16,256,160]{2,1,0:T(8,128)(2,1)S(1)} %get-tuple-element.20.st_ref, bf16[1280,2304]{1,0:T(8,128)(2,1)S(1)} %convolution_convert_fusion.1.y0_ref, bf16[1280,2304]{1,0:T(8,128)(2,1)S(1)} %convolution_convert_fusion.y1_ref), custom_call_target="tpu_custom_call" | custom-call | flops 3019898880 | bytes 28311552 | tf_op jit(solution)/shard_map/put/pallas_call | solution.py:233
  238.5 3.7 convolution_convert_fusion.3.y0_ref
  242.2 1.9 convolution_convert_fusion.2.y1_ref
  244.1 5.8 %put_halves.1 = (bf16[4,1024,256]{2,1,0:T(8,128)(2,1)S(1)}, bf16[4,1024,256]{2,1,0:T(8,128)(2,1)S(1)}, bf16[4,1024,384]{2,1,0:T(8,128)(2,1)S(1)}, bf16[4,1024,384]{2,1,0:T(8,128)(2,1)S(1)}) custom-call(s32[1]{0:T(128)} %bitcast.11.plane, bf16[16,256,160]{2,1,0:T(8,128)(2,1)S(1)} %get-tuple-element.20.st_ref, ...), custom_call_target="tpu_custom_call" | custom-call | flops 1677721600 | bytes 15728640 | tf_op jit(solution)/shard_map/put_halves/pallas_call | solution.py:233
  250.0 1.9 collective-permute-start.9
  252.0 1.2 collective-permute-start.15
  253.3 0.9 collective-permute-start.6
  254.5 10.3 %collective-permute-done.9 = bf16[1024,256]{1,0:T(8,128)(2,1)S(1)} collective-permute-done((bf16[1024,256]{1,0:T(8,128)(2,1)S(1)}, bf16[1024,256]{1,0:T(8,128)(2,1)S(1)}, u32[]{:S(2)}, u32[]{:S(2)}) %collective-permute-start.9) | collective-permute-done | bytes 524320 | tf_op jit(solution)/shard_map/ppermute | solution.py:311
  265.0 2.0 collective-permute-start.10
  267.0 1.2 collective-permute-done.6
  268.3 0.9 collective-permute-start.7
  269.2 12.5 %collective-permute-done.15 = bf16[1024,384]{1,0:T(8,128)(2,1)S(1)} collective-permute-done((bf16[1024,384]{1,0:T(8,128)(2,1)S(1)}, bf16[1024,384]{1,0:T(8,128)(2,1)S(1)}, u32[]{:S(2)}, u32[]{:S(2)}) %collective-permute-start.15) | collective-permute-done | bytes 786464 | tf_op jit(solution)/shard_map/ppermute | solution.py:311
  281.9 2.0 collective-permute-start.16
  283.9 1.1 collective-permute-done.12
  285.2 0.9 collective-permute-start.13
  286.2 6.8 %collective-permute-done.10 = bf16[1024,256]{1,0:T(8,128)(2,1)S(1)} collective-permute-done((bf16[1024,256]{1,0:T(8,128)(2,1)S(1)}, bf16[1024,256]{1,0:T(8,128)(2,1)S(1)}, u32[]{:S(2)}, u32[]{:S(2)}) %collective-permute-start.10) | collective-permute-done | bytes 524320 | tf_op jit(solution)/shard_map/ppermute | solution.py:311
  293.1 2.0 collective-permute-start.11
  295.0 1.2 collective-permute-done.7
  296.4 0.9 collective-permute-start.8
  297.3 12.5 %collective-permute-done.16 = bf16[1024,384]{1,0:T(8,128)(2,1)S(1)} collective-permute-done((bf16[1024,384]{1,0:T(8,128)(2,1)S(1)}, bf16[1024,384]{1,0:T(8,128)(2,1)S(1)}, u32[]{:S(2)}, u32[]{:S(2)}) %collective-permute-start.16) | collective-permute-done | bytes 786464 | tf_op jit(solution)/shard_map/ppermute | solution.py:311
  310.0 2.0 collective-permute-start.17
  312.0 1.1 collective-permute-done.13
  313.1 1.1 fusion.27
  314.2 0.9 collective-permute-start.14
  315.1 6.0 %collective-permute-done.11 = bf16[1024,256]{1,0:T(8,128)(2,1)S(1)} collective-permute-done((bf16[1024,256]{1,0:T(8,128)(2,1)S(1)}, bf16[1024,256]{1,0:T(8,128)(2,1)S(1)}, u32[]{:S(2)}, u32[]{:S(2)}) %collective-permute-start.11) | collective-permute-done | bytes 524320 | tf_op jit(solution)/shard_map/ppermute | solution.py:311
  321.2 3.2 collective-permute-done.8
  324.5 1.1 pad_maximum_fusion.2
  325.5 7.2 %all-to-all-start = ((bf16[16,64,512]{2,1,0:T(8,128)(2,1)}), bf16[16,64,512]{2,1,0:T(8,128)(2,1)S(1)}, u32[]{:S(2)}, u32[]{:S(2)}) async-start(bf16[16,64,512]{2,1,0:T(8,128)(2,1)} %bitcast.43), calls=%async_computation.1 | async-start | bytes 2097152 | tf_op jit(solution)/shard_map/all_to_all | solution.py:316
  332.8 3.8 collective-permute-done.17
  336.6 1.6 fusion.23
  338.2 1.3 collective-permute-done.14
  339.5 1.6 fusion.26
  341.0 1.3 pad_maximum_fusion.1
  342.3 7.1 %all-to-all-done = bf16[16,64,512]{2,1,0:T(8,128)(2,1)S(1)} async-done(((bf16[16,64,512]{2,1,0:T(8,128)(2,1)}), bf16[16,64,512]{2,1,0:T(8,128)(2,1)S(1)}, u32[]{:S(2)}, u32[]{:S(2)}) %all-to-all-start) | async-done | bytes 1048608 | tf_op jit(solution)/shard_map/all_to_all | solution.py:316
  349.4 9.3 %all-to-all-start.1 = ((bf16[16,64,768]{2,1,0:T(8,128)(2,1)}), bf16[16,64,768]{2,1,0:T(8,128)(2,1)}, u32[]{:S(2)}, u32[]{:S(2)}) async-start(bf16[16,64,768]{2,1,0:T(8,128)(2,1)} %bitcast.53), calls=%async_computation.2 | async-start | bytes 3145728 | tf_op jit(solution)/shard_map/all_to_all | solution.py:316
  358.8 1.2 fusion.73.logits_ref
  360.0 1.8 balance.1
  362.7 18.5 %reduce-scatter.2.cloned.1.call-done = bf16[256,2304]{1,0:T(8,128)(2,1)} async-done(((bf16[4096,2304]{1,0:T(8,128)(2,1)}), bf16[256,2304]{1,0:T(8,128)(2,1)}) %reduce-scatter.2.cloned.1.call-update) | async-done | bytes 1179664 | tf_op jit(solution)/shard_map/reduce_scatter | solution.py:301
  381.2 2.0 dynamic-slice_bitcast_fusion.2
  383.3 2.2 collective-permute-start.4
  385.5 1.3 collective-permute-start.3
  387.0 1.6 convert_reduce_fusion
  388.6 4.6 %collective-permute-done.5 = bf16[64,2304]{1,0:T(8,128)(2,1)} collective-permute-done((bf16[64,2304]{1,0:T(8,128)(2,1)}, bf16[64,2304]{1,0:T(8,128)(2,1)}, u32[]{:S(2)}, u32[]{:S(2)}) %collective-permute-start.5) | collective-permute-done | bytes 294944 | tf_op jit(solution)/shard_map/ppermute | solution.py:322
  393.2 5.9 %collective-permute-done.4 = bf16[64,2304]{1,0:T(8,128)(2,1)} collective-permute-done((bf16[64,2304]{1,0:T(8,128)(2,1)}, bf16[64,2304]{1,0:T(8,128)(2,1)}, u32[]{:S(2)}, u32[]{:S(2)}) %collective-permute-start.4) | collective-permute-done | bytes 294944 | tf_op jit(solution)/shard_map/ppermute | solution.py:322
  399.1 1.6 collective-permute-done.3
  400.7 1.4 fusion.69
  404.5 2.6 copy.23
  (86 shorter events, 9.5 us)
Async XLA Ops:
  6.5 7.2 %copy-start = (bf16[24,14336]{1,0:T(8,128)(2,1)S(1)}, bf16[24,14336]{1,0:T(8,128)(2,1)}, u32[]{:S(2)}) copy-start(bf16[24,14336]{1,0:T(8,128)(2,1)} %param.10) | copy-start | bytes 2064388
  6.5 3.1 copy-start.4
  6.5 162.7 %all-gather.2.cloned.1.call-start = ((), (), s32[]{:S(2)}) async-start(), calls=%async_computation.3 | async-start | bytes 30883840 | tf_op jit(solution)/shard_map/all_gather | solution.py:285
  12.3 0.7 copy-start.13
  12.3 0.7 copy-start.11
  12.8 3.0 copy-start.12
  15.9 1.6 copy-start.16
  19.0 362.2 %reduce-scatter.2.cloned.1.call-start = ((), (), s32[]{:S(2)}) async-start(), calls=%async_computation.4 | async-start | bytes 20054016 | tf_op jit(solution)/shard_map/reduce_scatter | solution.py:301
  19.0 6.8 %collective-permute-start = (bf16[512,3584]{1,0:T(8,128)(2,1)}, bf16[512,3584]{1,0:T(8,128)(2,1)}, u32[]{:S(2)}, u32[]{:S(2)}) collective-permute-start(bf16[512,3584]{1,0:T(8,128)(2,1)} %bitcast.198), channel_id=1, source_target_pairs={{0,1},{1,0},{2,3},{3,2},{4,5},{5,4},{6,7},{7,6},{8,9},{9,8},{10,11... | collective-permute-start | bytes 11010056 | tf_op jit(solution)/shard_map/ppermute | solution.py:280
  19.1 175.6 %collective-permute-start.1 = (bf16[3584,512]{1,0:T(8,128)(2,1)}, bf16[3584,512]{1,0:T(8,128)(2,1)}, u32[]{:S(2)}, u32[]{:S(2)}) collective-permute-start(bf16[3584,512]{1,0:T(8,128)(2,1)} %bitcast.208), channel_id=1, source_target_pairs={{0,1},{1,0},{2,3},{3,2},{4,5},{5,4},{6,7},{7,6},{8,9},{9,8},{10,11... | collective-permute-start | bytes 11010056 | tf_op jit(solution)/shard_map/ppermute | solution.py:280
  19.6 191.2 %collective-permute-start.2 = (bf16[3584,512]{1,0:T(8,128)(2,1)}, bf16[3584,512]{1,0:T(8,128)(2,1)}, u32[]{:S(2)}, u32[]{:S(2)}) collective-permute-start(bf16[3584,512]{1,0:T(8,128)(2,1)} %bitcast.209), channel_id=1, source_target_pairs={{0,1},{1,0},{2,3},{3,2},{4,5},{5,4},{6,7},{7,6},{8,9},{9,8},{10,11... | collective-permute-start | bytes 11010056 | tf_op jit(solution)/shard_map/ppermute | solution.py:280
  169.3 19.0 %copy-start.14 = (bf16[1,3584,512]{2,1,0:T(8,128)(2,1)S(1)}, bf16[1,3584,512]{2,1,0:T(8,128)(2,1)}, u32[]{:S(2)}) copy-start(bf16[1,3584,512]{2,1,0:T(8,128)(2,1)} %param.15) | copy-start | bytes 11010052
  194.7 8.6 %copy-start.15 = (bf16[1,3584,512]{2,1,0:T(8,128)(2,1)S(1)}, bf16[1,3584,512]{2,1,0:T(8,128)(2,1)}, u32[]{:S(2)}) copy-start(bf16[1,3584,512]{2,1,0:T(8,128)(2,1)} %param.16) | copy-start | bytes 11010052
  210.8 8.8 %copy-start.8 = (bf16[512,2304]{1,0:T(8,128)(2,1)S(1)}, bf16[512,2304]{1,0:T(8,128)(2,1)}, u32[]{:S(2)}) copy-start(bf16[512,2304]{1,0:T(8,128)(2,1)} %slice.279) | copy-start | bytes 7077892
  219.6 5.3 %copy-start.9 = (bf16[512,2304]{1,0:T(8,128)(2,1)S(1)}, bf16[512,2304]{1,0:T(8,128)(2,1)}, u32[]{:S(2)}) copy-start(bf16[512,2304]{1,0:T(8,128)(2,1)} %slice.280) | copy-start | bytes 7077892
  219.6 5.3 %copy-start.17 = (bf16[1280,512]{1,0:T(8,128)(2,1)S(1)}, bf16[1280,512]{1,0:T(8,128)(2,1)}, u32[]{:S(2)}) copy-start(bf16[1280,512]{1,0:T(8,128)(2,1)} %multiply_convert_fusion.1) | copy-start | bytes 3932164
  238.5 3.8 copy-start.10
  238.5 3.8 copy-start.18
  249.9 59.9 %copy-start.3 = (bf16[4,1024,384]{2,1,0:T(8,128)(2,1)}, bf16[4,1024,384]{2,1,0:T(8,128)(2,1)S(1)}, u32[]{:S(2)}) copy-start(bf16[4,1024,384]{2,1,0:T(8,128)(2,1)S(1)} %get-tuple-element.32) | copy-start | bytes 9437188
  250.0 63.2 %copy-start.2 = (bf16[4,1024,384]{2,1,0:T(8,128)(2,1)}, bf16[4,1024,384]{2,1,0:T(8,128)(2,1)S(1)}, u32[]{:S(2)}) copy-start(bf16[4,1024,384]{2,1,0:T(8,128)(2,1)S(1)} %get-tuple-element.31) | copy-start | bytes 9437188
  250.0 14.9 %collective-permute-start.9 = (bf16[1024,256]{1,0:T(8,128)(2,1)S(1)}, bf16[1024,256]{1,0:T(8,128)(2,1)S(1)}, u32[]{:S(2)}, u32[]{:S(2)}) collective-permute-start(bf16[1024,256]{1,0:T(8,128)(2,1)S(1)} %slice_bitcast_fusion.2), channel_id=1, source_target_pairs={{0,96},{32,0},{64,32},{96,64},{1,97},{33,1},{65,33},{97,65},{2,98}... | collective-permute-start | bytes 1572872 | tf_op jit(solution)/shard_map/ppermute | solution.py:311
  252.0 29.7 %collective-permute-start.15 = (bf16[1024,384]{1,0:T(8,128)(2,1)S(1)}, bf16[1024,384]{1,0:T(8,128)(2,1)S(1)}, u32[]{:S(2)}, u32[]{:S(2)}) collective-permute-start(bf16[1024,384]{1,0:T(8,128)(2,1)S(1)} %slice_bitcast_fusion), channel_id=1, source_target_pairs={{0,96},{32,0},{64,32},{96,64},{1,97},{33,1},{65,33},{97,65},{2,98}... | collective-permute-start | bytes 2359304 | tf_op jit(solution)/shard_map/ppermute | solution.py:311
  253.3 14.9 %collective-permute-start.6 = (bf16[1024,256]{1,0:T(8,128)(2,1)S(1)}, bf16[1024,256]{1,0:T(8,128)(2,1)S(1)}, u32[]{:S(2)}, u32[]{:S(2)}) collective-permute-start(bf16[1024,256]{1,0:T(8,128)(2,1)S(1)} %slice_bitcast_fusion.3), channel_id=1, source_target_pairs={{0,32},{32,64},{64,96},{96,0},{1,33},{33,65},{65,97},{97,1},{2,34}... | collective-permute-start | bytes 1572872 | tf_op jit(solution)/shard_map/ppermute | solution.py:311
  254.3 30.7 %collective-permute-start.12 = (bf16[1024,384]{1,0:T(8,128)(2,1)S(1)}, bf16[1024,384]{1,0:T(8,128)(2,1)S(1)}, u32[]{:S(2)}, u32[]{:S(2)}) collective-permute-start(bf16[1024,384]{1,0:T(8,128)(2,1)S(1)} %slice_bitcast_fusion.1), channel_id=1, source_target_pairs={{0,32},{32,64},{64,96},{96,0},{1,33},{33,65},{65,97},{97,1},{2,34}... | collective-permute-start | bytes 2359304 | tf_op jit(solution)/shard_map/ppermute | solution.py:311
  265.0 28.0 %collective-permute-start.10 = (bf16[1024,256]{1,0:T(8,128)(2,1)S(1)}, bf16[1024,256]{1,0:T(8,128)(2,1)S(1)}, u32[]{:S(2)}, u32[]{:S(2)}) collective-permute-start(bf16[1024,256]{1,0:T(8,128)(2,1)S(1)} %fusion.35), channel_id=1, source_target_pairs={{0,96},{32,0},{64,32},{96,64},{1,97},{33,1},{65,33},{97,65},{2,98}... | collective-permute-start | bytes 1572872 | tf_op jit(solution)/shard_map/ppermute | solution.py:311
  268.3 28.0 %collective-permute-start.7 = (bf16[1024,256]{1,0:T(8,128)(2,1)S(1)}, bf16[1024,256]{1,0:T(8,128)(2,1)S(1)}, u32[]{:S(2)}, u32[]{:S(2)}) collective-permute-start(bf16[1024,256]{1,0:T(8,128)(2,1)S(1)} %fusion.38), channel_id=1, source_target_pairs={{0,32},{32,64},{64,96},{96,0},{1,33},{33,65},{65,97},{97,1},{2,34}... | collective-permute-start | bytes 1572872 | tf_op jit(solution)/shard_map/ppermute | solution.py:311
  281.9 27.9 %collective-permute-start.16 = (bf16[1024,384]{1,0:T(8,128)(2,1)S(1)}, bf16[1024,384]{1,0:T(8,128)(2,1)S(1)}, u32[]{:S(2)}, u32[]{:S(2)}) collective-permute-start(bf16[1024,384]{1,0:T(8,128)(2,1)S(1)} %fusion.25), channel_id=1, source_target_pairs={{0,96},{32,0},{64,32},{96,64},{1,97},{33,1},{65,33},{97,65},{2,98}... | collective-permute-start | bytes 2359304 | tf_op jit(solution)/shard_map/ppermute | solution.py:311
  285.2 27.9 %collective-permute-start.13 = (bf16[1024,384]{1,0:T(8,128)(2,1)S(1)}, bf16[1024,384]{1,0:T(8,128)(2,1)S(1)}, u32[]{:S(2)}, u32[]{:S(2)}) collective-permute-start(bf16[1024,384]{1,0:T(8,128)(2,1)S(1)} %fusion.28), channel_id=1, source_target_pairs={{0,32},{32,64},{64,96},{96,0},{1,33},{33,65},{65,97},{97,1},{2,34}... | collective-permute-start | bytes 2359304 | tf_op jit(solution)/shard_map/ppermute | solution.py:311
  293.1 28.0 %collective-permute-start.11 = (bf16[1024,256]{1,0:T(8,128)(2,1)S(1)}, bf16[1024,256]{1,0:T(8,128)(2,1)S(1)}, u32[]{:S(2)}, u32[]{:S(2)}) collective-permute-start(bf16[1024,256]{1,0:T(8,128)(2,1)S(1)} %fusion.34), channel_id=1, source_target_pairs={{0,96},{32,0},{64,32},{96,64},{1,97},{33,1},{65,33},{97,65},{2,98}... | collective-permute-start | bytes 1572872 | tf_op jit(solution)/shard_map/ppermute | solution.py:311
  296.4 28.0 %collective-permute-start.8 = (bf16[1024,256]{1,0:T(8,128)(2,1)S(1)}, bf16[1024,256]{1,0:T(8,128)(2,1)S(1)}, u32[]{:S(2)}, u32[]{:S(2)}) collective-permute-start(bf16[1024,256]{1,0:T(8,128)(2,1)S(1)} %fusion.37), channel_id=1, source_target_pairs={{0,32},{32,64},{64,96},{96,0},{1,33},{33,65},{65,97},{97,1},{2,34}... | collective-permute-start | bytes 1572872 | tf_op jit(solution)/shard_map/ppermute | solution.py:311
  310.0 26.6 %collective-permute-start.17 = (bf16[1024,384]{1,0:T(8,128)(2,1)S(1)}, bf16[1024,384]{1,0:T(8,128)(2,1)S(1)}, u32[]{:S(2)}, u32[]{:S(2)}) collective-permute-start(bf16[1024,384]{1,0:T(8,128)(2,1)S(1)} %fusion.24), channel_id=1, source_target_pairs={{0,96},{32,0},{64,32},{96,64},{1,97},{33,1},{65,33},{97,65},{2,98}... | collective-permute-start | bytes 2359304 | tf_op jit(solution)/shard_map/ppermute | solution.py:311
  314.2 25.3 %collective-permute-start.14 = (bf16[1024,384]{1,0:T(8,128)(2,1)}, bf16[1024,384]{1,0:T(8,128)(2,1)}, u32[]{:S(2)}, u32[]{:S(2)}) collective-permute-start(bf16[1024,384]{1,0:T(8,128)(2,1)} %fusion.27), channel_id=1, source_target_pairs={{0,32},{32,64},{64,96},{96,0},{1,33},{33,65},{65,97},{97,1},{2,34}... | collective-permute-start | bytes 2359304 | tf_op jit(solution)/shard_map/ppermute | solution.py:311
  325.5 23.9 %all-to-all-start = ((bf16[16,64,512]{2,1,0:T(8,128)(2,1)}), bf16[16,64,512]{2,1,0:T(8,128)(2,1)S(1)}, u32[]{:S(2)}, u32[]{:S(2)}) async-start(bf16[16,64,512]{2,1,0:T(8,128)(2,1)} %bitcast.43), calls=%async_computation.1 | async-start | bytes 2097152 | tf_op jit(solution)/shard_map/all_to_all | solution.py:316
  349.4 37.6 %all-to-all-start.1 = ((bf16[16,64,768]{2,1,0:T(8,128)(2,1)}), bf16[16,64,768]{2,1,0:T(8,128)(2,1)}, u32[]{:S(2)}, u32[]{:S(2)}) async-start(bf16[16,64,768]{2,1,0:T(8,128)(2,1)} %bitcast.53), calls=%async_computation.2 | async-start | bytes 3145728 | tf_op jit(solution)/shard_map/all_to_all | solution.py:316
  383.2 18.9 %copy-start.5 = (bf16[64,1,3584]{2,0,1:T(8,128)(2,1)S(1)}, bf16[64,1,3584]{2,0,1:T(8,128)(2,1)}, u32[]{:S(2)}) copy-start(bf16[64,1,3584]{2,0,1:T(8,128)(2,1)} %get-tuple-element.37) | copy-start | bytes 1376260
  383.2 18.9 %copy-start.6 = (bf16[64,1,3584]{2,0,1:T(8,128)(2,1)S(1)}, bf16[64,1,3584]{2,0,1:T(8,128)(2,1)}, u32[]{:S(2)}) copy-start(bf16[64,1,3584]{2,0,1:T(8,128)(2,1)} %get-tuple-element.38) | copy-start | bytes 1376260
  383.2 18.9 %copy-start.7 = (bf16[64,1,3584]{2,0,1:T(8,128)(2,1)S(1)}, bf16[64,1,3584]{2,0,1:T(8,128)(2,1)}, u32[]{:S(2)}) copy-start(bf16[64,1,3584]{2,0,1:T(8,128)(2,1)} %get-tuple-element.39) | copy-start | bytes 1376260
  383.2 10.0 %collective-permute-start.5 = (bf16[64,2304]{1,0:T(8,128)(2,1)}, bf16[64,2304]{1,0:T(8,128)(2,1)}, u32[]{:S(2)}, u32[]{:S(2)}) collective-permute-start(bf16[64,2304]{1,0:T(8,128)(2,1)} %get-tuple-element.45), channel_id=1, source_target_pairs={{0,96},{32,0},{64,32},{96,64},{1,97},{33,1},{65,33},{97,65},{2,98}... | collective-permute-start | bytes 884744 | tf_op jit(solution)/shard_map/ppermute | solution.py:322
  383.3 15.9 %collective-permute-start.4 = (bf16[64,2304]{1,0:T(8,128)(2,1)}, bf16[64,2304]{1,0:T(8,128)(2,1)}, u32[]{:S(2)}, u32[]{:S(2)}) collective-permute-start(bf16[64,2304]{1,0:T(8,128)(2,1)} %get-tuple-element.46), channel_id=1, source_target_pairs={{0,64},{32,96},{64,0},{96,32},{1,65},{33,97},{65,1},{97,33},{2,66}... | collective-permute-start | bytes 884744 | tf_op jit(solution)/shard_map/ppermute | solution.py:322
  385.5 15.2 %collective-permute-start.3 = (bf16[64,2304]{1,0:T(8,128)(2,1)S(1)}, bf16[64,2304]{1,0:T(8,128)(2,1)}, u32[]{:S(2)}, u32[]{:S(2)}) collective-permute-start(bf16[64,2304]{1,0:T(8,128)(2,1)S(1)} %get-tuple-element.44), channel_id=1, source_target_pairs={{0,32},{32,64},{64,96},{96,0},{1,33},{33,65},{65,97},{97,1},{2,34}... | collective-permute-start | bytes 884744 | tf_op jit(solution)/shard_map/ppermute | solution.py:322
  404.2 2.9 copy-start.1
Sparse Core Ops, SparseCore 0:
  19.1 150.1 all-gather.1
  238.6 142.5 reduce-scatter.1

commit v7 on v6

--- a/solution.py
+++ b/solution.py
@@ -106,7 +106,7 @@
     return jnp.where(inner // CAP == token // TOK, lax.rem(inner, CAP) + 1, -1)
 
 
-def pick_kernel(ids, x_ref, rows_ref, gate_ref, st_ref, upto_ref, want_ref, wanted_ref):
+def pick_kernel(ids, x0_ref, x1_ref, rows_ref, gate_ref, st_ref, upto_ref, want_ref, wanted_ref):
     width = rows_ref.shape[-1]
     tile = min(512, width)
     across = (((1,), (1,)), ((), ()))
@@ -126,12 +126,9 @@
 
     high, low = slot_tables(ids)
     table = high.astype(jnp.float32).astype(jnp.bfloat16)
-
-    @pl.loop(0, x_ref.shape[0] // GROUP)
-    def _(g):
-        tokens = pl.ds(pl.multiple_of(g * GROUP, GROUP), GROUP)
-        mine = pl.ds(pl.multiple_of(g * SLOTS, 16), SLOTS)
-        gates = x_ref[tokens, width : width + GATE_LANES]
+    for g, x_ref in enumerate((x0_ref, x1_ref)):
+        mine = slice(g * SLOTS, (g + 1) * SLOTS)
+        gates = x_ref[:, width : width + GATE_LANES]
         hit = (gates.astype(jnp.float32) != 0.0).astype(jnp.float32)
         count = jnp.dot(
             upto_ref[...], hit.astype(jnp.bfloat16), preferred_element_type=jnp.float32
@@ -144,7 +141,7 @@
         st_ref[g] = put.astype(jnp.bfloat16)
         for n in range(width // tile):
             cols = slice(n * tile, (n + 1) * tile)
-            rows = jnp.dot(pick, x_ref[tokens, cols], preferred_element_type=jnp.float32)
+            rows = jnp.dot(pick, x_ref[:, cols], preferred_element_type=jnp.float32)
             rows = rows.astype(jnp.bfloat16)
             rows_ref[0, mine, cols] = rows[:SLOTS]
             rows_ref[1, mine, cols] = rows[SLOTS:]
@@ -167,7 +164,10 @@
         grid_spec=pltpu.PrefetchScalarGridSpec(
             num_scalar_prefetch=1,
             grid=(groups // step,),
-            in_specs=[pl.BlockSpec((step * GROUP, width + GATE_LANES), lambda g, ids: (g, 0))],
+            in_specs=[
+                pl.BlockSpec((GROUP, width + GATE_LANES), lambda g, ids: (2 * g, 0)),
+                pl.BlockSpec((GROUP, width + GATE_LANES), lambda g, ids: (2 * g + 1, 0)),
+            ],
             out_specs=(
                 pl.BlockSpec((2, step * SLOTS, width), lambda g, ids: (0, g, 0)),
                 pl.BlockSpec((2, step * SLOTS, GATE_LANES), lambda g, ids: (0, g, 0)),
@@ -188,7 +188,7 @@
             transcendentals=0,
         ),
         name="pick",
-    )(ids, gathered)
+    )(ids, gathered, gathered)
 
 
 def put_kernel(widths, plane, st_ref, y0_ref, y1_ref, *outs):
@@ -227,7 +227,7 @@
     else:
         out_shape = jax.ShapeDtypeStruct((RING * RING, RING, TOK, columns), jnp.bfloat16)
         out_specs = pl.BlockSpec(
-            (RING * RING, 1, TOK, columns), lambda z, plane: (0, z, 0, 0)
+            (RING * RING, 1, TOK, columns), lambda z, plane: (0, (z + RING - plane[0]) & 3, 0, 0)
         )
     rows = pl.BlockSpec((RING * SLOTS, columns), lambda z, plane: (z, 0))
     return pl.pallas_call(
@@ -315,11 +315,10 @@
         shares = shares.reshape(RING * RING, TOK, cut)
         shares = lax.all_to_all(shares, ("y", "x"), split_axis=0, concat_axis=0, tiled=True)
         early_out.append(jnp.sum(shares.astype(jnp.float32), axis=0))
-    late_out = lax.dynamic_index_in_dim(summed, plane, 0, keepdims=False).astype(jnp.float32)
+    late_out = summed[0].astype(jnp.float32)
     for shift in range(1, RING):
-        away = lax.dynamic_index_in_dim(summed, (plane + shift) % RING, 0, keepdims=False)
         ring = [(i, (i + shift) % RING) for i in range(RING)]
-        late_out = late_out + lax.ppermute(away, "z", ring).astype(jnp.float32)
+        late_out = late_out + lax.ppermute(summed[shift], "z", ring).astype(jnp.float32)
     moe_out = jnp.concatenate([late_out] + early_out, axis=1)
     return mix_output(streams, mixing, post, moe_out)
 

time: 417 us -> 417 us (level); the launches traced: 414 us -> 409 us
  transfers between devices with their start and end apart: 22 -> 22, of which waited for: 19 -> 13; matrix products, arithmetic and copies ran while one was open for 13% -> 13% of each run, Pallas kernels for 6% -> 6%
where the time goes in v7:
time: 417 us; the launch traced here: 409 us
  waiting for transfers between devices  237 us (57%)
  matrix products  43.7 us (10%)
  Pallas kernels  35.4 us (8%)
  starting transfers between devices  34.2 us (8%)
  local copies, waits for them, and re-layouts  22.3 us (5%)
  other arithmetic  22.1 us (5%)
  between operations  14.1 us (3%)
    all_gather x1, waiting for transfers between devices, body(): gathered = lax.all_gather(packed, ('z', 'y', 'x'), axis=0, tiled=True)  138 us
    ppermute x12, waiting for transfers between devices, body(): lax.ppermute(travel[part], 'z', ring)  61.7 us
    reduce_scatter x1, waiting for transfers between devices, body(): lax.psum_scatter(dense.reshape(-1, late), ('y', 'x'), scatter_dimension=0...  20.1 us
    pallas_call x1, Pallas kernels, pick_call(): pl.pallas_call(pick_kernel, out_shape=(jax.ShapeDtypeStruct((2, groups *...  17.9 us
    all_to_all x2, starting transfers between devices, body(): lax.all_to_all(shares, ('y', 'x'), split_axis=0, concat_axis=0, tiled=True)  16.7 us
    pallas_call x2, Pallas kernels, put_call(): pl.pallas_call(functools.partial(put_kernel, widths), out_shape=out_shape...  15.7 us
    dot_general x2, matrix products, run_hidden(): gate_part = jnp.dot(rows, w_gate, preferred_element_type=jnp.float32)  15.1 us
    dot_general x2, matrix products, run_hidden(): up_part = jnp.dot(rows, w_up, preferred_element_type=jnp.float32)  15 us
  transfers between devices with their start and end apart: 22, of which 13 were waited for; matrix products, arithmetic and copies ran while one was open for 13% of the time, Pallas kernels for 6%

profile of v7, /device:TPU:44, one launch (start us, length us, event | category | flops | bytes accessed | tf_op | source)
XLA Modules:
  0.0 408.8 jit_solution(4098849381422868082)
XLA Ops:
  6.5 3.1 multiply_reduce_fusion
  9.7 2.7 fusion.84
  12.5 0.6 fusion.86
  13.2 0.5 copy.29
  13.7 0.7 fusion.21
  14.3 1.3 fusion.81
  15.7 1.6 fusion.63
  17.8 0.9 concatenate.49
  18.8 0.5 collective-permute-start.1
  19.3 0.5 collective-permute-start.2
  19.9 2.5 slice.301
  22.4 3.3 slice.299
  25.7 2.5 slice.302
  28.2 3.2 slice.300
  31.4 137.6 %all-gather.2.cloned.1.call-done.x0_ref.x1_ref = bf16[4096,3712]{1,0:T(8,128)(2,1)} async-done(((bf16[64,3712]{1,0:T(8,128)(2,1)}), bf16[4096,3712]{1,0:T(8,128)(2,1)}) %all-gather.2.cloned.1.call-update) | async-done | bytes 30408720 | tf_op jit(solution)/shard_map/all_gather | solution.py:285
  169.0 17.9 %pick.1 = (bf16[2,1280,3584]{2,1,0:T(8,128)(2,1)S(1)}, f32[2,1280,128]{2,1,0:T(8,128)S(1)}, bf16[16,256,160]{2,1,0:T(8,128)(2,1)S(1)}) custom-call(s32[2]{0:T(128)S(1)} %pad_add_fusion.ids, bf16[4096,3712]{1,0:T(8,128)(2,1)} %all-gather.2.cloned.1.call-done.x0_ref.x1_ref, bf16[4096,3712]{1,0:T(8,128)(2,1)} %all-gather.2.cloned.1.call-done.x0_ref.x1_ref), custom_call_target="tpu_custom_call" | custom-call | flops 4697620480 | bytes 58720256 | tf_op jit(solution)/shard_map/pick/pallas_call | solution.py:157
  187.3 6.5 %fusion.6 = f32[1280,512]{1,0:T(8,128)} fusion(bf16[2,1280,3584]{2,1,0:T(8,128)(2,1)S(1)} %get-tuple-element.21, bf16[1,3584,512]{2,1,0:T(8,128)(2,1)S(1)} %copy-done.14), kind=kOutput, calls=%fused_computation.8 | convolution fusion | flops 4697620480 | bytes 15466496 | tf_op jit(solution)/shard_map/dot_general | solution.py:258
  193.7 8.6 %fusion.2 = f32[1280,512]{1,0:T(8,128)} fusion(bf16[3584,512]{1,0:T(8,128)(2,1)} %collective-permute-done.1, bf16[2,1280,3584]{2,1,0:T(8,128)(2,1)S(1)} %get-tuple-element.21), kind=kOutput, calls=%fused_computation.4 | convolution fusion | flops 4697620480 | bytes 15466496 | tf_op jit(solution)/shard_map/dot_general | solution.py:258
  202.3 6.7 %fusion.18 = bf16[1280,512]{1,0:T(8,128)(2,1)S(1)} fusion(bf16[2,1280,3584]{2,1,0:T(8,128)(2,1)S(1)} %get-tuple-element.21, f32[1280,512]{1,0:T(8,128)} %fusion.6, f32[1280]{0:T(1024)S(1)} %get-tuple-element.34, bf16[1,3584,512]{2,1,0:T(8,128)(2,1)S(1)} %copy-done.15), kind=kOutput, calls=%fused_computation.21 | convolution fusion | flops 4702208000 | bytes 16785408 | tf_op jit(solution)/shard_map/dot_general | solution.py:259
  209.1 8.3 %multiply_convert_fusion.1 = bf16[1280,512]{1,0:T(8,128)(2,1)S(1)} fusion(f32[1280,512]{1,0:T(8,128)} %fusion.2, f32[1280]{0:T(1024)S(1)} %get-tuple-element.33, bf16[3584,512]{1,0:T(8,128)(2,1)} %collective-permute-done.2, bf16[2,1280,3584]{2,1,0:T(8,128)(2,1)S(1)} %get-tuple-element.21), kind=kOutput, calls=%fused_computation.22 | convolution fusion | flops 4702208000 | bytes 16785408 | tf_op jit(solution)/shard_map/dot_general | solution.py:259
  217.4 3.4 convolution_convert_fusion.y1_ref
  220.9 3.6 convolution_convert_fusion.1.y0_ref
  224.5 9.9 %put.1 = bf16[16,4,64,2304]{3,2,1,0:T(8,128)(2,1)} custom-call(s32[1]{0:T(128)} %bitcast.11.plane, bf16[16,256,160]{2,1,0:T(8,128)(2,1)S(1)} %get-tuple-element.20.st_ref, bf16[1280,2304]{1,0:T(8,128)(2,1)S(1)} %convolution_convert_fusion.1.y0_ref, bf16[1280,2304]{1,0:T(8,128)(2,1)S(1)} %convolution_convert_fusion.y1_ref), custom_call_target="tpu_custom_call" | custom-call | flops 3019898880 | bytes 28311552 | tf_op jit(solution)/shard_map/put/pallas_call | solution.py:233
  234.4 3.7 convolution_convert_fusion.3.y0_ref
  238.2 1.9 convolution_convert_fusion.2.y1_ref
  240.0 5.8 %put_halves.1 = (bf16[4,1024,256]{2,1,0:T(8,128)(2,1)S(1)}, bf16[4,1024,256]{2,1,0:T(8,128)(2,1)S(1)}, bf16[4,1024,384]{2,1,0:T(8,128)(2,1)S(1)}, bf16[4,1024,384]{2,1,0:T(8,128)(2,1)S(1)}) custom-call(s32[1]{0:T(128)} %bitcast.11.plane, bf16[16,256,160]{2,1,0:T(8,128)(2,1)S(1)} %get-tuple-element.20.st_ref, ...), custom_call_target="tpu_custom_call" | custom-call | flops 1677721600 | bytes 15728640 | tf_op jit(solution)/shard_map/put_halves/pallas_call | solution.py:233
  245.9 2.0 collective-permute-start.9
  248.2 2.0 collective-permute-start.15
  250.5 10.3 %collective-permute-done.9 = bf16[1024,256]{1,0:T(8,128)(2,1)S(1)} collective-permute-done((bf16[1024,256]{1,0:T(8,128)(2,1)S(1)}, bf16[1024,256]{1,0:T(8,128)(2,1)S(1)}, u32[]{:S(2)}, u32[]{:S(2)}) %collective-permute-start.9) | collective-permute-done | bytes 524320 | tf_op jit(solution)/shard_map/ppermute | solution.py:311
  260.9 2.0 collective-permute-start.10
  263.2 14.4 %collective-permute-done.15 = bf16[1024,384]{1,0:T(8,128)(2,1)S(1)} collective-permute-done((bf16[1024,384]{1,0:T(8,128)(2,1)S(1)}, bf16[1024,384]{1,0:T(8,128)(2,1)S(1)}, u32[]{:S(2)}, u32[]{:S(2)}) %collective-permute-start.15) | collective-permute-done | bytes 786464 | tf_op jit(solution)/shard_map/ppermute | solution.py:311
  277.9 2.0 collective-permute-start.16
  280.2 8.7 %collective-permute-done.10 = bf16[1024,256]{1,0:T(8,128)(2,1)S(1)} collective-permute-done((bf16[1024,256]{1,0:T(8,128)(2,1)S(1)}, bf16[1024,256]{1,0:T(8,128)(2,1)S(1)}, u32[]{:S(2)}, u32[]{:S(2)}) %collective-permute-start.10) | collective-permute-done | bytes 524320 | tf_op jit(solution)/shard_map/ppermute | solution.py:311
  289.0 2.0 collective-permute-start.11
  291.3 14.4 %collective-permute-done.16 = bf16[1024,384]{1,0:T(8,128)(2,1)S(1)} collective-permute-done((bf16[1024,384]{1,0:T(8,128)(2,1)S(1)}, bf16[1024,384]{1,0:T(8,128)(2,1)S(1)}, u32[]{:S(2)}, u32[]{:S(2)}) %collective-permute-start.16) | collective-permute-done | bytes 786464 | tf_op jit(solution)/shard_map/ppermute | solution.py:311
  305.7 1.1 fusion.24
  306.8 1.9 collective-permute-start.17
  308.7 1.1 fusion.27
  310.0 7.0 %collective-permute-done.11 = bf16[1024,256]{1,0:T(8,128)(2,1)S(1)} collective-permute-done((bf16[1024,256]{1,0:T(8,128)(2,1)S(1)}, bf16[1024,256]{1,0:T(8,128)(2,1)S(1)}, u32[]{:S(2)}, u32[]{:S(2)}) %collective-permute-start.11) | collective-permute-done | bytes 524320 | tf_op jit(solution)/shard_map/ppermute | solution.py:311
  317.1 1.9 collective-permute-done.8
  319.1 1.1 pad_maximum_fusion.2
  320.2 7.5 %all-to-all-start = ((bf16[16,64,512]{2,1,0:T(8,128)(2,1)}), bf16[16,64,512]{2,1,0:T(8,128)(2,1)S(1)}, u32[]{:S(2)}, u32[]{:S(2)}) async-start(bf16[16,64,512]{2,1,0:T(8,128)(2,1)} %bitcast.38), calls=%async_computation.1 | async-start | bytes 2097152 | tf_op jit(solution)/shard_map/all_to_all | solution.py:316
  327.8 4.8 %collective-permute-done.17 = bf16[1024,384]{1,0:T(8,128)(2,1)S(1)} collective-permute-done((bf16[1024,384]{1,0:T(8,128)(2,1)}, bf16[1024,384]{1,0:T(8,128)(2,1)S(1)}, u32[]{:S(2)}, u32[]{:S(2)}) %collective-permute-start.17) | collective-permute-done | bytes 786464 | tf_op jit(solution)/shard_map/ppermute | solution.py:311
  332.5 1.6 fusion.23
  334.3 1.6 fusion.26
  335.9 1.3 pad_maximum_fusion.1
  337.2 6.1 %all-to-all-done = bf16[16,64,512]{2,1,0:T(8,128)(2,1)S(1)} async-done(((bf16[16,64,512]{2,1,0:T(8,128)(2,1)}), bf16[16,64,512]{2,1,0:T(8,128)(2,1)S(1)}, u32[]{:S(2)}, u32[]{:S(2)}) %all-to-all-start) | async-done | bytes 1048608 | tf_op jit(solution)/shard_map/all_to_all | solution.py:316
  343.2 9.2 %all-to-all-start.1 = ((bf16[16,64,768]{2,1,0:T(8,128)(2,1)}), bf16[16,64,768]{2,1,0:T(8,128)(2,1)}, u32[]{:S(2)}, u32[]{:S(2)}) async-start(bf16[16,64,768]{2,1,0:T(8,128)(2,1)} %bitcast.48), calls=%async_computation.2 | async-start | bytes 3145728 | tf_op jit(solution)/shard_map/all_to_all | solution.py:316
  352.4 1.3 fusion.70.logits_ref
  353.7 1.8 balance.1
  355.5 0.9 slice_bitcast_fusion.19
  356.4 20.1 %reduce-scatter.2.cloned.1.call-done = bf16[256,2304]{1,0:T(8,128)(2,1)} async-done(((bf16[4096,2304]{1,0:T(8,128)(2,1)}), bf16[256,2304]{1,0:T(8,128)(2,1)}) %reduce-scatter.2.cloned.1.call-update) | async-done | bytes 1179664 | tf_op jit(solution)/shard_map/reduce_scatter | solution.py:301
  376.4 2.1 fusion.85
  378.9 1.7 collective-permute-start.5
  380.7 1.4 collective-permute-start.4
  382.2 1.6 convert_reduce_fusion
  383.9 4.9 %collective-permute-done.3 = bf16[64,2304]{1,0:T(8,128)(2,1)S(1)} collective-permute-done((bf16[64,2304]{1,0:T(8,128)(2,1)}, bf16[64,2304]{1,0:T(8,128)(2,1)S(1)}, u32[]{:S(2)}, u32[]{:S(2)}) %collective-permute-start.3) | collective-permute-done | bytes 294944 | tf_op jit(solution)/shard_map/ppermute | solution.py:321
  388.7 6.7 %collective-permute-done.4 = bf16[64,2304]{1,0:T(8,128)(2,1)} collective-permute-done((bf16[64,2304]{1,0:T(8,128)(2,1)}, bf16[64,2304]{1,0:T(8,128)(2,1)}, u32[]{:S(2)}, u32[]{:S(2)}) %collective-permute-start.4) | collective-permute-done | bytes 294944 | tf_op jit(solution)/shard_map/ppermute | solution.py:321
  395.4 1.3 add_bitcast_fusion
  396.7 0.5 fusion.48
  397.3 0.5 fusion.53
  397.8 0.5 fusion.58
  398.3 0.5 fusion.43
  399.1 2.6 copy.23
  (88 shorter events, 5.0 us)
Async XLA Ops:
  6.5 7.1 %copy-start = (bf16[24,14336]{1,0:T(8,128)(2,1)S(1)}, bf16[24,14336]{1,0:T(8,128)(2,1)}, u32[]{:S(2)}) copy-start(bf16[24,14336]{1,0:T(8,128)(2,1)} %param.10) | copy-start | bytes 2064388
  6.5 3.1 copy-start.4
  6.5 162.4 %all-gather.2.cloned.1.call-start = ((), (), s32[]{:S(2)}) async-start(), calls=%async_computation.3 | async-start | bytes 30883840 | tf_op jit(solution)/shard_map/all_gather | solution.py:285
  9.6 2.7 copy-start.13
  9.7 2.8 copy-start.11
  9.7 3.4 copy-start.12
  15.7 1.7 copy-start.16
  18.7 357.7 %reduce-scatter.2.cloned.1.call-start = ((), (), s32[]{:S(2)}) async-start(), calls=%async_computation.4 | async-start | bytes 20054016 | tf_op jit(solution)/shard_map/reduce_scatter | solution.py:301
  18.7 7.0 %collective-permute-start = (bf16[512,3584]{1,0:T(8,128)(2,1)}, bf16[512,3584]{1,0:T(8,128)(2,1)}, u32[]{:S(2)}, u32[]{:S(2)}) collective-permute-start(bf16[512,3584]{1,0:T(8,128)(2,1)} %bitcast.188), channel_id=1, source_target_pairs={{0,1},{1,0},{2,3},{3,2},{4,5},{5,4},{6,7},{7,6},{8,9},{9,8},{10,11... | collective-permute-start | bytes 11010056 | tf_op jit(solution)/shard_map/ppermute | solution.py:280
  18.8 174.9 %collective-permute-start.1 = (bf16[3584,512]{1,0:T(8,128)(2,1)}, bf16[3584,512]{1,0:T(8,128)(2,1)}, u32[]{:S(2)}, u32[]{:S(2)}) collective-permute-start(bf16[3584,512]{1,0:T(8,128)(2,1)} %bitcast.196), channel_id=1, source_target_pairs={{0,1},{1,0},{2,3},{3,2},{4,5},{5,4},{6,7},{7,6},{8,9},{9,8},{10,11... | collective-permute-start | bytes 11010056 | tf_op jit(solution)/shard_map/ppermute | solution.py:280
  19.3 189.7 %collective-permute-start.2 = (bf16[3584,512]{1,0:T(8,128)(2,1)}, bf16[3584,512]{1,0:T(8,128)(2,1)}, u32[]{:S(2)}, u32[]{:S(2)}) collective-permute-start(bf16[3584,512]{1,0:T(8,128)(2,1)} %bitcast.197), channel_id=1, source_target_pairs={{0,1},{1,0},{2,3},{3,2},{4,5},{5,4},{6,7},{7,6},{8,9},{9,8},{10,11... | collective-permute-start | bytes 11010056 | tf_op jit(solution)/shard_map/ppermute | solution.py:280
  169.0 18.3 %copy-start.14 = (bf16[1,3584,512]{2,1,0:T(8,128)(2,1)S(1)}, bf16[1,3584,512]{2,1,0:T(8,128)(2,1)}, u32[]{:S(2)}) copy-start(bf16[1,3584,512]{2,1,0:T(8,128)(2,1)} %param.15) | copy-start | bytes 11010052
  193.7 8.6 %copy-start.15 = (bf16[1,3584,512]{2,1,0:T(8,128)(2,1)S(1)}, bf16[1,3584,512]{2,1,0:T(8,128)(2,1)}, u32[]{:S(2)}) copy-start(bf16[1,3584,512]{2,1,0:T(8,128)(2,1)} %param.16) | copy-start | bytes 11010052
  209.0 11.8 %copy-start.17 = (bf16[1280,512]{1,0:T(8,128)(2,1)}, bf16[1280,512]{1,0:T(8,128)(2,1)S(1)}, u32[]{:S(2)}) copy-start(bf16[1280,512]{1,0:T(8,128)(2,1)S(1)} %fusion.18) | copy-start | bytes 3932164
  209.1 8.3 %copy-start.9 = (bf16[512,2304]{1,0:T(8,128)(2,1)S(1)}, bf16[512,2304]{1,0:T(8,128)(2,1)}, u32[]{:S(2)}) copy-start(bf16[512,2304]{1,0:T(8,128)(2,1)} %slice.300) | copy-start | bytes 7077892
  217.4 3.5 copy-start.18
  217.4 3.5 copy-start.8
  234.4 3.8 copy-start.10
  234.4 3.8 copy-start.19
  245.9 59.9 %copy-start.3 = (bf16[4,1024,384]{2,1,0:T(8,128)(2,1)}, bf16[4,1024,384]{2,1,0:T(8,128)(2,1)S(1)}, u32[]{:S(2)}) copy-start(bf16[4,1024,384]{2,1,0:T(8,128)(2,1)S(1)} %get-tuple-element.32) | copy-start | bytes 9437188
  245.9 62.9 %copy-start.2 = (bf16[4,1024,384]{2,1,0:T(8,128)(2,1)}, bf16[4,1024,384]{2,1,0:T(8,128)(2,1)S(1)}, u32[]{:S(2)}) copy-start(bf16[4,1024,384]{2,1,0:T(8,128)(2,1)S(1)} %get-tuple-element.31) | copy-start | bytes 9437188
  245.9 14.9 %collective-permute-start.9 = (bf16[1024,256]{1,0:T(8,128)(2,1)S(1)}, bf16[1024,256]{1,0:T(8,128)(2,1)S(1)}, u32[]{:S(2)}, u32[]{:S(2)}) collective-permute-start(bf16[1024,256]{1,0:T(8,128)(2,1)S(1)} %slice_bitcast_fusion.2), channel_id=1, source_target_pairs={{0,96},{32,0},{64,32},{96,64},{1,97},{33,1},{65,33},{97,65},{2,98}... | collective-permute-start | bytes 1572872 | tf_op jit(solution)/shard_map/ppermute | solution.py:311
  247.9 15.0 %collective-permute-start.6 = (bf16[1024,256]{1,0:T(8,128)(2,1)S(1)}, bf16[1024,256]{1,0:T(8,128)(2,1)S(1)}, u32[]{:S(2)}, u32[]{:S(2)}) collective-permute-start(bf16[1024,256]{1,0:T(8,128)(2,1)S(1)} %slice_bitcast_fusion.3), channel_id=1, source_target_pairs={{0,32},{32,64},{64,96},{96,0},{1,33},{33,65},{65,97},{97,1},{2,34}... | collective-permute-start | bytes 1572872 | tf_op jit(solution)/shard_map/ppermute | solution.py:311
  248.2 29.4 %collective-permute-start.15 = (bf16[1024,384]{1,0:T(8,128)(2,1)S(1)}, bf16[1024,384]{1,0:T(8,128)(2,1)S(1)}, u32[]{:S(2)}, u32[]{:S(2)}) collective-permute-start(bf16[1024,384]{1,0:T(8,128)(2,1)S(1)} %slice_bitcast_fusion), channel_id=1, source_target_pairs={{0,96},{32,0},{64,32},{96,64},{1,97},{33,1},{65,33},{97,65},{2,98}... | collective-permute-start | bytes 2359304 | tf_op jit(solution)/shard_map/ppermute | solution.py:311
  250.3 29.6 %collective-permute-start.12 = (bf16[1024,384]{1,0:T(8,128)(2,1)S(1)}, bf16[1024,384]{1,0:T(8,128)(2,1)S(1)}, u32[]{:S(2)}, u32[]{:S(2)}) collective-permute-start(bf16[1024,384]{1,0:T(8,128)(2,1)S(1)} %slice_bitcast_fusion.1), channel_id=1, source_target_pairs={{0,32},{32,64},{64,96},{96,0},{1,33},{33,65},{65,97},{97,1},{2,34}... | collective-permute-start | bytes 2359304 | tf_op jit(solution)/shard_map/ppermute | solution.py:311
  260.9 28.0 %collective-permute-start.10 = (bf16[1024,256]{1,0:T(8,128)(2,1)S(1)}, bf16[1024,256]{1,0:T(8,128)(2,1)S(1)}, u32[]{:S(2)}, u32[]{:S(2)}) collective-permute-start(bf16[1024,256]{1,0:T(8,128)(2,1)S(1)} %fusion.35), channel_id=1, source_target_pairs={{0,96},{32,0},{64,32},{96,64},{1,97},{33,1},{65,33},{97,65},{2,98}... | collective-permute-start | bytes 1572872 | tf_op jit(solution)/shard_map/ppermute | solution.py:311
  263.0 28.0 %collective-permute-start.7 = (bf16[1024,256]{1,0:T(8,128)(2,1)S(1)}, bf16[1024,256]{1,0:T(8,128)(2,1)S(1)}, u32[]{:S(2)}, u32[]{:S(2)}) collective-permute-start(bf16[1024,256]{1,0:T(8,128)(2,1)S(1)} %fusion.38), channel_id=1, source_target_pairs={{0,32},{32,64},{64,96},{96,0},{1,33},{33,65},{65,97},{97,1},{2,34}... | collective-permute-start | bytes 1572872 | tf_op jit(solution)/shard_map/ppermute | solution.py:311
  277.9 27.9 %collective-permute-start.16 = (bf16[1024,384]{1,0:T(8,128)(2,1)S(1)}, bf16[1024,384]{1,0:T(8,128)(2,1)S(1)}, u32[]{:S(2)}, u32[]{:S(2)}) collective-permute-start(bf16[1024,384]{1,0:T(8,128)(2,1)S(1)} %fusion.25), channel_id=1, source_target_pairs={{0,96},{32,0},{64,32},{96,64},{1,97},{33,1},{65,33},{97,65},{2,98}... | collective-permute-start | bytes 2359304 | tf_op jit(solution)/shard_map/ppermute | solution.py:311
  280.0 28.7 %collective-permute-start.13 = (bf16[1024,384]{1,0:T(8,128)(2,1)S(1)}, bf16[1024,384]{1,0:T(8,128)(2,1)S(1)}, u32[]{:S(2)}, u32[]{:S(2)}) collective-permute-start(bf16[1024,384]{1,0:T(8,128)(2,1)S(1)} %fusion.28), channel_id=1, source_target_pairs={{0,32},{32,64},{64,96},{96,0},{1,33},{33,65},{65,97},{97,1},{2,34}... | collective-permute-start | bytes 2359304 | tf_op jit(solution)/shard_map/ppermute | solution.py:311
  289.0 28.0 %collective-permute-start.11 = (bf16[1024,256]{1,0:T(8,128)(2,1)S(1)}, bf16[1024,256]{1,0:T(8,128)(2,1)S(1)}, u32[]{:S(2)}, u32[]{:S(2)}) collective-permute-start(bf16[1024,256]{1,0:T(8,128)(2,1)S(1)} %fusion.34), channel_id=1, source_target_pairs={{0,96},{32,0},{64,32},{96,64},{1,97},{33,1},{65,33},{97,65},{2,98}... | collective-permute-start | bytes 1572872 | tf_op jit(solution)/shard_map/ppermute | solution.py:311
  291.1 27.9 %collective-permute-start.8 = (bf16[1024,256]{1,0:T(8,128)(2,1)S(1)}, bf16[1024,256]{1,0:T(8,128)(2,1)S(1)}, u32[]{:S(2)}, u32[]{:S(2)}) collective-permute-start(bf16[1024,256]{1,0:T(8,128)(2,1)S(1)} %fusion.37), channel_id=1, source_target_pairs={{0,32},{32,64},{64,96},{96,0},{1,33},{33,65},{65,97},{97,1},{2,34}... | collective-permute-start | bytes 1572872 | tf_op jit(solution)/shard_map/ppermute | solution.py:311
  306.8 25.7 %collective-permute-start.17 = (bf16[1024,384]{1,0:T(8,128)(2,1)}, bf16[1024,384]{1,0:T(8,128)(2,1)S(1)}, u32[]{:S(2)}, u32[]{:S(2)}) collective-permute-start(bf16[1024,384]{1,0:T(8,128)(2,1)} %fusion.24), channel_id=1, source_target_pairs={{0,96},{32,0},{64,32},{96,64},{1,97},{33,1},{65,33},{97,65},{2,98}... | collective-permute-start | bytes 2359304 | tf_op jit(solution)/shard_map/ppermute | solution.py:311
  309.8 24.5 %collective-permute-start.14 = (bf16[1024,384]{1,0:T(8,128)(2,1)}, bf16[1024,384]{1,0:T(8,128)(2,1)}, u32[]{:S(2)}, u32[]{:S(2)}) collective-permute-start(bf16[1024,384]{1,0:T(8,128)(2,1)} %fusion.27), channel_id=1, source_target_pairs={{0,32},{32,64},{64,96},{96,0},{1,33},{33,65},{65,97},{97,1},{2,34}... | collective-permute-start | bytes 2359304 | tf_op jit(solution)/shard_map/ppermute | solution.py:311
  320.2 23.1 %all-to-all-start = ((bf16[16,64,512]{2,1,0:T(8,128)(2,1)}), bf16[16,64,512]{2,1,0:T(8,128)(2,1)S(1)}, u32[]{:S(2)}, u32[]{:S(2)}) async-start(bf16[16,64,512]{2,1,0:T(8,128)(2,1)} %bitcast.38), calls=%async_computation.1 | async-start | bytes 2097152 | tf_op jit(solution)/shard_map/all_to_all | solution.py:316
  343.2 39.0 %all-to-all-start.1 = ((bf16[16,64,768]{2,1,0:T(8,128)(2,1)}), bf16[16,64,768]{2,1,0:T(8,128)(2,1)}, u32[]{:S(2)}, u32[]{:S(2)}) async-start(bf16[16,64,768]{2,1,0:T(8,128)(2,1)} %bitcast.48), calls=%async_computation.2 | async-start | bytes 3145728 | tf_op jit(solution)/shard_map/all_to_all | solution.py:316
  378.6 18.1 %copy-start.5 = (bf16[64,1,3584]{2,0,1:T(8,128)(2,1)S(1)}, bf16[64,1,3584]{2,0,1:T(8,128)(2,1)}, u32[]{:S(2)}) copy-start(bf16[64,1,3584]{2,0,1:T(8,128)(2,1)} %get-tuple-element.37) | copy-start | bytes 1376260
  378.6 18.2 %copy-start.6 = (bf16[64,1,3584]{2,0,1:T(8,128)(2,1)S(1)}, bf16[64,1,3584]{2,0,1:T(8,128)(2,1)}, u32[]{:S(2)}) copy-start(bf16[64,1,3584]{2,0,1:T(8,128)(2,1)} %get-tuple-element.38) | copy-start | bytes 1376260
  378.6 18.2 %copy-start.7 = (bf16[64,1,3584]{2,0,1:T(8,128)(2,1)S(1)}, bf16[64,1,3584]{2,0,1:T(8,128)(2,1)}, u32[]{:S(2)}) copy-start(bf16[64,1,3584]{2,0,1:T(8,128)(2,1)} %get-tuple-element.39) | copy-start | bytes 1376260
  378.6 10.2 %collective-permute-start.3 = (bf16[64,2304]{1,0:T(8,128)(2,1)}, bf16[64,2304]{1,0:T(8,128)(2,1)S(1)}, u32[]{:S(2)}, u32[]{:S(2)}) collective-permute-start(bf16[64,2304]{1,0:T(8,128)(2,1)} %get-tuple-element.44), channel_id=1, source_target_pairs={{0,32},{32,64},{64,96},{96,0},{1,33},{33,65},{65,97},{97,1},{2,34}... | collective-permute-start | bytes 884744 | tf_op jit(solution)/shard_map/ppermute | solution.py:321
  378.9 9.8 %collective-permute-start.5 = (bf16[64,2304]{1,0:T(8,128)(2,1)}, bf16[64,2304]{1,0:T(8,128)(2,1)}, u32[]{:S(2)}, u32[]{:S(2)}) collective-permute-start(bf16[64,2304]{1,0:T(8,128)(2,1)} %get-tuple-element.45), channel_id=1, source_target_pairs={{0,96},{32,0},{64,32},{96,64},{1,97},{33,1},{65,33},{97,65},{2,98}... | collective-permute-start | bytes 884744 | tf_op jit(solution)/shard_map/ppermute | solution.py:321
  380.7 14.8 %collective-permute-start.4 = (bf16[64,2304]{1,0:T(8,128)(2,1)}, bf16[64,2304]{1,0:T(8,128)(2,1)}, u32[]{:S(2)}, u32[]{:S(2)}) collective-permute-start(bf16[64,2304]{1,0:T(8,128)(2,1)} %get-tuple-element.46), channel_id=1, source_target_pairs={{0,64},{32,96},{64,0},{96,32},{1,65},{33,97},{65,1},{97,33},{2,66}... | collective-permute-start | bytes 884744 | tf_op jit(solution)/shard_map/ppermute | solution.py:321
  398.8 2.9 copy-start.1
Sparse Core Ops, SparseCore 0:
  18.8 150.1 all-gather.1
  234.5 141.8 reduce-scatter.1

commit v8 on v6

--- a/solution.py
+++ b/solution.py
@@ -15,7 +15,7 @@
 SLOTS = GROUP // TOK * CAP
 GATE_LANES = 128
 RING = 4
-CHUNKS = (512, 768)
+CHUNKS = (1280,)
 
 
 def balance_kernel(logits_ref, out_ref):
@@ -227,7 +227,7 @@
     else:
         out_shape = jax.ShapeDtypeStruct((RING * RING, RING, TOK, columns), jnp.bfloat16)
         out_specs = pl.BlockSpec(
-            (RING * RING, 1, TOK, columns), lambda z, plane: (0, z, 0, 0)
+            (RING * RING, 1, TOK, columns), lambda z, plane: (0, (z + RING - plane[0]) & 3, 0, 0)
         )
     rows = pl.BlockSpec((RING * SLOTS, columns), lambda z, plane: (z, 0))
     return pl.pallas_call(
@@ -315,11 +315,10 @@
         shares = shares.reshape(RING * RING, TOK, cut)
         shares = lax.all_to_all(shares, ("y", "x"), split_axis=0, concat_axis=0, tiled=True)
         early_out.append(jnp.sum(shares.astype(jnp.float32), axis=0))
-    late_out = lax.dynamic_index_in_dim(summed, plane, 0, keepdims=False).astype(jnp.float32)
+    late_out = summed[0].astype(jnp.float32)
     for shift in range(1, RING):
-        away = lax.dynamic_index_in_dim(summed, (plane + shift) % RING, 0, keepdims=False)
         ring = [(i, (i + shift) % RING) for i in range(RING)]
-        late_out = late_out + lax.ppermute(away, "z", ring).astype(jnp.float32)
+        late_out = late_out + lax.ppermute(summed[shift], "z", ring).astype(jnp.float32)
     moe_out = jnp.concatenate([late_out] + early_out, axis=1)
     return mix_output(streams, mixing, post, moe_out)
 

time: 417 us -> 419 us (level)
  waiting for transfers between devices: 237 us -> 263 us
  starting transfers between devices: 36.8 us -> 19 us
    ppermute x12 -> x6, waiting for transfers between devices: 61 us -> 85 us  [body(): lax.ppermute(travel[part], 'z', ring)]
    reduce_scatter x1, waiting for transfers between devices: 18.5 us -> 28.3 us  [body(): lax.psum_scatter(dense.reshape(-1, late), ('y', 'x'), scatter_dimension=0...]
    ppermute x12 -> x6, starting transfers between devices: 15.8 us -> 6.35 us  [body(): lax.ppermute(travel[part], 'z', ring)]
    all_to_all x2 -> x1, starting transfers between devices: 16.6 us -> 7.33 us  [body(): lax.all_to_all(shares, ('y', 'x'), split_axis=0, concat_axis=0, tiled=True)]
    all_to_all x2 -> x1, waiting for transfers between devices: 7.13 us -> 0.01 us  [body(): lax.all_to_all(shares, ('y', 'x'), split_axis=0, concat_axis=0, tiled=True)]
  transfers between devices with their start and end apart: 22 -> 15, of which waited for: 19 -> 10; matrix products, arithmetic and copies ran while one was open for 13% -> 12% of each run, Pallas kernels for 6% -> 6%
where the time goes in v8:
time: 419 us; the launch traced here: 415 us
  waiting for transfers between devices  263 us (63%)
  matrix products  43.5 us (10%)
  Pallas kernels  36.6 us (9%)
  local copies, waits for them, and re-layouts  22.3 us (5%)
  starting transfers between devices  19 us (5%)
  other arithmetic  17.3 us (4%)
  between operations  13.9 us (3%)
    all_gather x1, waiting for transfers between devices, body(): gathered = lax.all_gather(packed, ('z', 'y', 'x'), axis=0, tiled=True)  138 us
    ppermute x6, waiting for transfers between devices, body(): lax.ppermute(travel[part], 'z', ring)  85 us
    reduce_scatter x1, waiting for transfers between devices, body(): lax.psum_scatter(dense.reshape(-1, late), ('y', 'x'), scatter_dimension=0...  28.3 us
    pallas_call x1, Pallas kernels, pick_call(): pl.pallas_call(pick_kernel, out_shape=(jax.ShapeDtypeStruct((2, groups *...  18.8 us
    pallas_call x2, Pallas kernels, put_call(): pl.pallas_call(functools.partial(put_kernel, widths), out_shape=out_shape...  16 us
    dot_general x2, matrix products, run_hidden(): gate_part = jnp.dot(rows, w_gate, preferred_element_type=jnp.float32)  15.1 us
    dot_general x2, matrix products, run_hidden(): up_part = jnp.dot(rows, w_up, preferred_element_type=jnp.float32)  15 us
    dot_general x4, matrix products, run_down(): jnp.dot(h, w, preferred_element_type=jnp.float32).astype(jnp.bfloat16)  12.4 us
  transfers between devices with their start and end apart: 15, of which 10 were waited for; matrix products, arithmetic and copies ran while one was open for 12% of the time, Pallas kernels for 6%

profile of v8, /device:TPU:44, one launch (start us, length us, event | category | flops | bytes accessed | tf_op | source)
XLA Modules:
  0.0 415.4 jit_solution(5906857483048814815)
XLA Ops:
  6.5 3.1 multiply_reduce_fusion
  9.7 2.7 fusion.78
  12.5 0.7 fusion.80
  13.2 0.5 copy.29
  13.7 0.7 fusion.27
  14.4 1.4 fusion.75
  15.8 1.8 fusion.57
  17.6 0.4 fusion.82
  18.1 0.9 concatenate.44
  19.1 0.5 collective-permute-start.1
  19.6 0.1 collective-permute-start.2
  19.7 2.5 slice.269
  22.2 3.3 slice.267
  25.6 0.3 collective-permute-done
  25.9 2.5 slice.270
  28.4 3.2 slice.268
  31.6 137.7 %all-gather.2.cloned.1.call-done.x_ref = bf16[4096,3712]{1,0:T(8,128)(2,1)} async-done(((bf16[64,3712]{1,0:T(8,128)(2,1)}), bf16[4096,3712]{1,0:T(8,128)(2,1)}) %all-gather.2.cloned.1.call-update) | async-done | bytes 30408720 | tf_op jit(solution)/shard_map/all_gather | solution.py:285
  169.3 18.8 %pick.1 = (bf16[2,1280,3584]{2,1,0:T(8,128)(2,1)S(1)}, f32[2,1280,128]{2,1,0:T(8,128)S(1)}, bf16[16,256,160]{2,1,0:T(8,128)(2,1)S(1)}) custom-call(s32[2]{0:T(128)S(1)} %pad_add_fusion.ids, bf16[4096,3712]{1,0:T(8,128)(2,1)} %all-gather.2.cloned.1.call-done.x_ref), custom_call_target="tpu_custom_call" | custom-call | flops 4697620480 | bytes 58720256 | tf_op jit(solution)/shard_map/pick/pallas_call | solution.py:160
  188.1 0.4 slice_reduce_fusion
  188.5 6.5 %fusion.6 = f32[1280,512]{1,0:T(8,128)} fusion(bf16[2,1280,3584]{2,1,0:T(8,128)(2,1)S(1)} %get-tuple-element.19, bf16[1,3584,512]{2,1,0:T(8,128)(2,1)S(1)} %copy-done.13), kind=kOutput, calls=%fused_computation.8 | convolution fusion | flops 4697620480 | bytes 15466496 | tf_op jit(solution)/shard_map/dot_general | solution.py:258
  195.0 8.6 %fusion.2 = f32[1280,512]{1,0:T(8,128)} fusion(bf16[3584,512]{1,0:T(8,128)(2,1)} %collective-permute-done.1, bf16[2,1280,3584]{2,1,0:T(8,128)(2,1)S(1)} %get-tuple-element.19), kind=kOutput, calls=%fused_computation.4 | convolution fusion | flops 4697620480 | bytes 15466496 | tf_op jit(solution)/shard_map/dot_general | solution.py:258
  203.6 6.7 %fusion.18 = bf16[1280,512]{1,0:T(8,128)(2,1)S(1)} fusion(bf16[2,1280,3584]{2,1,0:T(8,128)(2,1)S(1)} %get-tuple-element.19, f32[1280,512]{1,0:T(8,128)} %fusion.6, f32[1280]{0:T(1024)S(1)} %get-tuple-element.30, bf16[1,3584,512]{2,1,0:T(8,128)(2,1)S(1)} %copy-done.14), kind=kOutput, calls=%fused_computation.21 | convolution fusion | flops 4702208000 | bytes 16785408 | tf_op jit(solution)/shard_map/dot_general | solution.py:259
  210.3 8.3 %multiply_convert_fusion.1 = bf16[1280,512]{1,0:T(8,128)(2,1)S(1)} fusion(f32[1280,512]{1,0:T(8,128)} %fusion.2, f32[1280]{0:T(1024)S(1)} %get-tuple-element.29, bf16[3584,512]{1,0:T(8,128)(2,1)} %collective-permute-done.2, bf16[2,1280,3584]{2,1,0:T(8,128)(2,1)S(1)} %get-tuple-element.19), kind=kOutput, calls=%fused_computation.35 | convolution fusion | flops 4702208000 | bytes 16785408 | tf_op jit(solution)/shard_map/dot_general | solution.py:259
  218.7 3.4 convolution_convert_fusion.y1_ref
  222.1 3.4 convolution_convert_fusion.1.y0_ref
  225.6 10.2 %put.1 = bf16[16,4,64,2304]{3,2,1,0:T(8,128)(2,1)} custom-call(s32[1]{0:T(128)} %bitcast.11.plane, bf16[16,256,160]{2,1,0:T(8,128)(2,1)S(1)} %get-tuple-element.18.st_ref, bf16[1280,2304]{1,0:T(8,128)(2,1)S(1)} %convolution_convert_fusion.1.y0_ref, bf16[1280,2304]{1,0:T(8,128)(2,1)S(1)} %convolution_convert_fusion.y1_ref), custom_call_target="tpu_custom_call" | custom-call | flops 3019898880 | bytes 28311552 | tf_op jit(solution)/shard_map/put/pallas_call | solution.py:233
  235.8 3.7 convolution_convert_fusion.3.y0_ref
  239.5 1.9 convolution_convert_fusion.2.y1_ref
  241.4 5.8 %put_halves.1 = (bf16[4,1024,640]{2,1,0:T(8,128)(2,1)S(1)}, bf16[4,1024,640]{2,1,0:T(8,128)(2,1)S(1)}) custom-call(s32[1]{0:T(128)} %bitcast.11.plane, bf16[16,256,160]{2,1,0:T(8,128)(2,1)S(1)} %get-tuple-element.18.st_ref, bf16[1280,1280]{1,0:T(8,128)(2,1)S(1)} %convolution_convert_fusion.3.y0_ref, bf16[1280,1280]{1,0:T(8,128)(2,1)S(1)} %convolution_convert_fusion.2.y1_ref), custom_call_target="tpu_custom_call" | custom-call | flops 1677721600 | bytes 15728640 | tf_op jit(solution)/shard_map/put_halves/pallas_call | solution.py:233
  247.2 0.1 slice_bitcast_fusion
  247.4 1.9 collective-permute-start.9
  249.3 0.1 slice_bitcast_fusion.1
  249.4 0.2 collective-permute-start.6
  249.6 28.1 %collective-permute-done.9 = bf16[1024,640]{1,0:T(8,128)(2,1)S(1)} collective-permute-done((bf16[1024,640]{1,0:T(8,128)(2,1)S(1)}, bf16[1024,640]{1,0:T(8,128)(2,1)S(1)}, u32[]{:S(2)}, u32[]{:S(2)}) %collective-permute-start.9) | collective-permute-done | bytes 1310752 | tf_op jit(solution)/shard_map/ppermute | solution.py:311
  277.8 0.3 fusion.23
  278.1 1.9 collective-permute-start.10
  280.1 0.3 fusion.26
  280.4 0.2 collective-permute-start.7
  280.6 27.1 %collective-permute-done.10 = bf16[1024,640]{1,0:T(8,128)(2,1)S(1)} collective-permute-done((bf16[1024,640]{1,0:T(8,128)(2,1)S(1)}, bf16[1024,640]{1,0:T(8,128)(2,1)S(1)}, u32[]{:S(2)}, u32[]{:S(2)}) %collective-permute-start.10) | collective-permute-done | bytes 1310752 | tf_op jit(solution)/shard_map/ppermute | solution.py:311
  307.8 0.3 fusion.22
  308.1 1.9 collective-permute-start.11
  310.1 0.3 collective-permute-done.7
  310.3 0.3 fusion.25
  310.7 26.5 %collective-permute-done.11 = bf16[1024,640]{1,0:T(8,128)(2,1)S(1)} collective-permute-done((bf16[1024,640]{1,0:T(8,128)(2,1)S(1)}, bf16[1024,640]{1,0:T(8,128)(2,1)S(1)}, u32[]{:S(2)}, u32[]{:S(2)}) %collective-permute-start.11) | collective-permute-done | bytes 1310752 | tf_op jit(solution)/shard_map/ppermute | solution.py:311
  337.3 0.3 fusion.21
  337.6 3.0 collective-permute-done.8
  340.6 0.3 fusion.24
  340.9 1.7 pad_maximum_fusion
  342.6 7.3 %all-to-all-start = ((bf16[16,64,1280]{2,1,0:T(8,128)(2,1)}), bf16[16,64,1280]{2,1,0:T(8,128)(2,1)S(1)}, u32[]{:S(2)}, u32[]{:S(2)}) async-start(bf16[16,64,1280]{2,1,0:T(8,128)(2,1)} %bitcast.160), calls=%async_computation.1 | async-start | bytes 5242880 | tf_op jit(solution)/shard_map/all_to_all | solution.py:316
  350.0 1.4 fusion.64.logits_ref
  351.4 1.8 balance.1
  353.2 0.9 slice_bitcast_fusion.17
  354.0 28.3 %reduce-scatter.2.cloned.1.call-done = bf16[256,2304]{1,0:T(8,128)(2,1)} async-done(((bf16[4096,2304]{1,0:T(8,128)(2,1)}), bf16[256,2304]{1,0:T(8,128)(2,1)}) %reduce-scatter.2.cloned.1.call-update) | async-done | bytes 1179664 | tf_op jit(solution)/shard_map/reduce_scatter | solution.py:301
  382.3 2.1 fusion.79
  384.4 2.8 collective-permute-start.3
  387.2 1.8 collective-permute-start.4
  389.0 0.4 convert_reduce_fusion
  389.4 9.3 %collective-permute-done.3 = bf16[64,2304]{1,0:T(8,128)(2,1)} collective-permute-done((bf16[64,2304]{1,0:T(8,128)(2,1)}, bf16[64,2304]{1,0:T(8,128)(2,1)}, u32[]{:S(2)}, u32[]{:S(2)}) %collective-permute-start.3) | collective-permute-done | bytes 294944 | tf_op jit(solution)/shard_map/ppermute | solution.py:321
  398.7 2.2 collective-permute-done.5
  400.9 1.4 add_bitcast_fusion
  402.3 2.3 fusion.42
  404.7 0.9 fusion.37
  405.6 0.2 pad_maximum_fusion.1
  405.9 2.6 copy.23
  (60 shorter events, 0.8 us)
Async XLA Ops:
  6.5 7.2 %copy-start = (bf16[24,14336]{1,0:T(8,128)(2,1)S(1)}, bf16[24,14336]{1,0:T(8,128)(2,1)}, u32[]{:S(2)}) copy-start(bf16[24,14336]{1,0:T(8,128)(2,1)} %param.10) | copy-start | bytes 2064388
  6.5 3.1 copy-start.2
  6.5 162.7 %all-gather.2.cloned.1.call-start = ((), (), s32[]{:S(2)}) async-start(), calls=%async_computation.2 | async-start | bytes 30883840 | tf_op jit(solution)/shard_map/all_gather | solution.py:285
  9.6 2.7 copy-start.12
  9.7 2.8 copy-start.10
  9.7 3.5 copy-start.11
  15.8 1.9 copy-start.15
  19.0 363.3 %reduce-scatter.2.cloned.1.call-start = ((), (), s32[]{:S(2)}) async-start(), calls=%async_computation.3 | async-start | bytes 20054016 | tf_op jit(solution)/shard_map/reduce_scatter | solution.py:301
  19.1 6.8 %collective-permute-start = (bf16[512,3584]{1,0:T(8,128)(2,1)}, bf16[512,3584]{1,0:T(8,128)(2,1)}, u32[]{:S(2)}, u32[]{:S(2)}) collective-permute-start(bf16[512,3584]{1,0:T(8,128)(2,1)} %bitcast.161), channel_id=1, source_target_pairs={{0,1},{1,0},{2,3},{3,2},{4,5},{5,4},{6,7},{7,6},{8,9},{9,8},{10,11... | collective-permute-start | bytes 11010056 | tf_op jit(solution)/shard_map/ppermute | solution.py:280
  19.1 175.8 %collective-permute-start.1 = (bf16[3584,512]{1,0:T(8,128)(2,1)}, bf16[3584,512]{1,0:T(8,128)(2,1)}, u32[]{:S(2)}, u32[]{:S(2)}) collective-permute-start(bf16[3584,512]{1,0:T(8,128)(2,1)} %bitcast.167), channel_id=1, source_target_pairs={{0,1},{1,0},{2,3},{3,2},{4,5},{5,4},{6,7},{7,6},{8,9},{9,8},{10,11... | collective-permute-start | bytes 11010056 | tf_op jit(solution)/shard_map/ppermute | solution.py:280
  19.6 190.6 %collective-permute-start.2 = (bf16[3584,512]{1,0:T(8,128)(2,1)}, bf16[3584,512]{1,0:T(8,128)(2,1)}, u32[]{:S(2)}, u32[]{:S(2)}) collective-permute-start(bf16[3584,512]{1,0:T(8,128)(2,1)} %bitcast.168), channel_id=1, source_target_pairs={{0,1},{1,0},{2,3},{3,2},{4,5},{5,4},{6,7},{7,6},{8,9},{9,8},{10,11... | collective-permute-start | bytes 11010056 | tf_op jit(solution)/shard_map/ppermute | solution.py:280
  169.3 19.2 %copy-start.13 = (bf16[1,3584,512]{2,1,0:T(8,128)(2,1)S(1)}, bf16[1,3584,512]{2,1,0:T(8,128)(2,1)}, u32[]{:S(2)}) copy-start(bf16[1,3584,512]{2,1,0:T(8,128)(2,1)} %param.15) | copy-start | bytes 11010052
  195.0 8.6 %copy-start.14 = (bf16[1,3584,512]{2,1,0:T(8,128)(2,1)S(1)}, bf16[1,3584,512]{2,1,0:T(8,128)(2,1)}, u32[]{:S(2)}) copy-start(bf16[1,3584,512]{2,1,0:T(8,128)(2,1)} %param.16) | copy-start | bytes 11010052
  210.3 11.8 %copy-start.16 = (bf16[1280,512]{1,0:T(8,128)(2,1)}, bf16[1280,512]{1,0:T(8,128)(2,1)S(1)}, u32[]{:S(2)}) copy-start(bf16[1280,512]{1,0:T(8,128)(2,1)S(1)} %fusion.18) | copy-start | bytes 3932164
  210.3 8.3 %copy-start.8 = (bf16[512,2304]{1,0:T(8,128)(2,1)S(1)}, bf16[512,2304]{1,0:T(8,128)(2,1)}, u32[]{:S(2)}) copy-start(bf16[512,2304]{1,0:T(8,128)(2,1)} %slice.268) | copy-start | bytes 7077892
  218.6 3.5 copy-start.17
  218.7 3.5 copy-start.7
  235.8 3.8 copy-start.9
  235.8 3.8 copy-start.18
  247.4 30.4 %collective-permute-start.9 = (bf16[1024,640]{1,0:T(8,128)(2,1)S(1)}, bf16[1024,640]{1,0:T(8,128)(2,1)S(1)}, u32[]{:S(2)}, u32[]{:S(2)}) collective-permute-start(bf16[1024,640]{1,0:T(8,128)(2,1)S(1)} %slice_bitcast_fusion), channel_id=1, source_target_pairs={{0,96},{32,0},{64,32},{96,64},{1,97},{33,1},{65,33},{97,65},{2,98}... | collective-permute-start | bytes 3932168 | tf_op jit(solution)/shard_map/ppermute | solution.py:311
  249.4 30.7 %collective-permute-start.6 = (bf16[1024,640]{1,0:T(8,128)(2,1)S(1)}, bf16[1024,640]{1,0:T(8,128)(2,1)S(1)}, u32[]{:S(2)}, u32[]{:S(2)}) collective-permute-start(bf16[1024,640]{1,0:T(8,128)(2,1)S(1)} %slice_bitcast_fusion.1), channel_id=1, source_target_pairs={{0,32},{32,64},{64,96},{96,0},{1,33},{33,65},{65,97},{97,1},{2,34}... | collective-permute-start | bytes 3932168 | tf_op jit(solution)/shard_map/ppermute | solution.py:311
  278.1 29.7 %collective-permute-start.10 = (bf16[1024,640]{1,0:T(8,128)(2,1)S(1)}, bf16[1024,640]{1,0:T(8,128)(2,1)S(1)}, u32[]{:S(2)}, u32[]{:S(2)}) collective-permute-start(bf16[1024,640]{1,0:T(8,128)(2,1)S(1)} %fusion.23), channel_id=1, source_target_pairs={{0,96},{32,0},{64,32},{96,64},{1,97},{33,1},{65,33},{97,65},{2,98}... | collective-permute-start | bytes 3932168 | tf_op jit(solution)/shard_map/ppermute | solution.py:311
  280.4 29.9 %collective-permute-start.7 = (bf16[1024,640]{1,0:T(8,128)(2,1)S(1)}, bf16[1024,640]{1,0:T(8,128)(2,1)S(1)}, u32[]{:S(2)}, u32[]{:S(2)}) collective-permute-start(bf16[1024,640]{1,0:T(8,128)(2,1)S(1)} %fusion.26), channel_id=1, source_target_pairs={{0,32},{32,64},{64,96},{96,0},{1,33},{33,65},{65,97},{97,1},{2,34}... | collective-permute-start | bytes 3932168 | tf_op jit(solution)/shard_map/ppermute | solution.py:311
  308.1 29.1 %collective-permute-start.11 = (bf16[1024,640]{1,0:T(8,128)(2,1)S(1)}, bf16[1024,640]{1,0:T(8,128)(2,1)S(1)}, u32[]{:S(2)}, u32[]{:S(2)}) collective-permute-start(bf16[1024,640]{1,0:T(8,128)(2,1)S(1)} %fusion.22), channel_id=1, source_target_pairs={{0,96},{32,0},{64,32},{96,64},{1,97},{33,1},{65,33},{97,65},{2,98}... | collective-permute-start | bytes 3932168 | tf_op jit(solution)/shard_map/ppermute | solution.py:311
  310.7 29.9 %collective-permute-start.8 = (bf16[1024,640]{1,0:T(8,128)(2,1)S(1)}, bf16[1024,640]{1,0:T(8,128)(2,1)S(1)}, u32[]{:S(2)}, u32[]{:S(2)}) collective-permute-start(bf16[1024,640]{1,0:T(8,128)(2,1)S(1)} %fusion.25), channel_id=1, source_target_pairs={{0,32},{32,64},{64,96},{96,0},{1,33},{33,65},{65,97},{97,1},{2,34}... | collective-permute-start | bytes 3932168 | tf_op jit(solution)/shard_map/ppermute | solution.py:311
  342.6 46.4 %all-to-all-start = ((bf16[16,64,1280]{2,1,0:T(8,128)(2,1)}), bf16[16,64,1280]{2,1,0:T(8,128)(2,1)S(1)}, u32[]{:S(2)}, u32[]{:S(2)}) async-start(bf16[16,64,1280]{2,1,0:T(8,128)(2,1)} %bitcast.160), calls=%async_computation.1 | async-start | bytes 5242880 | tf_op jit(solution)/shard_map/all_to_all | solution.py:316
  384.4 14.3 %collective-permute-start.3 = (bf16[64,2304]{1,0:T(8,128)(2,1)}, bf16[64,2304]{1,0:T(8,128)(2,1)}, u32[]{:S(2)}, u32[]{:S(2)}) collective-permute-start(bf16[64,2304]{1,0:T(8,128)(2,1)} %get-tuple-element.44), channel_id=1, source_target_pairs={{0,32},{32,64},{64,96},{96,0},{1,33},{33,65},{65,97},{97,1},{2,34}... | collective-permute-start | bytes 884744 | tf_op jit(solution)/shard_map/ppermute | solution.py:321
  387.2 13.7 %collective-permute-start.5 = (bf16[64,2304]{1,0:T(8,128)(2,1)}, bf16[64,2304]{1,0:T(8,128)(2,1)}, u32[]{:S(2)}, u32[]{:S(2)}) collective-permute-start(bf16[64,2304]{1,0:T(8,128)(2,1)} %get-tuple-element.45), channel_id=1, source_target_pairs={{0,96},{32,0},{64,32},{96,64},{1,97},{33,1},{65,33},{97,65},{2,98}... | collective-permute-start | bytes 884744 | tf_op jit(solution)/shard_map/ppermute | solution.py:321
  387.2 13.7 %collective-permute-start.4 = (bf16[64,2304]{1,0:T(8,128)(2,1)}, bf16[64,2304]{1,0:T(8,128)(2,1)}, u32[]{:S(2)}, u32[]{:S(2)}) collective-permute-start(bf16[64,2304]{1,0:T(8,128)(2,1)} %get-tuple-element.46), channel_id=1, source_target_pairs={{0,64},{32,96},{64,0},{96,32},{1,65},{33,97},{65,1},{97,33},{2,66}... | collective-permute-start | bytes 884744 | tf_op jit(solution)/shard_map/ppermute | solution.py:321
  389.4 15.3 %copy-start.3 = (bf16[64,1,3584]{2,0,1:T(8,128)(2,1)S(1)}, bf16[64,1,3584]{2,0,1:T(8,128)(2,1)}, u32[]{:S(2)}) copy-start(bf16[64,1,3584]{2,0,1:T(8,128)(2,1)} %get-tuple-element.32) | copy-start | bytes 1376260
  389.4 15.3 %copy-start.4 = (bf16[64,1,3584]{2,0,1:T(8,128)(2,1)S(1)}, bf16[64,1,3584]{2,0,1:T(8,128)(2,1)}, u32[]{:S(2)}) copy-start(bf16[64,1,3584]{2,0,1:T(8,128)(2,1)} %get-tuple-element.33) | copy-start | bytes 1376260
  389.4 15.3 %copy-start.5 = (bf16[64,1,3584]{2,0,1:T(8,128)(2,1)S(1)}, bf16[64,1,3584]{2,0,1:T(8,128)(2,1)}, u32[]{:S(2)}) copy-start(bf16[64,1,3584]{2,0,1:T(8,128)(2,1)} %get-tuple-element.34) | copy-start | bytes 1376260
  389.4 15.3 %copy-start.6 = (bf16[64,1,3584]{2,0,1:T(8,128)(2,1)S(1)}, bf16[64,1,3584]{2,0,1:T(8,128)(2,1)}, u32[]{:S(2)}) copy-start(bf16[64,1,3584]{2,0,1:T(8,128)(2,1)} %get-tuple-element.35) | copy-start | bytes 1376260
  405.6 2.9 copy-start.1
Sparse Core Ops, SparseCore 0:
  19.1 150.1 all-gather.1
  235.9 146.3 reduce-scatter.1
